TPU v7x, 32 devices: a whole 2x2x4 slice. The times are simulated.
32 devices in a mesh: gx: 4 (over y, x), gy: 8 (over z, core).
Axes of the slice: x: 2, y: 2, z: 4, core: 2. Of those that a mesh axis runs over, the one named last changes fastest.
Arguments:
- gradient: float32 [16, 512, 1024], P(None, 'gy', 'gx'), may hold values from -6 to 6
- members: float32 [8, 16, 256, 512], P(None, None, 'gy', 'gx'), may hold values from -6 to 6
Outputs:
- covariance_product: float32 [16, 512, 1024], P(None, 'gy', 'gx')
All inputs are finite; a program needn't handle non-finite values.
Results may differ from a plain program's by a relative error of at most 0.0001.
Values sent between devices are 32-bit elements; how exact they have to be, the bound alone decides.
No kernel may reach another device: no remote copies, remote signals or barrier semaphores. Data moves between devices by JAX's collectives and lax.ppermute only.
A program may use at most 128 MiB of HBM per device.

v0:
```python
import functools

import jax
import jax.numpy as jnp
import numpy as np
from jax import lax
from jax.experimental import pallas as pl
from jax.experimental.pallas import tpu as pltpu
from jax.sharding import PartitionSpec as P

beta_raw = [(1.0 - (offset - 4) ** 2 / 25.0) ** 2 for offset in range(9)]
beta_taps = [value / sum(beta_raw) for value in beta_raw]
generations = ((1, 0.5), (2, 0.075), (4, 0.0125))

LANES = 128
GROUP = 8
EXTRA2, EXTRA4, EXTRA1 = 96, 97, 98
EDGE = 120
BF16, F32 = jnp.bfloat16, jnp.float32


def twice_filter(width, first, last):
    low, high = (0 if first else -99), (width - 1 if last else width + 99)
    table = np.zeros((width + 17, width + 1))
    for source in range(-8, width + 9):
        if not low <= source <= high:
            continue
        for middle in range(source - 4, source + 5):
            if not low <= middle <= high:
                continue
            for target in range(max(0, middle - 4), min(width, middle + 4) + 1):
                if target <= high:
                    table[source + 8, target] += beta_taps[middle - source + 4] * beta_taps[target - middle + 4]
    return table


def column_table(width, first, last):
    filters = {factor: twice_filter(width // factor, first, last) for factor, _ in generations}
    base = {1: 0, 2: LANES, 4: LANES + width // 2}
    extra = {1: LANES + EXTRA1, 2: LANES + EXTRA2, 4: LANES + EXTRA4}

    def row(places):
        out = np.zeros(2 * LANES)
        for factor, place in places.items():
            count = width // factor
            out[base[factor]:base[factor] + count] += filters[factor][place + 8, :count]
            out[extra[factor]] += filters[factor][place + 8, count]
        return out

    rows = [row({1: c, 2: c // 2, 4: c // 4}) for c in range(width)]
    rows += [row({1: c, 2: c // 2, 4: c // 4}) for c in range(-8, 0)]
    rows += [row({2: c, 4: c // 2}) for c in range(-8, -4)]
    rows += [row({4: c}) for c in range(-8, -4)]
    rows += [row({1: c, 2: c // 2, 4: c // 4}) for c in range(width, width + 8)] + [row({1: width + 8})]
    half, quarter = width // 2, width // 4
    rows += [row({2: c, 4: c // 2}) for c in range(half + 4, half + 8)] + [row({2: half + 8})]
    rows += [row({4: c}) for c in range(quarter + 4, quarter + 9)]
    return np.stack(rows)


def message_lanes():
    places = []
    for line in range(GROUP):
        places += [(0, line * 8 + c, c, 1, line) for c in range(8)]
        places += [(1, line * 9 + c, 16 + c, 1, line) for c in range(9)]
    for line in range(0, GROUP, 2):
        places += [(0, 64 + line // 2 * 4 + c, 8 + c, 2, line) for c in range(4)]
        places += [(1, 72 + line // 2 * 5 + c, 25 + c, 2, line) for c in range(5)]
    for line in range(0, GROUP, 4):
        places += [(0, 80 + line // 4 * 4 + c, 12 + c, 4, line) for c in range(4)]
        places += [(1, 92 + line // 4 * 5 + c, 30 + c, 4, line) for c in range(5)]
    return places


def packing_table(width):
    table = np.zeros((GROUP, width, 2 * LANES), np.float32)
    east = list(range(width - 8, width)) + [width // 2 - 8 + c for c in range(4)] + [width // 4 - 8 + c for c in range(4)]
    west = list(range(9)) + [4 + c for c in range(5)] + [4 + c for c in range(5)]
    for side, lane, compact, factor, line in message_lanes():
        start = (west[compact - 16] if side else east[compact]) * factor
        table[line:line + factor, start:start + factor, side * LANES + lane] = 1.0
    return table


def placing_table():
    table = np.zeros((GROUP, 2 * LANES, 36), np.float32)
    for side, lane, compact, factor, line in message_lanes():
        table[line, side * LANES + lane, compact] = 1.0
    for line in range(GROUP):
        table[line, EDGE + line, 35] = 1.0
        table[line, LANES + EDGE + line, 16] = 1.0
    return table


def restriction_table(width):
    table = np.zeros((2 * width, 2 * LANES), np.float32)
    for i in range(width):
        table[2 * i, i] += 1.0
        table[2 * i + 1, i] += 0.5
        table[2 * i + 1, i + 1] += 0.5
    return table


def refining_table(width):
    table = np.zeros((2, LANES, 2 * LANES), np.float32)
    for i in range(width):
        table[0, i // 2, i] = 1.0
        table[1, width // 2 + i // 4, i] = 1.0
    table[0, EXTRA2, LANES + EXTRA1] = 1.0
    table[1, EXTRA4, LANES + EXTRA1] = 1.0
    return table


def interpolation_table(width):
    table = np.zeros((2 * LANES, 2 * width), np.float32)
    for i in range(width):
        table[i, 2 * i] += 1.0
        table[i, 2 * i + 1] += 0.5
        table[i + 1 if i + 1 < width else LANES + EXTRA1, 2 * i + 1] += 0.5
    return table


def split(value):
    high = value.astype(BF16)
    return high, (value - high.astype(F32)).astype(BF16)


def mul(a, b):
    return jnp.dot(a, b, preferred_element_type=F32)


def exact_dot(value, table):
    high, low = split(value)
    return mul(high, table) + mul(low, table)


def pack_kernel(levels, height, place, gradient, members, south, restrict, packing,
                coarse_out, products, message_a, message_b, across, east):
    blocks = height // GROUP
    rows = members.reshape(8 * levels * height, LANES)
    tile = gradient[...].reshape(levels * 2 * height, gradient.shape[2])
    value = exact_dot(tile, restrict[...]).reshape(levels, 2 * height, 2 * LANES)
    below = exact_dot(south[...], restrict[...])
    for half in range(2):
        lanes = slice(half * LANES, (half + 1) * LANES)
        across[half, :, 8:, :] = value[:, :, lanes]
        for level in range(levels):
            across[half, level, 7:8, :] = below[level:level + 1, lanes]
    lane = lax.broadcasted_iota(jnp.int32, (GROUP, LANES), 1)
    line_of = lax.broadcasted_iota(jnp.int32, (GROUP, LANES), 0)

    def level_step(level, _):
        for half in range(2):
            value = across[half, level, pl.ds(8, height, 2), :] + 0.5 * (
                across[half, level, pl.ds(9, height, 2), :] + across[half, level, pl.ds(7, height, 2), :]
            )
            if half == 0:
                coarse_out[level] = value
            else:
                east[...] = value
        for block in range(blocks):
            place_rows = pl.ds(pl.multiple_of((level * blocks + block) * 8, 8), 8)
            edge = jnp.zeros((GROUP, LANES), F32)
            for line in range(GROUP):
                y = block * GROUP + line
                member = rows[pl.ds(level * height + y, 8, levels * height), :]
                products[line, place_rows, :] = member * coarse_out[level, y:y + 1, :]
                edge = jnp.where(lane == EDGE + line, pltpu.roll(member, EDGE + line, 1), edge)
            column = jnp.broadcast_to(east[block * GROUP:(block + 1) * GROUP, 0:1], (GROUP, LANES))
            column = jnp.sum(jnp.where(lane == EDGE + line_of, column, 0.0), axis=0, keepdims=True)
            message_a[place_rows, :] = jnp.broadcast_to(column, (GROUP, LANES))
            message_b[place_rows, :] = edge
        return 0

    lax.fori_loop(0, levels, level_step, 0)
    total = jnp.zeros((levels * blocks * 8, 2 * LANES), F32)
    for line in range(GROUP):
        total = total + exact_dot(products[line], packing[line])
    to_east = total[:, :LANES] + message_a[...]
    to_west = total[:, LANES:] + message_b[...]
    even = place[0] == 0
    message_a[...] = jnp.where(even, to_east, to_west)
    message_b[...] = jnp.where(even, to_west, to_east)


def columns_kernel(levels, height, place, products, own_a, own_b, got_a, got_b, own_high, own_low, halo_high, halo_low,
                   filtered, message_a, message_b):
    blocks = height // GROUP
    count = levels * blocks * 8
    lane = lax.broadcasted_iota(jnp.int32, (count, LANES), 1)
    even = place[0] == 0
    own_east, own_west = jnp.where(even, own_a[...], own_b[...]), jnp.where(even, own_b[...], own_a[...])
    west, east = jnp.where(even, got_b[...], got_a[...]), jnp.where(even, got_a[...], got_b[...])
    halo = jnp.concatenate(
        [jnp.where(lane >= EDGE, west * own_west, west), jnp.where(lane >= EDGE, east * own_east, east)], axis=1
    )
    halo_h, halo_l = split(halo)
    for line in range(GROUP):
        high, low = split(products[line])
        value = mul(high, own_high[...]) + mul(low, own_high[...]) + mul(high, own_low[...])
        value = value + (mul(halo_h, halo_high[line]) + mul(halo_l, halo_high[line]) + mul(halo_h, halo_low[line]))
        filtered[line] = value
    small = lax.broadcasted_iota(jnp.int32, (8, LANES), 1)
    second = (small < 64) | (small == EXTRA2)
    first = small == EXTRA1
    up_a = place[1] == 0
    start_a, start_b = jnp.where(up_a, blocks - 1, 0), jnp.where(up_a, 0, blocks - 1)
    coarse_a, coarse_b = jnp.where(up_a, blocks - 2, 0), jnp.where(up_a, 0, blocks - 2)

    def at(level, block, line):
        return filtered[line, pl.ds(pl.multiple_of((level * blocks + block) * 8, 8), 8), LANES:]

    def level_step(level, _):
        fourth = []
        for block in range(blocks):
            for half in range(2):
                fourth.append(sum(at(level, block, half * 4 + k) for k in range(1, 4)) + at(level, block, half * 4))
        for message, start, coarse in ((message_a, start_a, coarse_a), (message_b, start_b, coarse_b)):
            rows = pl.ds(pl.multiple_of((level * blocks + start) * 8, 8), 8)
            for line in range(GROUP):
                message[level, line] = filtered[line, rows, :LANES]
                block, pair = coarse + line // 4, line % 4
                pairs = at(level, block, 2 * pair) + at(level, block, 2 * pair + 1)
                value = jnp.where(second, pairs, fourth[line])
                message[level, 8 + line] = jnp.where(first, filtered[line, rows, LANES:], value)
        return 0

    lax.fori_loop(0, levels, level_step, 0)


def combine_kernel(levels, height, place, filtered, got_a, got_b, members, east_a, east_b, refining, combined,
                   fine, pairs, second_up, fourth_up, weighted):
    blocks = height // GROUP
    rows = members.reshape(8 * levels * height, LANES)
    up_a = place[1] == 0
    low, high = place[2].astype(F32), place[3].astype(F32)
    even = place[0] == 0
    lane = lax.broadcasted_iota(jnp.int32, (8, LANES), 1)
    second = (lane < 64) | (lane == EXTRA2)
    taps = [jnp.float32(tap) for tap in beta_taps[:5]]
    scale = jnp.where(second, jnp.float32(generations[1][1]), jnp.float32(generations[2][1]))

    def convolve(window):
        value = taps[4] * window[4]
        for k in range(4):
            value = value + taps[k] * (window[k] + window[8 - k])
        return value

    def filter_twice(load, count, keep, store):
        once, window = [], []
        for r in range(-8, count + 8):
            window.append(load(r))
            if len(window) > 9:
                window.pop(0)
            if len(window) == 9:
                once.append(keep(r - 4, convolve(window)))
                if len(once) > 9:
                    once.pop(0)
                if len(once) == 9:
                    store(r - 8, convolve(once))

    def level_step(level, _):
        def at(y, lanes):
            return filtered[y % 8, pl.ds(pl.multiple_of((level * blocks + y // 8) * 8, 8), 8), lanes]

        def north(r):
            return jnp.where(up_a, got_a[level, r], got_b[level, r])

        def south(r):
            return jnp.where(up_a, got_b[level, r], got_a[level, r])

        def edges(r, value):
            return value * low if r < 0 else value * high if r >= height else value

        def load_first(r):
            return south(r + 8) if r < 0 else north(r - height) if r >= height else at(r, slice(0, LANES))

        def load_extra(r):
            return south(r + 16) if r < 0 else north(r - height + 8) if r >= height else at(r, slice(LANES, 2 * LANES))

        def store_first(r, value):
            fine[0, r] = value

        def store_extra(r, value):
            fine[1, r] = value

        filter_twice(load_first, height, edges, store_first)
        filter_twice(load_extra, height, edges, store_extra)

        half, quarter = height // 2, height // 4

        def pair(r):
            return at(2 * r, slice(LANES, 2 * LANES)) + at(2 * r + 1, slice(LANES, 2 * LANES))

        def load_coarse(r):
            if r < 0:
                return south(r + 16)
            if r >= half:
                return north(r - half + 8)
            if r < quarter:
                return jnp.where(second, pair(r), pair(2 * r) + pair(2 * r + 1))
            return jnp.where(second, pair(r), north(r - quarter + 8))

        def keep_coarse(r, value):
            if r < 0:
                return value * low
            if r >= half:
                return value * high
            if quarter <= r < quarter + 4:
                return jnp.where(second, value, value * high)
            return value

        def store_coarse(r, value):
            pairs[pl.ds(pl.multiple_of((level * half + r) * 8, 8), 8), :] = value * scale

        filter_twice(load_coarse, half, keep_coarse, store_coarse)
        start = pl.multiple_of(level * half * 8, 8)
        second_up[...] = exact_dot(pairs[pl.ds(start, half * 8), :], refining[0])
        fourth_up[...] = exact_dot(pairs[pl.ds(start, quarter * 8), :], refining[1])
        weight = jnp.float32(generations[0][1])
        for block in range(blocks):
            message_rows = pl.ds(pl.multiple_of((level * blocks + block) * 8, 8), 8)
            from_east = jnp.where(even, east_a[message_rows, :], east_b[message_rows, :])
            for line in range(GROUP):
                y = block * GROUP + line
                member = rows[pl.ds(level * height + y, 8, levels * height), :]
                edge = pltpu.roll(from_east, (EXTRA1 - EDGE - line) % LANES, 1)
                for part, factor in ((0, member), (1, edge)):
                    lanes = slice(part * LANES, (part + 1) * LANES)
                    value = weight * fine[part, y]
                    value = value + second_up[y // 2 * 8:y // 2 * 8 + 8, lanes] + fourth_up[y // 4 * 8:y // 4 * 8 + 8, lanes]
                    weighted[part, line * 8:line * 8 + 8, :] = factor * value
            for part in range(2):
                total = weighted[part, pl.ds(0, 8, 8), :]
                for m in range(1, 8):
                    total = total + weighted[part, pl.ds(m, 8, 8), :]
                combined[level, block * GROUP:(block + 1) * GROUP, part * LANES:(part + 1) * LANES] = total * (1.0 / 7.0)
        return 0

    lax.fori_loop(0, levels, level_step, 0)


def interpolate_kernel(levels, height, combined, north, interpolation, out, extended, rows):
    for level in range(levels):
        extended[0:height, :] = combined[level]
        extended[height:height + 1, :] = north[level:level + 1, :]
        for half in range(2):
            lanes = slice(half * LANES, (half + 1) * LANES)
            here = extended[0:height, lanes]
            rows[half, level, pl.ds(0, height, 2), :] = here
            rows[half, level, pl.ds(1, height, 2), :] = 0.5 * (here + extended[1:height + 1, lanes])
    value = exact_dot(
        jnp.concatenate([rows[half].reshape(levels * 2 * height, LANES) for half in range(2)], axis=1), interpolation[...]
    )
    out[...] = value.reshape(levels, 2 * height, out.shape[2])


def partner(index, size, second):
    other = ((index + 1) ^ 1) - 1 if second else index ^ 1
    return other if 0 <= other < size else None


def swap(value, axis, second):
    size = lax.axis_size(axis)
    pairs = [(i, partner(i, size, second)) for i in range(size)]
    return lax.ppermute(value, axis, [(i, j) for i, j in pairs if j is not None])


def call(kernel, outs, scratch, *args):
    smem = pl.BlockSpec(memory_space=pltpu.SMEM)
    vmem = pl.BlockSpec(memory_space=pltpu.VMEM)
    return pl.pallas_call(
        kernel,
        out_shape=tuple(jax.ShapeDtypeStruct(shape, F32) for shape in outs),
        in_specs=[smem if a.dtype == jnp.int32 else vmem for a in args],
        out_specs=tuple(vmem for _ in outs),
        scratch_shapes=[pltpu.VMEM(shape, F32) for shape in scratch],
    )(*args)


def shards(gradient, members):
    levels, fine_height, fine_width = gradient.shape
    count, _, height, width = members.shape
    assert count == 8 and width == LANES and height % 32 == 0
    blocks = height // GROUP
    group_rows = levels * blocks * 8
    gx, gy = lax.axis_index("gx"), lax.axis_index("gy")
    nx, ny = lax.axis_size("gx"), lax.axis_size("gy")
    assert nx > 1
    place = jnp.stack([gx % 2, gy % 2, (gy > 0).astype(jnp.int32), (gy < ny - 1).astype(jnp.int32)]).astype(jnp.int32)

    up = [(i, i + 1) for i in range(ny - 1)]
    south = lax.ppermute(gradient[:, -1, :], "gy", up)

    case = jnp.where(gx == 0, 0, jnp.where(gx == nx - 1, 2, 1))
    tables = np.stack([column_table(width, i == 0, i == 2) for i in range(3)]).astype(np.float32)
    high_tables = tables.astype(BF16)
    low_tables = (tables - high_tables.astype(np.float32)).astype(BF16)
    high, low = (lax.dynamic_index_in_dim(jnp.asarray(t), case, 0, keepdims=False) for t in (high_tables, low_tables))
    placing = jnp.asarray(placing_table(), BF16).reshape(GROUP * 2 * LANES, 36)
    order = list(range(width, width + 35)) + [0]
    compact_high, compact_low = high[np.array(order)], low[np.array(order)]
    halo_high = mul(placing, compact_high).astype(BF16).reshape(GROUP, 2 * LANES, 2 * LANES)
    halo_low = mul(placing, compact_low).astype(BF16).reshape(GROUP, 2 * LANES, 2 * LANES)

    coarse, products, own_a, own_b = call(
        functools.partial(pack_kernel, levels, height),
        [(levels, height, LANES), (GROUP, group_rows, LANES), (group_rows, LANES), (group_rows, LANES)],
        [(2, levels, 8 + 2 * height, LANES), (height, LANES)],
        place, gradient, members, south, jnp.asarray(restriction_table(width), BF16), jnp.asarray(packing_table(width), BF16),
    )
    got_a, got_b = swap(own_a, "gx", False), swap(own_b, "gx", True)
    filtered, rows_a, rows_b = call(
        functools.partial(columns_kernel, levels, height),
        [(GROUP, group_rows, 2 * LANES), (levels, 16, 8, LANES), (levels, 16, 8, LANES)],
        [],
        place, products, own_a, own_b, got_a, got_b, high[:width], low[:width], halo_high, halo_low,
    )
    far_b, far_a = swap(rows_b, "gy", True), swap(rows_a, "gy", False)
    (combined,) = call(
        functools.partial(combine_kernel, levels, height),
        [(levels, height, 2 * LANES)],
        [(2, height, 8, LANES), (levels * height // 2 * 8, LANES), (height // 2 * 8, 2 * LANES),
         (height // 4 * 8, 2 * LANES), (2, 64, LANES)],
        place, filtered, far_a, far_b, members, got_a, got_b, jnp.asarray(refining_table(width), BF16),
    )
    north = lax.ppermute(combined[:, 0, :], "gy", [(j, i) for i, j in up])
    (out,) = call(
        functools.partial(interpolate_kernel, levels, height),
        [(levels, fine_height, fine_width)],
        [(height + 8, 2 * LANES), (2, levels, 2 * height, LANES)],
        combined, north, jnp.asarray(interpolation_table(width), BF16),
    )
    return out


def solution(mesh):
    in_specs = (P(None, "gy", "gx"), P(None, None, "gy", "gx"))
    out_specs = P(None, "gy", "gx")
    return jax.shard_map(shards, mesh=mesh, in_specs=in_specs, out_specs=out_specs, check_vma=False)
```

profile of v0, /device:TPU:21, one launch (start us, length us, event | category | flops | bytes accessed | tf_op | source)
XLA Modules:
  0.0 82.3 jit_solution(4642357151486754031)
XLA Ops:
  0.0 0.9 %slice.18 = f32[16,1,256]{2,1,0:T(1,128)S(1)} slice(f32[16,64,256]{2,1,0:T(8,128)} %gradient.1), slice={[0:16], [63:64], [0:256]} | slice | bytes 32768 | tf_op jit(solution)/shard_map/slice | solution.py:393
  0.9 3.8 %collective-permute-start = (f32[16,256]{1,0:T(8,128)S(1)}, f32[16,256]{1,0:T(8,128)S(1)}, u32[]{:S(2)}, u32[]{:S(2)}) collective-permute-start(f32[16,256]{1,0:T(8,128)S(1)} %bitcast.30), channel_id=1, source_target_pairs={{0,1},{1,2},{2,3},{3,4},{4,5},{5,6},{6,7},{8,9},{9,10},{10,11},{11... | collective-permute-start | bytes 49160 | tf_op jit(solution)/shard_map/ppermute | solution.py:393
  4.7 0.7 pad_clamp_fusion
  5.4 0.9 %dynamic-slice_bitcast_fusion = (bf16[163,256]{1,0:T(8,128)(2,1)S(1)}, bf16[163,256]{1,0:T(8,128)(2,1)S(1)}) fusion(bf16[3,163,256]{2,1,0:T(8,128)(2,1)} %constant.59.clone, s32[]{:T(128)S(6)} %select_n.31, bf16[3,163,256]{2,1,0:T(8,128)(2,1)} %constant.58.clone), kind=kLoop, calls=%fused_computation.6 | loop fusion | bytes 333828 | tf_op jit(solution)/shard_map/jit(dynamic_index_in_dim)/squeeze | solution.py:399
  6.3 0.6 gather_fusion
  7.0 1.5 %fusion = bf16[2048,256]{0,1:T(8,128)(2,1)S(1)} fusion(bf16[36,256]{1,0:T(8,128)(2,1)S(1)} %gather_fusion, bf16[2048,36]{1,0:T(8,128)(2,1)} %constant.68), kind=kOutput, calls=%fused_computation.4 | convolution fusion | flops 38273024 | bytes 1214464 | tf_op jit(solution)/shard_map/dot_general | solution.py:129
  8.5 0.6 pad_add_fusion.place
  9.1 0.6 gather_fusion.1
  9.8 1.3 %copy.15 = bf16[2048,256]{1,0:T(8,128)(2,1)} copy(bf16[2048,256]{0,1:T(8,128)(2,1)S(1)} %fusion) | data formatting | bytes 2097152 | tf_op jit(solution)/shard_map/convert_element_type | solution.py:403
  11.1 0.0 copy-start
  11.1 0.0 collective-permute-done.south
  11.1 0.0 copy-start.5
  11.1 0.6 copy-done.5
  11.7 7.7 %shard_map.127 = (f32[16,32,128]{2,1,0:T(8,128)}, f32[8,512,128]{2,1,0:T(8,128)}, f32[512,128]{1,0:T(8,128)}, f32[512,128]{1,0:T(8,128)}) custom-call(s32[4]{0:T(128)} %pad_add_fusion.place, f32[16,64,256]{2,1,0:T(8,128)} %gradient.1, f32[8,16,32,128]{3,2,1,0:T(8,128)} %members.3, f32[16,256]{1,0:T(8,128)} %copy-done.5, ...), custom_call_target="tpu_custom_call" | custom-call | tf_op jit(solution)/shard_map/pallas_call | solution.py:372
  19.3 1.2 %collective-permute-start.1 = (f32[512,128]{1,0:T(8,128)}, f32[512,128]{1,0:T(8,128)S(1)}, u32[]{:S(2)}, u32[]{:S(2)}) collective-permute-start(f32[512,128]{1,0:T(8,128)} %get-tuple-element.12.own_a), channel_id=1, source_target_pairs={{0,8},{8,0},{16,24},{24,16},{1,9},{9,1},{17,25},{25,17},{2,10},{10... | collective-permute-start | bytes 786440 | tf_op jit(solution)/shard_map/ppermute | solution.py:366
  20.6 2.1 %collective-permute-start.2 = (f32[512,128]{1,0:T(8,128)}, f32[512,128]{1,0:T(8,128)S(1)}, u32[]{:S(2)}, u32[]{:S(2)}) collective-permute-start(f32[512,128]{1,0:T(8,128)} %get-tuple-element.13.own_b), channel_id=1, source_target_pairs={{8,16},{16,8},{9,17},{17,9},{10,18},{18,10},{11,19},{19,11},{12,20... | collective-permute-start | bytes 786440 | tf_op jit(solution)/shard_map/ppermute | solution.py:366
  22.7 0.0 copy-done
  22.7 0.5 fusion.1
  23.2 1.3 %copy.16 = bf16[2048,256]{1,0:T(8,128)(2,1)} copy(bf16[2048,256]{0,1:T(8,128)(2,1)S(1)} %fusion.1) | data formatting | bytes 2097152 | tf_op jit(solution)/shard_map/convert_element_type | solution.py:404
  24.5 1.5 %dynamic-slice_bitcast_fusion.2 = (bf16[128,256]{1,0:T(8,128)(2,1)}, bf16[128,256]{1,0:T(8,128)(2,1)}) fusion(bf16[3,163,256]{2,1,0:T(8,128)(2,1)} %constant.59.clone, s32[]{:T(128)S(6)} %select_n.31, bf16[3,163,256]{2,1,0:T(8,128)(2,1)} %constant.58.clone), kind=kLoop, calls=%fused_computation.8 | loop fusion | bytes 262148 | tf_op jit(solution)/shard_map/slice | solution.py:417
  26.0 1.2 %collective-permute-done.1.got_a.east_a = f32[512,128]{1,0:T(8,128)S(1)} collective-permute-done((f32[512,128]{1,0:T(8,128)}, f32[512,128]{1,0:T(8,128)S(1)}, u32[]{:S(2)}, u32[]{:S(2)}) %collective-permute-start.1) | collective-permute-done | bytes 262176 | tf_op jit(solution)/shard_map/ppermute | solution.py:366
  27.2 0.0 copy-start.3
  27.2 5.3 %collective-permute-done.2.got_b.east_b = f32[512,128]{1,0:T(8,128)S(1)} collective-permute-done((f32[512,128]{1,0:T(8,128)}, f32[512,128]{1,0:T(8,128)S(1)}, u32[]{:S(2)}, u32[]{:S(2)}) %collective-permute-start.2) | collective-permute-done | bytes 262176 | tf_op jit(solution)/shard_map/ppermute | solution.py:366
  32.4 0.0 copy-start.4
  32.4 0.0 copy-done.3
  32.4 0.7 copy-done.4
  33.2 9.4 %shard_map.128 = (f32[8,512,256]{2,1,0:T(8,128)}, f32[16,16,8,128]{3,2,1,0:T(8,128)}, f32[16,16,8,128]{3,2,1,0:T(8,128)}) custom-call(s32[4]{0:T(128)} %pad_add_fusion.place, f32[8,512,128]{2,1,0:T(8,128)} %get-tuple-element.11.products, f32[512,128]{1,0:T(8,128)} %get-tuple-element.12.own_a, f32[512,128]{1,0:T(8,128)} %get-tuple-element.13.own_b, ...), custom_call_target="tpu_custom_call" | custom-call | tf_op jit(solution)/shard_map/pallas_call | solution.py:372
  42.6 0.0 collective-permute-start.3
  42.6 2.0 %collective-permute-start.4 = (f32[16,16,8,128]{3,2,1,0:T(8,128)}, f32[16,16,8,128]{3,2,1,0:T(8,128)S(1)}, u32[]{:S(2)}, u32[]{:S(2)}) collective-permute-start(f32[16,16,8,128]{3,2,1,0:T(8,128)} %get-tuple-element.16), channel_id=1, source_target_pairs={{1,2},{2,1},{3,4},{4,3},{5,6},{6,5},{9,10},{10,9},{11,12},{12,11},... | collective-permute-start | bytes 3145736 | tf_op jit(solution)/shard_map/ppermute | solution.py:366
  44.6 0.9 %collective-permute-done.3.got_a = f32[16,16,8,128]{3,2,1,0:T(8,128)S(1)} collective-permute-done((f32[16,16,8,128]{3,2,1,0:T(8,128)}, f32[16,16,8,128]{3,2,1,0:T(8,128)S(1)}, u32[]{:S(2)}, u32[]{:S(2)}) %collective-permute-start.3) | collective-permute-done | bytes 1048608 | tf_op jit(solution)/shard_map/ppermute | solution.py:366
  45.5 0.0 copy-start.1
  45.5 13.6 %collective-permute-done.4.got_b = f32[16,16,8,128]{3,2,1,0:T(8,128)S(1)} collective-permute-done((f32[16,16,8,128]{3,2,1,0:T(8,128)}, f32[16,16,8,128]{3,2,1,0:T(8,128)S(1)}, u32[]{:S(2)}, u32[]{:S(2)}) %collective-permute-start.4) | collective-permute-done | bytes 1048608 | tf_op jit(solution)/shard_map/ppermute | solution.py:366
  59.0 0.0 copy-start.2
  59.0 0.0 copy-done.1
  59.0 1.0 %copy-done.2 = f32[16,16,8,128]{3,2,1,0:T(8,128)} copy-done((f32[16,16,8,128]{3,2,1,0:T(8,128)}, f32[16,16,8,128]{3,2,1,0:T(8,128)S(1)}, u32[]{:S(2)}) %copy-start.2) | copy-done | bytes 1048600
  60.0 13.2 %shard_map.129.combined = f32[16,32,256]{2,1,0:T(8,128)} custom-call(s32[4]{0:T(128)} %pad_add_fusion.place, f32[8,512,256]{2,1,0:T(8,128)} %get-tuple-element.14.filtered, f32[16,16,8,128]{3,2,1,0:T(8,128)} %copy-done.1, f32[16,16,8,128]{3,2,1,0:T(8,128)} %copy-done.2, f32[8,16,32,128]{3,2,1,0:T(8,128)} %members.3, f32[512,128]{1,0:T(8,128)} %copy-done.3, ...), custom_call_target="tpu_custom_call" | custom-call | tf_op jit(solution)/shard_map/pallas_call | solution.py:372
  73.3 0.9 %slice.28 = f32[16,1,256]{2,1,0:T(1,128)S(1)} slice(f32[16,32,256]{2,1,0:T(8,128)} %shard_map.129.combined), slice={[0:16], [0:1], [0:256]} | slice | bytes 32768 | tf_op jit(solution)/shard_map/slice | solution.py:427
  74.2 2.3 %collective-permute-start.5 = (f32[16,256]{1,0:T(8,128)S(1)}, f32[16,256]{1,0:T(8,128)S(1)}, u32[]{:S(2)}, u32[]{:S(2)}) collective-permute-start(f32[16,256]{1,0:T(8,128)S(1)} %bitcast.31), channel_id=1, source_target_pairs={{1,0},{2,1},{3,2},{4,3},{5,4},{6,5},{7,6},{9,8},{10,9},{11,10},{12... | collective-permute-start | bytes 49160 | tf_op jit(solution)/shard_map/ppermute | solution.py:427
  76.5 2.7 %collective-permute-done.5.north = f32[16,256]{1,0:T(8,128)S(1)} collective-permute-done((f32[16,256]{1,0:T(8,128)S(1)}, f32[16,256]{1,0:T(8,128)S(1)}, u32[]{:S(2)}, u32[]{:S(2)}) %collective-permute-start.5) | collective-permute-done | bytes 16416 | tf_op jit(solution)/shard_map/ppermute | solution.py:427
  79.2 0.0 copy-start.6
  79.2 0.6 copy-done.6
  79.8 2.5 %shard_map.130 = f32[16,64,256]{2,1,0:T(8,128)} custom-call(f32[16,32,256]{2,1,0:T(8,128)} %shard_map.129.combined, f32[16,256]{1,0:T(8,128)} %copy-done.6, bf16[256,256]{1,0:T(8,128)(2,1)} %constant.66.clone.interpolation), custom_call_target="tpu_custom_call" | custom-call | tf_op jit(solution)/shard_map/pallas_call | solution.py:372
  (2 shorter events, 0.0 us)
Async XLA Ops:
  0.9 10.1 %collective-permute-start = (f32[16,256]{1,0:T(8,128)S(1)}, f32[16,256]{1,0:T(8,128)S(1)}, u32[]{:S(2)}, u32[]{:S(2)}) collective-permute-start(f32[16,256]{1,0:T(8,128)S(1)} %bitcast.30), channel_id=1, source_target_pairs={{0,1},{1,2},{2,3},{3,4},{4,5},{5,6},{6,7},{8,9},{9,10},{10,11},{11... | collective-permute-start | bytes 49160 | tf_op jit(solution)/shard_map/ppermute | solution.py:393
  11.1 11.6 %copy-start = (bf16[2048,36]{1,0:T(8,128)(2,1)S(1)}, bf16[2048,36]{1,0:T(8,128)(2,1)}, u32[]{:S(2)}) copy-start(bf16[2048,36]{1,0:T(8,128)(2,1)} %constant.68) | copy-start | bytes 442372
  11.1 0.6 copy-start.5
  19.3 7.8 %collective-permute-start.1 = (f32[512,128]{1,0:T(8,128)}, f32[512,128]{1,0:T(8,128)S(1)}, u32[]{:S(2)}, u32[]{:S(2)}) collective-permute-start(f32[512,128]{1,0:T(8,128)} %get-tuple-element.12.own_a), channel_id=1, source_target_pairs={{0,8},{8,0},{16,24},{24,16},{1,9},{9,1},{17,25},{25,17},{2,10},{10... | collective-permute-start | bytes 786440 | tf_op jit(solution)/shard_map/ppermute | solution.py:366
  20.6 11.9 %collective-permute-start.2 = (f32[512,128]{1,0:T(8,128)}, f32[512,128]{1,0:T(8,128)S(1)}, u32[]{:S(2)}, u32[]{:S(2)}) collective-permute-start(f32[512,128]{1,0:T(8,128)} %get-tuple-element.13.own_b), channel_id=1, source_target_pairs={{8,16},{16,8},{9,17},{17,9},{10,18},{18,10},{11,19},{19,11},{12,20... | collective-permute-start | bytes 786440 | tf_op jit(solution)/shard_map/ppermute | solution.py:366
  27.2 5.3 %copy-start.3 = (f32[512,128]{1,0:T(8,128)}, f32[512,128]{1,0:T(8,128)S(1)}, u32[]{:S(2)}) copy-start(f32[512,128]{1,0:T(8,128)S(1)} %collective-permute-done.1.got_a.east_a) | copy-start | bytes 786436
  32.4 0.7 copy-start.4
  42.6 2.9 %collective-permute-start.3 = (f32[16,16,8,128]{3,2,1,0:T(8,128)}, f32[16,16,8,128]{3,2,1,0:T(8,128)S(1)}, u32[]{:S(2)}, u32[]{:S(2)}) collective-permute-start(f32[16,16,8,128]{3,2,1,0:T(8,128)} %get-tuple-element.15), channel_id=1, source_target_pairs={{0,1},{1,0},{2,3},{3,2},{4,5},{5,4},{6,7},{7,6},{8,9},{9,8},{10,11... | collective-permute-start | bytes 3145736 | tf_op jit(solution)/shard_map/ppermute | solution.py:366
  42.6 16.4 %collective-permute-start.4 = (f32[16,16,8,128]{3,2,1,0:T(8,128)}, f32[16,16,8,128]{3,2,1,0:T(8,128)S(1)}, u32[]{:S(2)}, u32[]{:S(2)}) collective-permute-start(f32[16,16,8,128]{3,2,1,0:T(8,128)} %get-tuple-element.16), channel_id=1, source_target_pairs={{1,2},{2,1},{3,4},{4,3},{5,6},{6,5},{9,10},{10,9},{11,12},{12,11},... | collective-permute-start | bytes 3145736 | tf_op jit(solution)/shard_map/ppermute | solution.py:366
  45.5 13.6 %copy-start.1 = (f32[16,16,8,128]{3,2,1,0:T(8,128)}, f32[16,16,8,128]{3,2,1,0:T(8,128)S(1)}, u32[]{:S(2)}) copy-start(f32[16,16,8,128]{3,2,1,0:T(8,128)S(1)} %collective-permute-done.3.got_a) | copy-start | bytes 3145732
  59.0 1.0 %copy-start.2 = (f32[16,16,8,128]{3,2,1,0:T(8,128)}, f32[16,16,8,128]{3,2,1,0:T(8,128)S(1)}, u32[]{:S(2)}) copy-start(f32[16,16,8,128]{3,2,1,0:T(8,128)S(1)} %collective-permute-done.4.got_b) | copy-start | bytes 3145732
  74.2 5.1 %collective-permute-start.5 = (f32[16,256]{1,0:T(8,128)S(1)}, f32[16,256]{1,0:T(8,128)S(1)}, u32[]{:S(2)}, u32[]{:S(2)}) collective-permute-start(f32[16,256]{1,0:T(8,128)S(1)} %bitcast.31), channel_id=1, source_target_pairs={{1,0},{2,1},{3,2},{4,3},{5,4},{6,5},{7,6},{9,8},{10,9},{11,10},{12... | collective-permute-start | bytes 49160 | tf_op jit(solution)/shard_map/ppermute | solution.py:427
  79.2 0.6 copy-start.6
where the time goes:
time: 83.7 us; the launch traced here: 82.3 us
  Pallas kernels  32.9 us (39%)
  waiting for transfers between devices  23.6 us (28%)
  starting transfers between devices  11.4 us (14%)
  local copies, waits for them, and re-layouts  11.1 us (13%)
  matrix products  2 us (2%)
  other arithmetic  1.28 us (2%)
    pallas_call x4, Pallas kernels, call(): pl.pallas_call(kernel, out_shape=tuple((jax.ShapeDtypeStruct(shape, F32)...  32.9 us
    ppermute x4, waiting for transfers between devices, swap(): lax.ppermute(value, axis, [(i, j) for i, j in pairs if j is not None])  20.9 us
    ppermute x4, starting transfers between devices, swap(): lax.ppermute(value, axis, [(i, j) for i, j in pairs if j is not None])  5.31 us
    ppermute x1, starting transfers between devices, shards(): south = lax.ppermute(gradient[:, -1, :], 'gy', up)  3.77 us
    unnamed x16, local copies, waits for them, and re-layouts  2.9 us
    ppermute x1, waiting for transfers between devices, shards(): north = lax.ppermute(combined[:, 0, :], 'gy', [(j, i) for i, j in up])  2.75 us
    ppermute x1, starting transfers between devices, shards(): north = lax.ppermute(combined[:, 0, :], 'gy', [(j, i) for i, j in up])  2.3 us
    dot_general x2, matrix products, mul(): return jnp.dot(a, b, preferred_element_type=F32)  2 us
  transfers between devices with their start and end apart: 6, of which 5 were waited for; matrix products, arithmetic and copies ran while one was open for 12% of the time, Pallas kernels for 0%

commit v1 on v0

v1 whole, which is shorter than its diff:
```python
import functools

import jax
import jax.numpy as jnp
import numpy as np
from jax import lax
from jax.experimental import pallas as pl
from jax.experimental.pallas import tpu as pltpu
from jax.sharding import PartitionSpec as P

beta_raw = [(1.0 - (offset - 4) ** 2 / 25.0) ** 2 for offset in range(9)]
beta_taps = [value / sum(beta_raw) for value in beta_raw]
generations = ((1, 0.5), (2, 0.075), (4, 0.0125))

LANES = 128
GROUP = 8
SLOT = 16
EDGE = 15
EXTRA2, EXTRA4, EXTRA1 = 96, 97, 98
CHUNKS = 1
VMEM_LIMIT = 20 * 2**20
BF16, F32 = jnp.bfloat16, jnp.float32
double_taps = [
    sum(beta_taps[k + 4] * beta_taps[offset - k + 4] for k in range(-4, 5) if -4 <= offset - k <= 4) for offset in range(9)
]
edge_taps = [
    [sum(beta_taps[i - k + 4] * beta_taps[k - j + 4] for k in range(-4, 0) if i - k <= 4 and j - k <= 4) for j in range(4)]
    for i in range(4)
]

def twice_filter(width, first, last):
    low, high = (0 if first else -99), (width - 1 if last else width + 99)
    table = np.zeros((width + 17, width + 1))
    for source in range(-8, width + 9):
        if not low <= source <= high:
            continue
        for middle in range(source - 4, source + 5):
            if not low <= middle <= high:
                continue
            for target in range(max(0, middle - 4), min(width, middle + 4) + 1):
                if target <= high:
                    table[source + 8, target] += beta_taps[middle - source + 4] * beta_taps[target - middle + 4]
    return table


def column_table(width, first, last):
    filters = {factor: twice_filter(width // factor, first, last) for factor, _ in generations}
    base = {1: 0, 2: LANES, 4: LANES + width // 2}
    extra = {1: LANES + EXTRA1, 2: LANES + EXTRA2, 4: LANES + EXTRA4}

    def row(places):
        out = np.zeros(2 * LANES)
        for factor, place in places.items():
            count = width // factor
            out[base[factor]:base[factor] + count] += filters[factor][place + 8, :count]
            out[extra[factor]] += filters[factor][place + 8, count]
        return out

    rows = [row({1: c, 2: c // 2, 4: c // 4}) for c in range(width)]
    rows += [row({1: c, 2: c // 2, 4: c // 4}) for c in range(-8, 0)]
    rows += [row({2: c, 4: c // 2}) for c in range(-8, -4)]
    rows += [row({4: c}) for c in range(-8, -4)]
    rows += [row({1: c, 2: c // 2, 4: c // 4}) for c in range(width, width + 8)] + [row({1: width + 8})]
    half, quarter = width // 2, width // 4
    rows += [row({2: c, 4: c // 2}) for c in range(half + 4, half + 8)] + [row({2: half + 8})]
    rows += [row({4: c}) for c in range(quarter + 4, quarter + 9)]
    return np.stack(rows)


def message_lanes():
    places = []
    for line in range(GROUP):
        places += [(0, line * SLOT + c, c, 1, line) for c in range(8)]
        places += [(1, line * SLOT + c, 16 + c, 1, line) for c in range(9)]
        if line % 2 == 0:
            places += [(0, line * SLOT + 8 + c, 8 + c, 2, line) for c in range(4)]
            places += [(1, line * SLOT + 9 + c, 25 + c, 2, line) for c in range(5)]
        if line % 4 == 1:
            places += [(0, line * SLOT + 8 + c, 12 + c, 4, line - 1) for c in range(4)]
            places += [(1, line * SLOT + 9 + c, 30 + c, 4, line - 1) for c in range(5)]
    return places


def packing_table(width):
    table = np.zeros((GROUP, width, 2 * LANES), np.float32)
    east = list(range(width - 8, width)) + [width // 2 - 8 + c for c in range(4)] + [width // 4 - 8 + c for c in range(4)]
    west = list(range(9)) + [4 + c for c in range(5)] + [4 + c for c in range(5)]
    for side, lane, compact, factor, line in message_lanes():
        start = (west[compact - 16] if side else east[compact]) * factor
        table[line:line + factor, start:start + factor, side * LANES + lane] = 1.0
    return table


def halo_table(columns, width):
    table = np.zeros((2, 2 * SLOT, 2 * LANES))
    outer = columns[width:]
    for side, lane, compact, factor, line in message_lanes():
        if line < 2 and lane < 2 * SLOT:
            table[lane // SLOT, side * SLOT + lane % SLOT] = outer[compact]
    table[:, EDGE] = columns[0]
    table[:, SLOT + EDGE] = outer[16]
    return table


def restriction_table(width):
    table = np.zeros((2 * width, 2 * LANES), np.float32)
    for i in range(width):
        table[2 * i, i] += 1.0
        table[2 * i + 1, i] += 0.5
        table[2 * i + 1, i + 1] += 0.5
    return table


def refining_table(width):
    table = np.zeros((LANES, 2 * LANES), np.float32)
    for i in range(width):
        table[i // 2, i] = 1.0
        table[width // 2 + i // 4, i] = 1.0
    table[EXTRA2, LANES + EXTRA1] = 1.0
    table[EXTRA4, LANES + EXTRA1] = 1.0
    return table


def interpolation_table(width):
    table = np.zeros((2 * LANES, 2 * width), np.float32)
    for i in range(width):
        table[i, 2 * i] += 1.0
        table[i, 2 * i + 1] += 0.5
        table[i + 1 if i + 1 < width else LANES + EXTRA1, 2 * i + 1] += 0.5
    return table


def split(value):
    high = value.astype(BF16)
    return high, (value - high.astype(F32)).astype(BF16)


def mul(a, b):
    return jnp.dot(a, b, preferred_element_type=F32)


def exact_dot(value, table):
    high, low = split(value)
    return mul(high, table) + mul(low, table)


def three_dots(value, high_table, low_table):
    high, low = split(value)
    return mul(high, high_table) + mul(low, high_table) + mul(high, low_table)


def column_case():
    gx, nx = lax.axis_index("gx"), lax.axis_size("gx")
    return jnp.where(gx == 0, 0, jnp.where(gx == nx - 1, 2, 1))


def tile(index):
    return pl.ds(pl.multiple_of(index * 8, 8), 8)


def pack_kernel(chunk, levels, height, gradient, members, south, restrict, packing, products, message_a, message_b, across, coarse):
    blocks = height // GROUP
    first = chunk * levels
    all_levels = members.shape[1]
    rows = members.reshape(8 * all_levels * height, LANES)
    fine = gradient[first:first + levels].reshape(levels * 2 * height, gradient.shape[2])
    value = exact_dot(fine, restrict[...]).reshape(levels, 2 * height, 2 * LANES)
    below = exact_dot(south[...], restrict[...])
    for half in range(2):
        lanes = slice(half * LANES, (half + 1) * LANES)
        across[half, :, 8:, :] = value[:, :, lanes]
        for level in range(levels):
            across[half, level, 7:8, :] = below[first + level:first + level + 1, lanes]
    lane = lax.broadcasted_iota(jnp.int32, (GROUP, LANES), 1)
    line_of = lax.broadcasted_iota(jnp.int32, (GROUP, LANES), 0)

    def level_step(level, _):
        for half in range(2):
            coarse[half] = across[half, level, pl.ds(8, height, 2), :] + 0.5 * (
                across[half, level, pl.ds(9, height, 2), :] + across[half, level, pl.ds(7, height, 2), :]
            )
        for block in range(blocks):
            place_rows = tile(level * blocks + block)
            edge = jnp.zeros((GROUP, LANES), F32)
            for line in range(GROUP):
                y = block * GROUP + line
                member = rows[pl.ds((first + level) * height + y, 8, all_levels * height), :]
                products[line, place_rows, :] = member * coarse[0, y:y + 1, :]
                spot = line * SLOT + EDGE
                edge = jnp.where(lane == spot, pltpu.roll(member, spot, 1), edge)
            column = jnp.broadcast_to(coarse[1, block * GROUP:(block + 1) * GROUP, 0:1], (GROUP, LANES))
            column = jnp.sum(jnp.where(lane == line_of * SLOT + EDGE, column, 0.0), axis=0, keepdims=True)
            message_a[place_rows, :] = jnp.broadcast_to(column, (GROUP, LANES))
            message_b[place_rows, :] = edge
        return 0

    lax.fori_loop(0, levels, level_step, 0)
    total = jnp.zeros((levels * blocks * 8, 2 * LANES), F32)
    for line in range(0, GROUP, 2):
        value = jnp.concatenate([products[line], products[line + 1]], axis=1)
        total = total + exact_dot(value, packing[line * LANES:(line + 2) * LANES, :])
    to_east = total[:, :LANES] + message_a[...]
    to_west = total[:, LANES:] + message_b[...]
    even = lax.axis_index("gx") % 2 == 0
    message_a[...] = jnp.where(even, to_east, to_west)
    message_b[...] = jnp.where(even, to_west, to_east)


def own_columns_kernel(levels, height, products, high_tables, low_tables, halo_highs, halo_lows, filtered, halo_high, halo_low):
    groups = levels * height // GROUP
    case = column_case()
    for variant in range(4):
        for source, target in ((halo_highs, halo_high), (halo_lows, halo_low)):
            target[variant] = jnp.zeros((LANES, 2 * LANES), BF16)
            kind = variant % 2
            target[variant, variant * SLOT:(variant + 1) * SLOT, :] = source[case, kind, :SLOT, :]
            target[variant, 64 + variant * SLOT:64 + (variant + 1) * SLOT, :] = source[case, kind, SLOT:, :]
    high, low = high_tables[case], low_tables[case]
    for line in range(GROUP):
        filtered[:, line] = three_dots(products[line], high, low).reshape(groups, 8, 2 * LANES)


def columns_kernel(levels, height, partial, own_a, own_b, got_a, got_b, halo_high, halo_low, filtered, message_a, message_b):
    blocks = height // GROUP
    groups = levels * blocks
    lane = lax.broadcasted_iota(jnp.int32, (groups * 8, LANES), 1)
    even = lax.axis_index("gx") % 2 == 0
    own_east, own_west = jnp.where(even, own_a[...], own_b[...]), jnp.where(even, own_b[...], own_a[...])
    west, east = jnp.where(even, got_b[...], got_a[...]), jnp.where(even, got_a[...], got_b[...])
    spot = lane % SLOT == EDGE
    west = jnp.where(spot, west * own_west, west)
    east = jnp.where(spot, east * own_east, east)
    halves = [
        split(jnp.where(lane < 64, west, pltpu.roll(east, 64, 1))),
        split(jnp.where(lane < 64, pltpu.roll(west, 64, 1), east)),
    ]
    for line in range(GROUP):
        high, low = halves[line // 4]
        value = mul(high, halo_high[line % 4]) + mul(low, halo_high[line % 4]) + mul(high, halo_low[line % 4])
        filtered[:, line] = partial[:, line] + value.reshape(groups, 8, 2 * LANES)
    small = lax.broadcasted_iota(jnp.int32, (8, LANES), 1)
    second = (small < 64) | (small == EXTRA2)
    first = small == EXTRA1
    up_a = lax.axis_index("gy") % 2 == 0
    start_a, start_b = jnp.where(up_a, blocks - 1, 0), jnp.where(up_a, 0, blocks - 1)
    coarse_a, coarse_b = jnp.where(up_a, blocks - 2, 0), jnp.where(up_a, 0, blocks - 2)

    def level_step(level, _):
        def at(block, line):
            return filtered[level * blocks + block, line, :, LANES:]

        fourth = []
        for block in range(blocks):
            for half in range(2):
                fourth.append(sum(at(block, half * 4 + k) for k in range(1, 4)) + at(block, half * 4))
        for message, start, coarse in ((message_a, start_a, coarse_a), (message_b, start_b, coarse_b)):
            for line in range(GROUP):
                message[level, line] = filtered[level * blocks + start, line, :, :LANES]
                block, pair = coarse + line // 4, line % 4
                pairs = at(block, 2 * pair) + at(block, 2 * pair + 1)
                value = jnp.where(second, pairs, fourth[line])
                message[level, 8 + line] = jnp.where(first, at(start, line), value)
        return 0

    lax.fori_loop(0, levels, level_step, 0)


def convolve_own(load, count, low_edges, high_edges, store):
    rows = {}

    def row(r):
        if r not in rows:
            rows[r] = load(r)
        return rows[r]

    for r in range(count):
        value = double_taps[0] * row(r)
        for k in range(1, 9):
            near = [row(q) for q in (r - k, r + k) if 0 <= q < count]
            if near:
                value = value + double_taps[k] * (near[0] if len(near) == 1 else near[0] + near[1])
        if r < 4:
            fix = edge_taps[r][0] * row(0)
            for j in range(1, 4):
                fix = fix + edge_taps[r][j] * row(j)
            value = value - low_edges * fix
        for flag, end in high_edges:
            i = end - 1 - r
            if 0 <= i < 4:
                fix = edge_taps[i][0] * row(end - 1)
                for j in range(1, 4):
                    fix = fix + edge_taps[i][j] * row(end - 1 - j)
                value = value - flag * fix
        store(r, value)
        rows.pop(r - 8, None)


def own_rows_kernel(levels, height, filtered, east_a, east_b, fine, extra, coarse, edge):
    blocks = height // GROUP
    half, quarter = height // 2, height // 4
    gy, ny = lax.axis_index("gy"), lax.axis_size("gy")
    low, high = jnp.where(gy == 0, 1.0, 0.0).astype(F32), jnp.where(gy == ny - 1, 1.0, 0.0).astype(F32)
    even = lax.axis_index("gx") % 2 == 0
    lane = lax.broadcasted_iota(jnp.int32, (8, LANES), 1)
    second = (lane < 64) | (lane == EXTRA2)
    high_second, high_fourth = jnp.where(second, high, 0.0), jnp.where(second, 0.0, high)

    def level_step(level, _):
        def at(y, part):
            return filtered[level * blocks + y // 8, y % 8, :, part * LANES:(part + 1) * LANES]

        def store_to(ref):
            def store(r, value):
                ref[level, r] = value
            return store

        for part, ref in ((0, fine), (1, extra)):
            convolve_own(lambda r: at(r, part), height, low, [(high, height)], store_to(ref))

        def pair(r):
            return at(2 * r, 1) + at(2 * r + 1, 1)

        def load_coarse(r):
            return jnp.where(second, pair(r), pair(2 * r) + pair(2 * r + 1) if r < quarter else 0.0)

        convolve_own(load_coarse, half, low, [(high_second, half), (high_fourth, quarter)], store_to(coarse))
        for block in range(blocks):
            rows = tile(level * blocks + block)
            east = jnp.where(even, east_a[rows, :], east_b[rows, :])
            for line in range(GROUP):
                edge[level, block * GROUP + line] = pltpu.roll(east, (EXTRA1 - EDGE - line * SLOT) % LANES, 1)
        return 0

    lax.fori_loop(0, levels, level_step, 0)


def combine_kernel(chunk, levels, height, fine, extra, coarse, edge, got_a, got_b, members, refining, combined, first_row,
                   stacked, refined, weighted):
    blocks = height // GROUP
    half, quarter = height // 2, height // 4
    first = chunk * levels
    all_levels = members.shape[1]
    rows = members.reshape(8 * all_levels * height, LANES)
    up_a = lax.axis_index("gy") % 2 == 0
    lane = lax.broadcasted_iota(jnp.int32, (8, LANES), 1)
    second = (lane < 64) | (lane == EXTRA2)
    scale = jnp.where(second, jnp.float32(generations[1][1]), jnp.float32(generations[2][1]))
    weight = jnp.float32(generations[0][1])

    def outside(load):
        values = [load(j) for j in range(8)]
        result = []
        for i in range(8):
            total = double_taps[i + 1] * values[0]
            for j in range(1, 8 - i):
                total = total + double_taps[i + 1 + j] * values[j]
            result.append(total)
        return result

    def level_step(level, _):
        def north(r):
            return jnp.where(up_a, got_a[level, r], got_b[level, r])

        def south(r):
            return jnp.where(up_a, got_b[level, r], got_a[level, r])

        fine_south = outside(lambda j: south(7 - j))
        coarse_south = outside(lambda j: south(15 - j))
        fine_north = outside(north)
        coarse_north = outside(lambda j: north(8 + j))
        parts = []
        for r in range(half):
            value = coarse[level, r]
            if r < 8:
                value = value + coarse_south[r]
            if r < quarter:
                i = quarter - 1 - r
                value = value + jnp.where(second, 0.0, coarse_north[i])
            if r >= half - 8:
                value = value + jnp.where(second, coarse_north[half - 1 - r], 0.0)
            parts.append(value * scale)
        for r in range(half):
            stacked[r * 8:r * 8 + 8, :] = jnp.where(second, parts[r], parts[r // 2])
        refined[...] = exact_dot(stacked[...], refining[...])
        for block in range(blocks):
            for line in range(GROUP):
                y = block * GROUP + line
                member = rows[pl.ds((first + level) * height + y, 8, all_levels * height), :]
                for part, factor in ((0, member), (1, edge[level, y])):
                    value = (fine, extra)[part][level, y]
                    if y < 8:
                        value = value + (fine_south, coarse_south)[part][y]
                    if y >= height - 8:
                        value = value + (fine_north, coarse_north)[part][height - 1 - y]
                    value = weight * value + refined[y // 2 * 8:y // 2 * 8 + 8, part * LANES:(part + 1) * LANES]
                    weighted[part, line * 8:line * 8 + 8, :] = factor * value
            for part in range(2):
                lanes = slice(part * LANES, (part + 1) * LANES)
                total = weighted[part, pl.ds(0, 8, 8), :]
                for m in range(1, 8):
                    total = total + weighted[part, pl.ds(m, 8, 8), :]
                total = total * (1.0 / 7.0)
                combined[level, block * GROUP:(block + 1) * GROUP, lanes] = total
        return 0

    lax.fori_loop(0, levels, level_step, 0)
    for level in range(levels):
        first_row[level:level + 1, :] = combined[level, 0:1, :]


def interpolate_kernel(height, *refs):
    chunks = (len(refs) - 4) // 2
    interpolation, out, extended, rows = refs[-4:]
    levels = refs[0].shape[0]
    for chunk in range(chunks):
        combined, north = refs[chunk], refs[chunks + chunk]
        for level in range(levels):
            extended[0:height, :] = combined[level]
            extended[height:height + 1, :] = north[level:level + 1, :]
            for half in range(2):
                lanes = slice(half * LANES, (half + 1) * LANES)
                here = extended[0:height, lanes]
                rows[half, level, pl.ds(0, height, 2), :] = here
                rows[half, level, pl.ds(1, height, 2), :] = 0.5 * (here + extended[1:height + 1, lanes])
        value = exact_dot(
            jnp.concatenate([rows[half].reshape(levels * 2 * height, LANES) for half in range(2)], axis=1), interpolation[...]
        )
        out[chunk * levels:(chunk + 1) * levels] = value.reshape(levels, 2 * height, out.shape[2])


def partner(index, size, second):
    other = ((index + 1) ^ 1) - 1 if second else index ^ 1
    return other if 0 <= other < size else None


def swap(value, axis, second):
    size = lax.axis_size(axis)
    pairs = [(i, partner(i, size, second)) for i in range(size)]
    return lax.ppermute(value, axis, [(i, j) for i, j in pairs if j is not None])


def call(kernel, outs, scratch, cost, *args):
    vmem = pl.BlockSpec(memory_space=pltpu.VMEM)
    return pl.pallas_call(
        kernel,
        out_shape=tuple(jax.ShapeDtypeStruct(*out) if isinstance(out[0], tuple) else jax.ShapeDtypeStruct(out, F32) for out in outs),
        in_specs=[vmem for _ in args],
        out_specs=tuple(vmem for _ in outs),
        scratch_shapes=[pltpu.VMEM(shape, F32) for shape in scratch],
        compiler_params=pltpu.CompilerParams(vmem_limit_bytes=VMEM_LIMIT),
        cost_estimate=pl.CostEstimate(flops=cost, bytes_accessed=2**20, transcendentals=0),
    )(*args)


def halves_of(table):
    high = table.astype(np.float32).astype(BF16)
    return jnp.asarray(high), jnp.asarray((table.astype(np.float32) - high.astype(np.float32)).astype(BF16))


def shards(gradient, members):
    all_levels, fine_height, fine_width = gradient.shape
    count, _, height, width = members.shape
    assert count == 8 and width == LANES and height == 32 and lax.axis_size("gx") > 1
    assert all_levels % CHUNKS == 0
    levels = all_levels // CHUNKS
    groups = levels * height // GROUP
    ny = lax.axis_size("gy")

    up = [(i, i + 1) for i in range(ny - 1)]
    south = lax.ppermute(gradient[:, -1, :], "gy", up)

    columns = [column_table(width, i == 0, i == 2) for i in range(3)]
    high_tables, low_tables = halves_of(np.stack([table[:width] for table in columns]))
    halo_highs, halo_lows = halves_of(np.stack([halo_table(table, width) for table in columns]))
    restrict = jnp.asarray(restriction_table(width), BF16)
    packing = jnp.asarray(packing_table(width), BF16).reshape(GROUP * width, 2 * LANES)
    refining = jnp.asarray(refining_table(width), BF16)
    interpolation = jnp.asarray(interpolation_table(width), BF16)
    flops = 10**9 // CHUNKS

    packed = [
        call(
            functools.partial(pack_kernel, chunk, levels, height),
            [(GROUP, groups * 8, LANES), (groups * 8, LANES), (groups * 8, LANES)],
            [(2, levels, 8 + 2 * height, LANES), (2, height, LANES)],
            flops, gradient, members, south, restrict, packing,
        )
        for chunk in range(CHUNKS)
    ]
    got = [(swap(own_a, "gx", False), swap(own_b, "gx", True)) for _, own_a, own_b in packed]
    partials = [
        call(
            functools.partial(own_columns_kernel, levels, height),
            [(groups, GROUP, 8, 2 * LANES), ((4, LANES, 2 * LANES), BF16), ((4, LANES, 2 * LANES), BF16)],
            [],
            flops, products, high_tables, low_tables, halo_highs, halo_lows,
        )
        for products, _, _ in packed
    ]
    filtered = [
        call(
            functools.partial(columns_kernel, levels, height),
            [(groups, GROUP, 8, 2 * LANES), (levels, 16, 8, LANES), (levels, 16, 8, LANES)],
            [],
            flops, partials[chunk][0], *packed[chunk][1:], *got[chunk], *partials[chunk][1:],
        )
        for chunk in range(CHUNKS)
    ]
    far = [(swap(rows_a, "gy", False), swap(rows_b, "gy", True)) for _, rows_a, rows_b in filtered]
    own = [
        call(
            functools.partial(own_rows_kernel, levels, height),
            [(levels, height, 8, LANES), (levels, height, 8, LANES), (levels, height // 2, 8, LANES), (levels, height, 8, LANES)],
            [],
            flops, filtered[chunk][0], *got[chunk],
        )
        for chunk in range(CHUNKS)
    ]
    combined, first_rows = zip(*(
        call(
            functools.partial(combine_kernel, chunk, levels, height),
            [(levels, height, 2 * LANES), (levels, 2 * LANES)],
            [(height // 2 * 8, LANES), (height // 2 * 8, 2 * LANES), (2, 64, LANES)],
            flops, *own[chunk], *far[chunk], members, refining,
        )
        for chunk in range(CHUNKS)
    ))
    norths = [lax.ppermute(row, "gy", [(j, i) for i, j in up]) for row in first_rows]
    (out,) = call(
        functools.partial(interpolate_kernel, height),
        [(all_levels, fine_height, fine_width)],
        [(height + 8, 2 * LANES), (2, levels, 2 * height, LANES)],
        flops, *combined, *norths, interpolation,
    )
    return out


def solution(mesh):
    in_specs = (P(None, "gy", "gx"), P(None, None, "gy", "gx"))
    out_specs = P(None, "gy", "gx")
    return jax.shard_map(shards, mesh=mesh, in_specs=in_specs, out_specs=out_specs, check_vma=False)
```

time: 83.7 us -> 59.4 us (0.71)
  the two profiles are of different devices: /device:TPU:21 before, /device:TPU:19 now
where the time goes in v1:
time: 59.4 us; the launch traced here: 59.1 us
  Pallas kernels  19.7 us (33%)
  waiting for transfers between devices  19.5 us (33%)
  starting transfers between devices  14 us (24%)
  local copies, waits for them, and re-layouts  5.71 us (10%)
    pallas_call x6, Pallas kernels, call(): pl.pallas_call(kernel, out_shape=tuple((jax.ShapeDtypeStruct(*out) if isi...  19.7 us
    ppermute x4, waiting for transfers between devices, swap(): lax.ppermute(value, axis, [(i, j) for i, j in pairs if j is not None])  15.5 us
    ppermute x4, starting transfers between devices, swap(): lax.ppermute(value, axis, [(i, j) for i, j in pairs if j is not None])  8.33 us
    unnamed x23, local copies, waits for them, and re-layouts  4.79 us
    ppermute x1, starting transfers between devices, shards(): south = lax.ppermute(gradient[:, -1, :], 'gy', up)  3.77 us
    ppermute x1, waiting for transfers between devices, shards(): lax.ppermute(row, 'gy', [(j, i) for i, j in up])  3.12 us
    ppermute x1, starting transfers between devices, shards(): lax.ppermute(row, 'gy', [(j, i) for i, j in up])  1.93 us
  transfers between devices with their start and end apart: 6, of which 5 were waited for; matrix products, arithmetic and copies ran while one was open for 0% of the time, Pallas kernels for 13%

profile of v1, /device:TPU:19, one launch (start us, length us, event | category | flops | bytes accessed | tf_op | source)
XLA Modules:
  0.0 59.1 jit_solution(9078473864276926660)
XLA Ops:
  0.0 0.9 %slice.3 = f32[16,1,256]{2,1,0:T(1,128)S(1)} slice(f32[16,64,256]{2,1,0:T(8,128)} %gradient.1), slice={[0:16], [63:64], [0:256]} | slice | bytes 32768 | tf_op jit(solution)/shard_map/slice | solution.py:470
  0.9 3.8 %collective-permute-start = (f32[16,256]{1,0:T(8,128)S(1)}, f32[16,256]{1,0:T(8,128)S(1)}, u32[]{:S(2)}, u32[]{:S(2)}) collective-permute-start(f32[16,256]{1,0:T(8,128)S(1)} %bitcast.3), channel_id=1, source_target_pairs={{0,1},{1,2},{2,3},{3,4},{4,5},{5,6},{6,7},{8,9},{9,10},{10,11},{11... | collective-permute-start | bytes 49160 | tf_op jit(solution)/shard_map/ppermute | solution.py:470
  4.7 0.8 %collective-permute-done.south = f32[16,256]{1,0:T(8,128)S(1)} collective-permute-done((f32[16,256]{1,0:T(8,128)S(1)}, f32[16,256]{1,0:T(8,128)S(1)}, u32[]{:S(2)}, u32[]{:S(2)}) %collective-permute-start) | collective-permute-done | bytes 16416 | tf_op jit(solution)/shard_map/ppermute | solution.py:470
  5.6 0.0 copy-start
  5.6 1.6 %copy-done = f32[8,16,32,128]{3,2,1,0:T(8,128)S(1)} copy-done((f32[8,16,32,128]{3,2,1,0:T(8,128)S(1)}, f32[8,16,32,128]{3,2,1,0:T(8,128)}, u32[]{:S(2)}) %copy-start) | copy-done | bytes 2097176
  7.1 0.0 copy-start.2
  7.1 1.2 %copy-done.2 = f32[16,64,256]{2,1,0:T(8,128)S(1)} copy-done((f32[16,64,256]{2,1,0:T(8,128)S(1)}, f32[16,64,256]{2,1,0:T(8,128)}, u32[]{:S(2)}) %copy-start.2) | copy-done | bytes 1048600
  8.4 0.0 copy-start.3
  8.4 1.0 %copy-done.3 = bf16[1024,256]{1,0:T(8,128)(2,1)S(1)} copy-done((bf16[1024,256]{1,0:T(8,128)(2,1)S(1)}, bf16[1024,256]{1,0:T(8,128)(2,1)}, u32[]{:S(2)}) %copy-start.3) | copy-done | bytes 524312
  9.4 0.0 copy-start.4
  9.4 0.9 %copy-done.4 = bf16[256,256]{1,0:T(8,128)(2,1)S(1)} copy-done((bf16[256,256]{1,0:T(8,128)(2,1)S(1)}, bf16[256,256]{1,0:T(8,128)(2,1)}, u32[]{:S(2)}) %copy-start.4) | copy-done | bytes 131096
  10.3 0.0 copy-start.6
  10.3 0.0 copy-start.7
  10.3 0.0 copy-start.9
  10.3 0.0 copy-start.10
  10.3 4.2 %shard_map.100 = (f32[8,512,128]{2,1,0:T(8,128)S(1)}, f32[512,128]{1,0:T(8,128)S(1)}, f32[512,128]{1,0:T(8,128)S(1)}) custom-call(f32[16,64,256]{2,1,0:T(8,128)S(1)} %copy-done.2, f32[8,16,32,128]{3,2,1,0:T(8,128)S(1)} %copy-done, f32[16,256]{1,0:T(8,128)S(1)} %collective-permute-done.south, bf16[256,256]{1,0:T(8,128)(2,1)S(1)} %copy-done.4, ...), custom_call_target="tpu_custom_call" | custom-call | flops 1000000000 | bytes 1048576 | tf_op jit(solution)/shard_map/pallas_call | solution.py:444
  14.6 0.3 collective-permute-start.1
  14.9 4.1 %collective-permute-start.2 = (f32[512,128]{1,0:T(8,128)S(1)}, f32[512,128]{1,0:T(8,128)S(1)}, u32[]{:S(2)}, u32[]{:S(2)}) collective-permute-start(f32[512,128]{1,0:T(8,128)S(1)} %get-tuple-element.23.own_b), channel_id=1, source_target_pairs={{8,16},{16,8},{9,17},{17,9},{10,18},{18,10},{11,19},{19,11},{12,20... | collective-permute-start | bytes 786440 | tf_op jit(solution)/shard_map/ppermute | solution.py:439
  19.0 0.0 copy-done.6
  19.0 0.0 copy-done.7
  19.0 0.0 copy-done.9
  19.0 0.0 copy-done.10
  19.0 1.8 %shard_map.101 = (f32[64,8,8,256]{3,2,1,0:T(8,128)S(1)}, bf16[4,128,256]{2,1,0:T(8,128)(2,1)S(1)}, bf16[4,128,256]{2,1,0:T(8,128)(2,1)S(1)}) custom-call(f32[8,512,128]{2,1,0:T(8,128)S(1)} %get-tuple-element.20.products, bf16[3,128,256]{2,1,0:T(8,128)(2,1)S(1)} %copy-done.7, bf16[3,128,256]{2,1,0:T(8,128)(2,1)S(1)} %copy-done.6, ...), custom_call_target="tpu_custom_call" | custom-call | flops 1000000000 | bytes 1048576 | tf_op jit(solution)/shard_map/pallas_call | solution.py:444
  20.8 0.6 %collective-permute-done.1.got_a.east_a = f32[512,128]{1,0:T(8,128)S(1)} collective-permute-done((f32[512,128]{1,0:T(8,128)S(1)}, f32[512,128]{1,0:T(8,128)S(1)}, u32[]{:S(2)}, u32[]{:S(2)}) %collective-permute-start.1) | collective-permute-done | bytes 262176 | tf_op jit(solution)/shard_map/ppermute | solution.py:439
  21.4 6.6 %collective-permute-done.2.got_b.east_b = f32[512,128]{1,0:T(8,128)S(1)} collective-permute-done((f32[512,128]{1,0:T(8,128)S(1)}, f32[512,128]{1,0:T(8,128)S(1)}, u32[]{:S(2)}, u32[]{:S(2)}) %collective-permute-start.2) | collective-permute-done | bytes 262176 | tf_op jit(solution)/shard_map/ppermute | solution.py:439
  28.0 2.3 %shard_map.102 = (f32[64,8,8,256]{3,2,1,0:T(8,128)S(1)}, f32[16,16,8,128]{3,2,1,0:T(8,128)S(1)}, f32[16,16,8,128]{3,2,1,0:T(8,128)S(1)}) custom-call(f32[64,8,8,256]{3,2,1,0:T(8,128)S(1)} %get-tuple-element.21.partial, f32[512,128]{1,0:T(8,128)S(1)} %get-tuple-element.22.own_a, f32[512,128]{1,0:T(8,128)S(1)} %get-tuple-element.23.own_b, ...), custom_call_target="tpu_custom_call" | custom-call | flops 1000000000 | bytes 1048576 | tf_op jit(solution)/shard_map/pallas_call | solution.py:444
  30.3 2.0 %collective-permute-start.3 = (f32[16,16,8,128]{3,2,1,0:T(8,128)S(1)}, f32[16,16,8,128]{3,2,1,0:T(8,128)S(1)}, u32[]{:S(2)}, u32[]{:S(2)}) collective-permute-start(f32[16,16,8,128]{3,2,1,0:T(8,128)S(1)} %get-tuple-element.31), channel_id=1, source_target_pairs={{0,1},{1,0},{2,3},{3,2},{4,5},{5,4},{6,7},{7,6},{8,9},{9,8},{10,11... | collective-permute-start | bytes 3145736 | tf_op jit(solution)/shard_map/ppermute | solution.py:439
  32.3 1.9 %collective-permute-start.4 = (f32[16,16,8,128]{3,2,1,0:T(8,128)S(1)}, f32[16,16,8,128]{3,2,1,0:T(8,128)S(1)}, u32[]{:S(2)}, u32[]{:S(2)}) collective-permute-start(f32[16,16,8,128]{3,2,1,0:T(8,128)S(1)} %get-tuple-element.32), channel_id=1, source_target_pairs={{1,2},{2,1},{3,4},{4,3},{5,6},{6,5},{9,10},{10,9},{11,12},{12,11},... | collective-permute-start | bytes 3145736 | tf_op jit(solution)/shard_map/ppermute | solution.py:439
  34.2 0.0 copy-start.1
  34.2 0.0 copy-start.5
  34.2 5.8 %shard_map.103 = (f32[16,32,8,128]{3,2,1,0:T(8,128)S(1)}, f32[16,32,8,128]{3,2,1,0:T(8,128)S(1)}, f32[16,16,8,128]{3,2,1,0:T(8,128)S(1)}, f32[16,32,8,128]{3,2,1,0:T(8,128)S(1)}) custom-call(f32[64,8,8,256]{3,2,1,0:T(8,128)S(1)} %get-tuple-element.26.filtered, f32[512,128]{1,0:T(8,128)S(1)} %collective-permute-done.1.got_a.east_a, ...), custom_call_target="tpu_custom_call" | custom-call | flops 1000000000 | bytes 1048576 | tf_op jit(solution)/shard_map/pallas_call | solution.py:444
  40.0 0.0 collective-permute-done.3.got_a
  40.0 8.4 %collective-permute-done.4.got_b = f32[16,16,8,128]{3,2,1,0:T(8,128)S(1)} collective-permute-done((f32[16,16,8,128]{3,2,1,0:T(8,128)S(1)}, f32[16,16,8,128]{3,2,1,0:T(8,128)S(1)}, u32[]{:S(2)}, u32[]{:S(2)}) %collective-permute-start.4) | collective-permute-done | bytes 1048608 | tf_op jit(solution)/shard_map/ppermute | solution.py:439
  48.4 0.0 copy-done.1
  48.4 0.0 copy-done.5
  48.4 0.0 copy-start.8
  48.4 4.2 %shard_map.104 = (f32[16,32,256]{2,1,0:T(8,128)S(1)}, f32[16,256]{1,0:T(8,128)S(1)}) custom-call(f32[16,32,8,128]{3,2,1,0:T(8,128)S(1)} %get-tuple-element.27.fine, f32[16,32,8,128]{3,2,1,0:T(8,128)S(1)} %get-tuple-element.28.extra, f32[16,16,8,128]{3,2,1,0:T(8,128)S(1)} %get-tuple-element.29.coarse, f32[16,32,8,128]{3,2,1,0:T(8,128)S(1)} %get-tuple-element.30.edge, ...), custom_call_target="tpu_custom_call" | custom-call | flops 1000000000 | bytes 1048576 | tf_op jit(solution)/shard_map/pallas_call | solution.py:444
  52.6 1.9 %collective-permute-start.5 = (f32[16,256]{1,0:T(8,128)S(1)}, f32[16,256]{1,0:T(8,128)S(1)}, u32[]{:S(2)}, u32[]{:S(2)}) collective-permute-start(f32[16,256]{1,0:T(8,128)S(1)} %get-tuple-element.34), channel_id=1, source_target_pairs={{1,0},{2,1},{3,2},{4,3},{5,4},{6,5},{7,6},{9,8},{10,9},{11,10},{12... | collective-permute-start | bytes 49160 | tf_op jit(solution)/shard_map/ppermute | solution.py:528
  54.5 3.1 %collective-permute-done.5.refs_1_ = f32[16,256]{1,0:T(8,128)S(1)} collective-permute-done((f32[16,256]{1,0:T(8,128)S(1)}, f32[16,256]{1,0:T(8,128)S(1)}, u32[]{:S(2)}, u32[]{:S(2)}) %collective-permute-start.5) | collective-permute-done | bytes 16416 | tf_op jit(solution)/shard_map/ppermute | solution.py:528
  57.6 0.0 copy-done.8
  57.6 1.4 %shard_map.105 = f32[16,64,256]{2,1,0:T(8,128)} custom-call(f32[16,32,256]{2,1,0:T(8,128)S(1)} %get-tuple-element.33.refs_0_, f32[16,256]{1,0:T(8,128)S(1)} %collective-permute-done.5.refs_1_, bf16[256,256]{1,0:T(8,128)(2,1)S(1)} %copy-done.8), custom_call_target="tpu_custom_call" | custom-call | flops 1000000000 | bytes 1048576 | tf_op jit(solution)/shard_map/pallas_call | solution.py:444
  (1 shorter events, 0.0 us)
Async XLA Ops:
  0.9 4.6 %collective-permute-start = (f32[16,256]{1,0:T(8,128)S(1)}, f32[16,256]{1,0:T(8,128)S(1)}, u32[]{:S(2)}, u32[]{:S(2)}) collective-permute-start(f32[16,256]{1,0:T(8,128)S(1)} %bitcast.3), channel_id=1, source_target_pairs={{0,1},{1,2},{2,3},{3,4},{4,5},{5,6},{6,7},{8,9},{9,10},{10,11},{11... | collective-permute-start | bytes 49160 | tf_op jit(solution)/shard_map/ppermute | solution.py:470
  5.6 1.6 %copy-start = (f32[8,16,32,128]{3,2,1,0:T(8,128)S(1)}, f32[8,16,32,128]{3,2,1,0:T(8,128)}, u32[]{:S(2)}) copy-start(f32[8,16,32,128]{3,2,1,0:T(8,128)} %members.3) | copy-start | bytes 6291460
  7.1 1.2 %copy-start.2 = (f32[16,64,256]{2,1,0:T(8,128)S(1)}, f32[16,64,256]{2,1,0:T(8,128)}, u32[]{:S(2)}) copy-start(f32[16,64,256]{2,1,0:T(8,128)} %gradient.1) | copy-start | bytes 3145732
  8.4 1.0 %copy-start.3 = (bf16[1024,256]{1,0:T(8,128)(2,1)S(1)}, bf16[1024,256]{1,0:T(8,128)(2,1)}, u32[]{:S(2)}) copy-start(bf16[1024,256]{1,0:T(8,128)(2,1)} %constant.24.packing) | copy-start | bytes 1572868
  9.4 0.9 %copy-start.4 = (bf16[256,256]{1,0:T(8,128)(2,1)S(1)}, bf16[256,256]{1,0:T(8,128)(2,1)}, u32[]{:S(2)}) copy-start(bf16[256,256]{1,0:T(8,128)(2,1)} %constant.20.clone.restrict) | copy-start | bytes 393220
  10.3 8.6 %copy-start.6 = (bf16[3,128,256]{2,1,0:T(8,128)(2,1)S(1)}, bf16[3,128,256]{2,1,0:T(8,128)(2,1)}, u32[]{:S(2)}) copy-start(bf16[3,128,256]{2,1,0:T(8,128)(2,1)} %constant.17.clone.low_tables) | copy-start | bytes 589828
  10.3 8.7 %copy-start.7 = (bf16[3,128,256]{2,1,0:T(8,128)(2,1)S(1)}, bf16[3,128,256]{2,1,0:T(8,128)(2,1)}, u32[]{:S(2)}) copy-start(bf16[3,128,256]{2,1,0:T(8,128)(2,1)} %constant.16.clone.high_tables) | copy-start | bytes 589828
  10.3 8.7 %copy-start.9 = (bf16[3,2,32,256]{3,2,1,0:T(8,128)(2,1)S(1)}, bf16[3,2,32,256]{3,2,1,0:T(8,128)(2,1)}, u32[]{:S(2)}) copy-start(bf16[3,2,32,256]{3,2,1,0:T(8,128)(2,1)} %constant.19.clone.halo_lows) | copy-start | bytes 294916
  10.3 8.7 %copy-start.10 = (bf16[3,2,32,256]{3,2,1,0:T(8,128)(2,1)S(1)}, bf16[3,2,32,256]{3,2,1,0:T(8,128)(2,1)}, u32[]{:S(2)}) copy-start(bf16[3,2,32,256]{3,2,1,0:T(8,128)(2,1)} %constant.18.clone.halo_highs) | copy-start | bytes 294916
  14.6 6.8 %collective-permute-start.1 = (f32[512,128]{1,0:T(8,128)S(1)}, f32[512,128]{1,0:T(8,128)S(1)}, u32[]{:S(2)}, u32[]{:S(2)}) collective-permute-start(f32[512,128]{1,0:T(8,128)S(1)} %get-tuple-element.22.own_a), channel_id=1, source_target_pairs={{0,8},{8,0},{16,24},{24,16},{1,9},{9,1},{17,25},{25,17},{2,10},{10... | collective-permute-start | bytes 786440 | tf_op jit(solution)/shard_map/ppermute | solution.py:439
  14.9 13.1 %collective-permute-start.2 = (f32[512,128]{1,0:T(8,128)S(1)}, f32[512,128]{1,0:T(8,128)S(1)}, u32[]{:S(2)}, u32[]{:S(2)}) collective-permute-start(f32[512,128]{1,0:T(8,128)S(1)} %get-tuple-element.23.own_b), channel_id=1, source_target_pairs={{8,16},{16,8},{9,17},{17,9},{10,18},{18,10},{11,19},{19,11},{12,20... | collective-permute-start | bytes 786440 | tf_op jit(solution)/shard_map/ppermute | solution.py:439
  30.3 9.8 %collective-permute-start.3 = (f32[16,16,8,128]{3,2,1,0:T(8,128)S(1)}, f32[16,16,8,128]{3,2,1,0:T(8,128)S(1)}, u32[]{:S(2)}, u32[]{:S(2)}) collective-permute-start(f32[16,16,8,128]{3,2,1,0:T(8,128)S(1)} %get-tuple-element.31), channel_id=1, source_target_pairs={{0,1},{1,0},{2,3},{3,2},{4,5},{5,4},{6,7},{7,6},{8,9},{9,8},{10,11... | collective-permute-start | bytes 3145736 | tf_op jit(solution)/shard_map/ppermute | solution.py:439
  32.3 16.1 %collective-permute-start.4 = (f32[16,16,8,128]{3,2,1,0:T(8,128)S(1)}, f32[16,16,8,128]{3,2,1,0:T(8,128)S(1)}, u32[]{:S(2)}, u32[]{:S(2)}) collective-permute-start(f32[16,16,8,128]{3,2,1,0:T(8,128)S(1)} %get-tuple-element.32), channel_id=1, source_target_pairs={{1,2},{2,1},{3,4},{4,3},{5,6},{6,5},{9,10},{10,9},{11,12},{12,11},... | collective-permute-start | bytes 3145736 | tf_op jit(solution)/shard_map/ppermute | solution.py:439
  34.2 14.2 %copy-start.1 = (f32[8,16,32,128]{3,2,1,0:T(8,128)S(1)}, f32[8,16,32,128]{3,2,1,0:T(8,128)}, u32[]{:S(2)}) copy-start(f32[8,16,32,128]{3,2,1,0:T(8,128)} %members.3) | copy-start | bytes 6291460
  34.2 14.2 %copy-start.5 = (bf16[128,256]{1,0:T(8,128)(2,1)S(1)}, bf16[128,256]{1,0:T(8,128)(2,1)}, u32[]{:S(2)}) copy-start(bf16[128,256]{1,0:T(8,128)(2,1)} %constant.22.clone.refining) | copy-start | bytes 196612
  48.4 9.2 %copy-start.8 = (bf16[256,256]{1,0:T(8,128)(2,1)S(1)}, bf16[256,256]{1,0:T(8,128)(2,1)}, u32[]{:S(2)}) copy-start(bf16[256,256]{1,0:T(8,128)(2,1)} %constant.23.clone.refs_2_) | copy-start | bytes 393220
  52.6 5.1 %collective-permute-start.5 = (f32[16,256]{1,0:T(8,128)S(1)}, f32[16,256]{1,0:T(8,128)S(1)}, u32[]{:S(2)}, u32[]{:S(2)}) collective-permute-start(f32[16,256]{1,0:T(8,128)S(1)} %get-tuple-element.34), channel_id=1, source_target_pairs={{1,0},{2,1},{3,2},{4,3},{5,4},{6,5},{7,6},{9,8},{10,9},{11,10},{12... | collective-permute-start | bytes 49160 | tf_op jit(solution)/shard_map/ppermute | solution.py:528

commit v2 on v1

--- a/solution.py
+++ b/solution.py
@@ -16,8 +16,8 @@
 GROUP = 8
 SLOT = 16
 EDGE = 15
-EXTRA2, EXTRA4, EXTRA1 = 96, 97, 98
-CHUNKS = 1
+COLUMN = 32
+CHUNKS = 2
 VMEM_LIMIT = 20 * 2**20
 BF16, F32 = jnp.bfloat16, jnp.float32
 double_taps = [
@@ -46,14 +46,12 @@
 def column_table(width, first, last):
     filters = {factor: twice_filter(width // factor, first, last) for factor, _ in generations}
     base = {1: 0, 2: LANES, 4: LANES + width // 2}
-    extra = {1: LANES + EXTRA1, 2: LANES + EXTRA2, 4: LANES + EXTRA4}
 
     def row(places):
         out = np.zeros(2 * LANES)
         for factor, place in places.items():
             count = width // factor
             out[base[factor]:base[factor] + count] += filters[factor][place + 8, :count]
-            out[extra[factor]] += filters[factor][place + 8, count]
         return out
 
     rows = [row({1: c, 2: c // 2, 4: c // 4}) for c in range(width)]
@@ -112,21 +110,62 @@
 
 
 def refining_table(width):
-    table = np.zeros((LANES, 2 * LANES), np.float32)
+    table = np.zeros((LANES, LANES), np.float32)
     for i in range(width):
         table[i // 2, i] = 1.0
         table[width // 2 + i // 4, i] = 1.0
-    table[EXTRA2, LANES + EXTRA1] = 1.0
-    table[EXTRA4, LANES + EXTRA1] = 1.0
+    return table
+
+
+def column_lane(factor, row):
+    count = GROUP // factor
+    return row // count * COLUMN + {1: 0, 2: 8, 4: 12}[factor] + row % count
+
+
+def column_filter_table(width):
+    table = np.zeros((2 * LANES, LANES))
+    filters = {factor: twice_filter(width // factor, False, False)[:, width // factor] for factor, _ in generations}
+    low = [width - 8 + c for c in range(8)] + [width // 2 - 8 + c for c in range(4)] + [width // 4 - 8 + c for c in range(4)]
+    high = [width + c for c in range(9)] + [width // 2 + 4 + c for c in range(5)] + [width // 4 + 4 + c for c in range(5)]
+    ends = {(1, 16 + 8): 1, (2, 25 + 4): 2}
+    for side, lane, compact, factor, line in message_lanes():
+        place = (high[compact - 16] if side else low[compact]) * factor
+        for generation, _ in generations:
+            if generation >= factor and generation <= ends.get((factor, compact), 4):
+                weight = filters[generation][place // generation + 8]
+                table[side * LANES + lane, column_lane(generation, line // generation)] += weight
+    for line in range(GROUP):
+        for generation, _ in generations:
+            weight = filters[generation][width // generation + 8]
+            table[LANES + line * SLOT + EDGE, column_lane(generation, line // generation)] += weight
+    return table
+
+
+def column_rows_table(height, first, last):
+    table = np.zeros((3, LANES, LANES))
+    for factor, weight in generations:
+        count = height // factor
+        filters = twice_filter(count, first, last)
+        for row in range(height):
+            for source in range(-8, count + 8):
+                kind, place = (1, source + count) if source < 0 else (2, source - count) if source >= count else (0, source)
+                table[kind, column_lane(factor, place), row] += weight * filters[source + 8, row // factor]
+    return table
+
+
+def edge_choice_table():
+    table = np.zeros((LANES, LANES), np.float32)
+    for line in range(GROUP):
+        table[line * SLOT + EDGE, line] = 1.0
     return table
 
 
 def interpolation_table(width):
     table = np.zeros((2 * LANES, 2 * width), np.float32)
     for i in range(width):
-        table[i, 2 * i] += 1.0
-        table[i, 2 * i + 1] += 0.5
-        table[i + 1 if i + 1 < width else LANES + EXTRA1, 2 * i + 1] += 0.5
+        table[i, 2 * i] = 1.0
+        table[i, 2 * i + 1] = 0.5
+        table[LANES + i, 2 * i + 1] = 0.5
     return table
 
 
@@ -158,40 +197,73 @@
     return pl.ds(pl.multiple_of(index * 8, 8), 8)
 
 
-def pack_kernel(chunk, levels, height, gradient, members, south, restrict, packing, products, message_a, message_b, across, coarse):
+def prepare_kernel(height, gradient, members, restrict, across, turned, edges, fine, raw, table, sems):
+    blocks = height // GROUP
+    levels = members.shape[1]
+    part = levels // 4
+    copies = [pltpu.make_async_copy(restrict, table, sems.at[8])]
+    for i in range(4):
+        span = pl.ds(i * part, part)
+        copies.append(pltpu.make_async_copy(gradient.at[span], fine.at[span], sems.at[i]))
+    for i in range(4):
+        span = pl.ds(i * part, part)
+        copies.append(pltpu.make_async_copy(members.at[:, span], raw.at[:, span], sems.at[4 + i]))
+    for copy in copies:
+        copy.start()
+    copies[0].wait()
+    for half in range(2):
+        across[half, :, 0:8, :] = jnp.zeros((levels, 8, LANES), F32)
+    for i in range(4):
+        copies[1 + i].wait()
+        value = exact_dot(fine[i * part:(i + 1) * part].reshape(part * 2 * height, fine.shape[2]), table[...])
+        value = value.reshape(part, 2 * height, 2 * LANES)
+        for half in range(2):
+            across[half, i * part:(i + 1) * part, 8:, :] = value[:, :, half * LANES:(half + 1) * LANES]
+    rows = raw.reshape(8 * levels * height, LANES)
+    lane = lax.broadcasted_iota(jnp.int32, (GROUP, LANES), 1)
+
+    def level_step(level, _):
+        for block in range(blocks):
+            edge = jnp.zeros((GROUP, LANES), F32)
+            for line in range(GROUP):
+                y = block * GROUP + line
+                member = rows[pl.ds(level * height + y, 8, levels * height), :]
+                turned[level, y] = member
+                spot = line * SLOT + EDGE
+                edge = jnp.where(lane == spot, pltpu.roll(member, spot, 1), edge)
+            edges[tile(level * blocks + block), :] = edge
+        return 0
+
+    for i in range(4):
+        copies[5 + i].wait()
+        lax.fori_loop(i * part, (i + 1) * part, level_step, 0)
+
+
+def pack_kernel(chunk, levels, height, across, turned, edges, south, restrict, packing, products, message_a, message_b, coarse, below):
     blocks = height // GROUP
     first = chunk * levels
-    all_levels = members.shape[1]
-    rows = members.reshape(8 * all_levels * height, LANES)
-    fine = gradient[first:first + levels].reshape(levels * 2 * height, gradient.shape[2])
-    value = exact_dot(fine, restrict[...]).reshape(levels, 2 * height, 2 * LANES)
-    below = exact_dot(south[...], restrict[...])
+    value = exact_dot(south[...], restrict[...])
     for half in range(2):
-        lanes = slice(half * LANES, (half + 1) * LANES)
-        across[half, :, 8:, :] = value[:, :, lanes]
-        for level in range(levels):
-            across[half, level, 7:8, :] = below[first + level:first + level + 1, lanes]
+        below[half] = value[:, half * LANES:(half + 1) * LANES]
     lane = lax.broadcasted_iota(jnp.int32, (GROUP, LANES), 1)
     line_of = lax.broadcasted_iota(jnp.int32, (GROUP, LANES), 0)
+    top = lax.broadcasted_iota(jnp.int32, (height, LANES), 0) == 0
 
     def level_step(level, _):
         for half in range(2):
-            coarse[half] = across[half, level, pl.ds(8, height, 2), :] + 0.5 * (
-                across[half, level, pl.ds(9, height, 2), :] + across[half, level, pl.ds(7, height, 2), :]
+            under = jnp.broadcast_to(below[half, pl.ds(first + level, 1), :], (height, LANES))
+            under = jnp.where(top, under, across[half, first + level, pl.ds(7, height, 2), :])
+            coarse[half] = across[half, first + level, pl.ds(8, height, 2), :] + 0.5 * (
+                across[half, first + level, pl.ds(9, height, 2), :] + under
             )
         for block in range(blocks):
             place_rows = tile(level * blocks + block)
-            edge = jnp.zeros((GROUP, LANES), F32)
             for line in range(GROUP):
                 y = block * GROUP + line
-                member = rows[pl.ds((first + level) * height + y, 8, all_levels * height), :]
-                products[line, place_rows, :] = member * coarse[0, y:y + 1, :]
-                spot = line * SLOT + EDGE
-                edge = jnp.where(lane == spot, pltpu.roll(member, spot, 1), edge)
+                products[line, place_rows, :] = turned[first + level, y] * coarse[0, y:y + 1, :]
             column = jnp.broadcast_to(coarse[1, block * GROUP:(block + 1) * GROUP, 0:1], (GROUP, LANES))
             column = jnp.sum(jnp.where(lane == line_of * SLOT + EDGE, column, 0.0), axis=0, keepdims=True)
             message_a[place_rows, :] = jnp.broadcast_to(column, (GROUP, LANES))
-            message_b[place_rows, :] = edge
         return 0
 
     lax.fori_loop(0, levels, level_step, 0)
@@ -200,7 +272,7 @@
         value = jnp.concatenate([products[line], products[line + 1]], axis=1)
         total = total + exact_dot(value, packing[line * LANES:(line + 2) * LANES, :])
     to_east = total[:, :LANES] + message_a[...]
-    to_west = total[:, LANES:] + message_b[...]
+    to_west = total[:, LANES:] + edges[first * blocks * 8:(first + levels) * blocks * 8, :]
     even = lax.axis_index("gx") % 2 == 0
     message_a[...] = jnp.where(even, to_east, to_west)
     message_b[...] = jnp.where(even, to_west, to_east)
@@ -220,7 +292,8 @@
         filtered[:, line] = three_dots(products[line], high, low).reshape(groups, 8, 2 * LANES)
 
 
-def columns_kernel(levels, height, partial, own_a, own_b, got_a, got_b, halo_high, halo_low, filtered, message_a, message_b):
+def columns_kernel(levels, height, partial, own_a, own_b, got_a, got_b, halo_high, halo_low, beyond_high, beyond_low, choice,
+                   filtered, message_a, message_b, factors):
     blocks = height // GROUP
     groups = levels * blocks
     lane = lax.broadcasted_iota(jnp.int32, (groups * 8, LANES), 1)
@@ -228,8 +301,21 @@
     own_east, own_west = jnp.where(even, own_a[...], own_b[...]), jnp.where(even, own_b[...], own_a[...])
     west, east = jnp.where(even, got_b[...], got_a[...]), jnp.where(even, got_a[...], got_b[...])
     spot = lane % SLOT == EDGE
+    chosen = exact_dot(east, choice[...]).reshape(levels, blocks, 8, LANES)
+    total = chosen[:, 0]
+    for block in range(1, blocks):
+        total = total + pltpu.roll(chosen[:, block], block * GROUP, 2)
+    factors[...] = total
     west = jnp.where(spot, west * own_west, west)
     east = jnp.where(spot, east * own_east, east)
+    inside = jnp.where(lax.axis_index("gx") == lax.axis_size("gx") - 1, 0.0, 1.0).astype(F32)
+    beyond = three_dots(jnp.concatenate([own_east, east], axis=1), beyond_high[...], beyond_low[...])
+    beyond = (beyond * inside).reshape(levels, blocks, 8, LANES)
+    total = beyond[:, 0]
+    for block in range(1, blocks):
+        total = total + pltpu.roll(beyond[:, block], block * COLUMN, 2)
+    for message in (message_a, message_b):
+        message[levels * 16:] = total
     halves = [
         split(jnp.where(lane < 64, west, pltpu.roll(east, 64, 1))),
         split(jnp.where(lane < 64, pltpu.roll(west, 64, 1), east)),
@@ -239,8 +325,7 @@
         value = mul(high, halo_high[line % 4]) + mul(low, halo_high[line % 4]) + mul(high, halo_low[line % 4])
         filtered[:, line] = partial[:, line] + value.reshape(groups, 8, 2 * LANES)
     small = lax.broadcasted_iota(jnp.int32, (8, LANES), 1)
-    second = (small < 64) | (small == EXTRA2)
-    first = small == EXTRA1
+    second = small < 64
     up_a = lax.axis_index("gy") % 2 == 0
     start_a, start_b = jnp.where(up_a, blocks - 1, 0), jnp.where(up_a, 0, blocks - 1)
     coarse_a, coarse_b = jnp.where(up_a, blocks - 2, 0), jnp.where(up_a, 0, blocks - 2)
@@ -255,11 +340,10 @@
                 fourth.append(sum(at(block, half * 4 + k) for k in range(1, 4)) + at(block, half * 4))
         for message, start, coarse in ((message_a, start_a, coarse_a), (message_b, start_b, coarse_b)):
             for line in range(GROUP):
-                message[level, line] = filtered[level * blocks + start, line, :, :LANES]
+                message[level * 16 + line] = filtered[level * blocks + start, line, :, :LANES]
                 block, pair = coarse + line // 4, line % 4
                 pairs = at(block, 2 * pair) + at(block, 2 * pair + 1)
-                value = jnp.where(second, pairs, fourth[line])
-                message[level, 8 + line] = jnp.where(first, at(start, line), value)
+                message[level * 16 + 8 + line] = jnp.where(second, pairs, fourth[line])
         return 0
 
     lax.fori_loop(0, levels, level_step, 0)
@@ -295,14 +379,12 @@
         rows.pop(r - 8, None)
 
 
-def own_rows_kernel(levels, height, filtered, east_a, east_b, fine, extra, coarse, edge):
+def own_rows_kernel(levels, height, filtered, fine, coarse):
     blocks = height // GROUP
     half, quarter = height // 2, height // 4
     gy, ny = lax.axis_index("gy"), lax.axis_size("gy")
     low, high = jnp.where(gy == 0, 1.0, 0.0).astype(F32), jnp.where(gy == ny - 1, 1.0, 0.0).astype(F32)
-    even = lax.axis_index("gx") % 2 == 0
-    lane = lax.broadcasted_iota(jnp.int32, (8, LANES), 1)
-    second = (lane < 64) | (lane == EXTRA2)
+    second = lax.broadcasted_iota(jnp.int32, (8, LANES), 1) < 64
     high_second, high_fourth = jnp.where(second, high, 0.0), jnp.where(second, 0.0, high)
 
     def level_step(level, _):
@@ -314,8 +396,7 @@
                 ref[level, r] = value
             return store
 
-        for part, ref in ((0, fine), (1, extra)):
-            convolve_own(lambda r: at(r, part), height, low, [(high, height)], store_to(ref))
+        convolve_own(lambda r: at(r, 0), height, low, [(high, height)], store_to(fine))
 
         def pair(r):
             return at(2 * r, 1) + at(2 * r + 1, 1)
@@ -324,28 +405,31 @@
             return jnp.where(second, pair(r), pair(2 * r) + pair(2 * r + 1) if r < quarter else 0.0)
 
         convolve_own(load_coarse, half, low, [(high_second, half), (high_fourth, quarter)], store_to(coarse))
-        for block in range(blocks):
-            rows = tile(level * blocks + block)
-            east = jnp.where(even, east_a[rows, :], east_b[rows, :])
-            for line in range(GROUP):
-                edge[level, block * GROUP + line] = pltpu.roll(east, (EXTRA1 - EDGE - line * SLOT) % LANES, 1)
         return 0
 
     lax.fori_loop(0, levels, level_step, 0)
 
 
-def combine_kernel(chunk, levels, height, fine, extra, coarse, edge, got_a, got_b, members, refining, combined, first_row,
-                   stacked, refined, weighted):
+def combine_kernel(chunk, levels, height, fine, coarse, got_a, got_b, own_rows, factors, turned, refining,
+                   row_highs, row_lows, combined, beyond, first_row, stacked, refined, weighted):
     blocks = height // GROUP
     half, quarter = height // 2, height // 4
     first = chunk * levels
-    all_levels = members.shape[1]
-    rows = members.reshape(8 * all_levels * height, LANES)
     up_a = lax.axis_index("gy") % 2 == 0
-    lane = lax.broadcasted_iota(jnp.int32, (8, LANES), 1)
-    second = (lane < 64) | (lane == EXTRA2)
+    gy, ny = lax.axis_index("gy"), lax.axis_size("gy")
+    second = lax.broadcasted_iota(jnp.int32, (8, LANES), 1) < 64
     scale = jnp.where(second, jnp.float32(generations[1][1]), jnp.float32(generations[2][1]))
     weight = jnp.float32(generations[0][1])
+
+    def side(value):
+        return value.reshape(levels * 8, LANES)
+
+    case = jnp.where(gy == 0, 0, jnp.where(gy == ny - 1, 2, 1))
+    far_a, far_b = side(got_a[levels * 16:]), side(got_b[levels * 16:])
+    value = three_dots(side(own_rows[levels * 16:]), row_highs[case, 0], row_lows[case, 0])
+    value = value + three_dots(jnp.where(up_a, far_b, far_a), row_highs[case, 1], row_lows[case, 1])
+    value = value + three_dots(jnp.where(up_a, far_a, far_b), row_highs[case, 2], row_lows[case, 2])
+    beyond[...] = jnp.sum(value.reshape(levels, 8, LANES) * factors[...], axis=1) * (1.0 / 7.0)
 
     def outside(load):
         values = [load(j) for j in range(8)]
@@ -359,10 +443,10 @@
 
     def level_step(level, _):
         def north(r):
-            return jnp.where(up_a, got_a[level, r], got_b[level, r])
+            return jnp.where(up_a, got_a[level * 16 + r], got_b[level * 16 + r])
 
         def south(r):
-            return jnp.where(up_a, got_b[level, r], got_a[level, r])
+            return jnp.where(up_a, got_b[level * 16 + r], got_a[level * 16 + r])
 
         fine_south = outside(lambda j: south(7 - j))
         coarse_south = outside(lambda j: south(15 - j))
@@ -385,43 +469,48 @@
         for block in range(blocks):
             for line in range(GROUP):
                 y = block * GROUP + line
-                member = rows[pl.ds((first + level) * height + y, 8, all_levels * height), :]
-                for part, factor in ((0, member), (1, edge[level, y])):
-                    value = (fine, extra)[part][level, y]
-                    if y < 8:
-                        value = value + (fine_south, coarse_south)[part][y]
-                    if y >= height - 8:
-                        value = value + (fine_north, coarse_north)[part][height - 1 - y]
-                    value = weight * value + refined[y // 2 * 8:y // 2 * 8 + 8, part * LANES:(part + 1) * LANES]
-                    weighted[part, line * 8:line * 8 + 8, :] = factor * value
-            for part in range(2):
-                lanes = slice(part * LANES, (part + 1) * LANES)
-                total = weighted[part, pl.ds(0, 8, 8), :]
-                for m in range(1, 8):
-                    total = total + weighted[part, pl.ds(m, 8, 8), :]
-                total = total * (1.0 / 7.0)
-                combined[level, block * GROUP:(block + 1) * GROUP, lanes] = total
+                value = fine[level, y]
+                if y < 8:
+                    value = value + fine_south[y]
+                if y >= height - 8:
+                    value = value + fine_north[height - 1 - y]
+                value = weight * value + refined[y // 2 * 8:y // 2 * 8 + 8, :]
+                weighted[line * 8:line * 8 + 8, :] = turned[first + level, y] * value
+            total = weighted[pl.ds(0, 8, 8), :]
+            for m in range(1, 8):
+                total = total + weighted[pl.ds(m, 8, 8), :]
+            combined[level, block * GROUP:(block + 1) * GROUP, :] = total * (1.0 / 7.0)
         return 0
 
     lax.fori_loop(0, levels, level_step, 0)
     for level in range(levels):
-        first_row[level:level + 1, :] = combined[level, 0:1, :]
+        first_row[level:level + 1, :LANES] = combined[level, 0:1, :]
+    first_row[:, LANES:] = beyond[...]
 
 
 def interpolate_kernel(height, *refs):
-    chunks = (len(refs) - 4) // 2
+    chunks = (len(refs) - 4) // 3
     interpolation, out, extended, rows = refs[-4:]
     levels = refs[0].shape[0]
+    lane = lax.broadcasted_iota(jnp.int32, (height, LANES), 1)
+    line = lax.broadcasted_iota(jnp.int32, (height, LANES), 0)
+    row_lane = lax.broadcasted_iota(jnp.int32, (1, LANES), 1)
     for chunk in range(chunks):
-        combined, north = refs[chunk], refs[chunks + chunk]
+        combined, beyond, north = refs[chunk], refs[chunks + chunk], refs[2 * chunks + chunk]
         for level in range(levels):
-            extended[0:height, :] = combined[level]
-            extended[height:height + 1, :] = north[level:level + 1, :]
+            here = combined[level]
+            last = jnp.broadcast_to(beyond[level:level + 1, :], (height, LANES))
+            last = jnp.sum(jnp.where(lane == line, last, 0.0), axis=1, keepdims=True)
+            after = north[level:level + 1, :LANES]
+            corner = jnp.broadcast_to(north[level:level + 1, LANES:LANES + 1], (1, LANES))
+            extended[0, 0:height, :] = here
+            extended[0, height:height + 1, :] = after
+            extended[1, 0:height, :] = jnp.where(lane == LANES - 1, last, pltpu.roll(here, LANES - 1, 1))
+            extended[1, height:height + 1, :] = jnp.where(row_lane == LANES - 1, corner, pltpu.roll(after, LANES - 1, 1))
             for half in range(2):
-                lanes = slice(half * LANES, (half + 1) * LANES)
-                here = extended[0:height, lanes]
-                rows[half, level, pl.ds(0, height, 2), :] = here
-                rows[half, level, pl.ds(1, height, 2), :] = 0.5 * (here + extended[1:height + 1, lanes])
+                value = extended[half, 0:height, :]
+                rows[half, level, pl.ds(0, height, 2), :] = value
+                rows[half, level, pl.ds(1, height, 2), :] = 0.5 * (value + extended[half, 1:height + 1, :])
         value = exact_dot(
             jnp.concatenate([rows[half].reshape(levels * 2 * height, LANES) for half in range(2)], axis=1), interpolation[...]
         )
@@ -439,14 +528,14 @@
     return lax.ppermute(value, axis, [(i, j) for i, j in pairs if j is not None])
 
 
-def call(kernel, outs, scratch, cost, *args):
+def call(kernel, outs, scratch, cost, *args, in_hbm=0):
     vmem = pl.BlockSpec(memory_space=pltpu.VMEM)
     return pl.pallas_call(
         kernel,
         out_shape=tuple(jax.ShapeDtypeStruct(*out) if isinstance(out[0], tuple) else jax.ShapeDtypeStruct(out, F32) for out in outs),
-        in_specs=[vmem for _ in args],
+        in_specs=[pl.BlockSpec(memory_space=pltpu.HBM) if i < in_hbm else vmem for i in range(len(args))],
         out_specs=tuple(vmem for _ in outs),
-        scratch_shapes=[pltpu.VMEM(shape, F32) for shape in scratch],
+        scratch_shapes=[pltpu.VMEM(shape, F32) if isinstance(shape, tuple) else shape for shape in scratch],
         compiler_params=pltpu.CompilerParams(vmem_limit_bytes=VMEM_LIMIT),
         cost_estimate=pl.CostEstimate(flops=cost, bytes_accessed=2**20, transcendentals=0),
     )(*args)
@@ -476,14 +565,24 @@
     packing = jnp.asarray(packing_table(width), BF16).reshape(GROUP * width, 2 * LANES)
     refining = jnp.asarray(refining_table(width), BF16)
     interpolation = jnp.asarray(interpolation_table(width), BF16)
+    beyond_high, beyond_low = halves_of(column_filter_table(width))
+    row_highs, row_lows = halves_of(np.stack([column_rows_table(height, i == 0, i == 2) for i in range(3)]))
+    choice = jnp.asarray(edge_choice_table(), BF16)
     flops = 10**9 // CHUNKS
-
+    far_rows = (levels * 17, 8, LANES)
+
+    across, turned, edges = call(
+        functools.partial(prepare_kernel, height),
+        [(2, all_levels, 8 + 2 * height, LANES), (all_levels, height, 8, LANES), (all_levels * height, LANES)],
+        [gradient.shape, members.shape, pltpu.VMEM(restrict.shape, BF16), pltpu.SemaphoreType.DMA((9,))],
+        flops, gradient, members, restrict, in_hbm=3,
+    )
     packed = [
         call(
             functools.partial(pack_kernel, chunk, levels, height),
             [(GROUP, groups * 8, LANES), (groups * 8, LANES), (groups * 8, LANES)],
-            [(2, levels, 8 + 2 * height, LANES), (2, height, LANES)],
-            flops, gradient, members, south, restrict, packing,
+            [(2, height, LANES), (2, all_levels, LANES)],
+            flops, across, turned, edges, south, restrict, packing,
         )
         for chunk in range(CHUNKS)
     ]
@@ -500,28 +599,28 @@
     filtered = [
         call(
             functools.partial(columns_kernel, levels, height),
-            [(groups, GROUP, 8, 2 * LANES), (levels, 16, 8, LANES), (levels, 16, 8, LANES)],
+            [(groups, GROUP, 8, 2 * LANES), far_rows, far_rows, (levels, 8, LANES)],
             [],
-            flops, partials[chunk][0], *packed[chunk][1:], *got[chunk], *partials[chunk][1:],
+            flops, partials[chunk][0], *packed[chunk][1:], *got[chunk], *partials[chunk][1:], beyond_high, beyond_low, choice,
         )
         for chunk in range(CHUNKS)
     ]
-    far = [(swap(rows_a, "gy", False), swap(rows_b, "gy", True)) for _, rows_a, rows_b in filtered]
+    far = [(swap(rows_a, "gy", False), swap(rows_b, "gy", True)) for _, rows_a, rows_b, _ in filtered]
     own = [
         call(
             functools.partial(own_rows_kernel, levels, height),
-            [(levels, height, 8, LANES), (levels, height, 8, LANES), (levels, height // 2, 8, LANES), (levels, height, 8, LANES)],
+            [(levels, height, 8, LANES), (levels, height // 2, 8, LANES)],
             [],
-            flops, filtered[chunk][0], *got[chunk],
+            flops, filtered[chunk][0],
         )
         for chunk in range(CHUNKS)
     ]
-    combined, first_rows = zip(*(
+    combined, beyond, first_rows = zip(*(
         call(
             functools.partial(combine_kernel, chunk, levels, height),
-            [(levels, height, 2 * LANES), (levels, 2 * LANES)],
-            [(height // 2 * 8, LANES), (height // 2 * 8, 2 * LANES), (2, 64, LANES)],
-            flops, *own[chunk], *far[chunk], members, refining,
+            [(levels, height, LANES), (levels, LANES), (levels, 2 * LANES)],
+            [(height // 2 * 8, LANES), (height // 2 * 8, LANES), (64, LANES)],
+            flops, *own[chunk], *far[chunk], filtered[chunk][1], filtered[chunk][3], turned, refining, row_highs, row_lows,
         )
         for chunk in range(CHUNKS)
     ))
@@ -529,8 +628,8 @@
     (out,) = call(
         functools.partial(interpolate_kernel, height),
         [(all_levels, fine_height, fine_width)],
-        [(height + 8, 2 * LANES), (2, levels, 2 * height, LANES)],
-        flops, *combined, *norths, interpolation,
+        [(2, height + 8, LANES), (2, levels, 2 * height, LANES)],
+        flops, *combined, *beyond, *norths, interpolation,
     )
     return out
 

time: 59.4 us -> 51.5 us (0.87)
  the two profiles are of different devices: /device:TPU:19 before, /device:TPU:21 now
where the time goes in v2:
time: 51.5 us; the launch traced here: 51.1 us
  starting transfers between devices  21.5 us (42%)
  Pallas kernels  19.7 us (38%)
  waiting for transfers between devices  4.83 us (9%)
  local copies, waits for them, and re-layouts  4.7 us (9%)
    pallas_call x12, Pallas kernels, call(): pl.pallas_call(kernel, out_shape=tuple((jax.ShapeDtypeStruct(*out) if isi...  19.7 us
    ppermute x8, starting transfers between devices, swap(): lax.ppermute(value, axis, [(i, j) for i, j in pairs if j is not None])  13.4 us
    ppermute x2, starting transfers between devices, shards(): lax.ppermute(row, 'gy', [(j, i) for i, j in up])  4.4 us
    unnamed x31, local copies, waits for them, and re-layouts  3.78 us
    ppermute x1, starting transfers between devices, shards(): south = lax.ppermute(gradient[:, -1, :], 'gy', up)  3.77 us
    ppermute x2, waiting for transfers between devices, shards(): lax.ppermute(row, 'gy', [(j, i) for i, j in up])  2.65 us
    ppermute x8, waiting for transfers between devices, swap(): lax.ppermute(value, axis, [(i, j) for i, j in pairs if j is not None])  2.18 us
  transfers between devices with their start and end apart: 11, of which 3 were waited for; matrix products, arithmetic and copies ran while one was open for 0% of the time, Pallas kernels for 32%

profile of v2, /device:TPU:21, one launch (start us, length us, event | category | flops | bytes accessed | tf_op | source)
XLA Modules:
  0.0 51.1 jit_solution(11226916360877220325)
XLA Ops:
  0.0 0.9 %slice.3 = f32[16,1,256]{2,1,0:T(1,128)S(1)} slice(f32[16,64,256]{2,1,0:T(8,128)} %gradient.1), slice={[0:16], [63:64], [0:256]} | slice | bytes 32768 | tf_op jit(solution)/shard_map/slice | solution.py:559
  0.9 3.8 %collective-permute-start = (f32[16,256]{1,0:T(8,128)S(1)}, f32[16,256]{1,0:T(8,128)S(1)}, u32[]{:S(2)}, u32[]{:S(2)}) collective-permute-start(f32[16,256]{1,0:T(8,128)S(1)} %bitcast.3), channel_id=1, source_target_pairs={{0,1},{1,2},{2,3},{3,4},{4,5},{5,6},{6,7},{8,9},{9,10},{10,11},{11... | collective-permute-start | bytes 49160 | tf_op jit(solution)/shard_map/ppermute | solution.py:559
  4.7 0.0 copy-start
  4.7 1.6 %copy-done = f32[8,16,32,128]{3,2,1,0:T(8,128)S(1)} copy-done((f32[8,16,32,128]{3,2,1,0:T(8,128)S(1)}, f32[8,16,32,128]{3,2,1,0:T(8,128)}, u32[]{:S(2)}) %copy-start) | copy-done | bytes 2097176
  6.3 0.0 copy-start.4
  6.3 0.9 %copy-done.4 = bf16[256,256]{1,0:T(8,128)(2,1)S(1)} copy-done((bf16[256,256]{1,0:T(8,128)(2,1)S(1)}, bf16[256,256]{1,0:T(8,128)(2,1)}, u32[]{:S(2)}) %copy-start.4) | copy-done | bytes 131096
  7.2 0.0 copy-start.5
  7.2 1.2 %copy-done.5 = f32[16,64,256]{2,1,0:T(8,128)S(1)} copy-done((f32[16,64,256]{2,1,0:T(8,128)S(1)}, f32[16,64,256]{2,1,0:T(8,128)}, u32[]{:S(2)}) %copy-start.5) | copy-done | bytes 1048600
  8.4 0.0 copy-start.1
  8.4 4.0 %shard_map.145 = (f32[2,16,72,128]{3,2,1,0:T(8,128)S(1)}, f32[16,32,8,128]{3,2,1,0:T(8,128)S(1)}, f32[512,128]{1,0:T(8,128)S(1)}) custom-call(f32[16,64,256]{2,1,0:T(8,128)S(1)} %copy-done.5, f32[8,16,32,128]{3,2,1,0:T(8,128)S(1)} %copy-done, bf16[256,256]{1,0:T(8,128)(2,1)S(1)} %copy-done.4), custom_call_target="tpu_custom_call" | custom-call | flops 500000000 | bytes 1048576 | tf_op jit(solution)/shard_map/pallas_call | solution.py:533
  12.4 0.0 collective-permute-done.south
  12.4 0.0 copy-done.1
  12.4 1.3 %shard_map.151 = (f32[8,256,128]{2,1,0:T(8,128)S(1)}, f32[256,128]{1,0:T(8,128)S(1)}, f32[256,128]{1,0:T(8,128)S(1)}) custom-call(f32[2,16,72,128]{3,2,1,0:T(8,128)S(1)} %get-tuple-element.38.across, f32[16,32,8,128]{3,2,1,0:T(8,128)S(1)} %get-tuple-element.39.turned, f32[512,128]{1,0:T(8,128)S(1)} %get-tuple-element.40.edges, ...), custom_call_target="tpu_custom_call" | custom-call | flops 500000000 | bytes 1048576 | tf_op jit(solution)/shard_map/pallas_call | solution.py:533
  13.8 1.3 %collective-permute-start.5 = (f32[256,128]{1,0:T(8,128)S(1)}, f32[256,128]{1,0:T(8,128)S(1)}, u32[]{:S(2)}, u32[]{:S(2)}) collective-permute-start(f32[256,128]{1,0:T(8,128)S(1)} %get-tuple-element.56.own_a), channel_id=1, source_target_pairs={{0,8},{8,0},{16,24},{24,16},{1,9},{9,1},{17,25},{25,17},{2,10},{10... | collective-permute-start | bytes 393224 | tf_op jit(solution)/shard_map/ppermute | solution.py:528
  15.0 0.0 copy-start.10
  15.0 0.0 copy-start.11
  15.0 0.0 copy-start.13
  15.0 0.0 copy-start.14
  15.1 0.0 copy-start.6
  15.1 0.0 copy-start.7
  15.1 0.0 copy-start.9
  15.1 2.2 %collective-permute-start.6 = (f32[256,128]{1,0:T(8,128)S(1)}, f32[256,128]{1,0:T(8,128)S(1)}, u32[]{:S(2)}, u32[]{:S(2)}) collective-permute-start(f32[256,128]{1,0:T(8,128)S(1)} %get-tuple-element.57.own_b), channel_id=1, source_target_pairs={{8,16},{16,8},{9,17},{17,9},{10,18},{18,10},{11,19},{19,11},{12,20... | collective-permute-start | bytes 393224 | tf_op jit(solution)/shard_map/ppermute | solution.py:528
  17.3 1.3 %shard_map.146 = (f32[8,256,128]{2,1,0:T(8,128)S(1)}, f32[256,128]{1,0:T(8,128)S(1)}, f32[256,128]{1,0:T(8,128)S(1)}) custom-call(f32[2,16,72,128]{3,2,1,0:T(8,128)S(1)} %get-tuple-element.38.across, f32[16,32,8,128]{3,2,1,0:T(8,128)S(1)} %get-tuple-element.39.turned, f32[512,128]{1,0:T(8,128)S(1)} %get-tuple-element.40.edges, ...), custom_call_target="tpu_custom_call" | custom-call | flops 500000000 | bytes 1048576 | tf_op jit(solution)/shard_map/pallas_call | solution.py:533
  18.7 0.1 collective-permute-start.1
  18.7 4.1 %collective-permute-start.2 = (f32[256,128]{1,0:T(8,128)S(1)}, f32[256,128]{1,0:T(8,128)S(1)}, u32[]{:S(2)}, u32[]{:S(2)}) collective-permute-start(f32[256,128]{1,0:T(8,128)S(1)} %get-tuple-element.44.own_b), channel_id=1, source_target_pairs={{8,16},{16,8},{9,17},{17,9},{10,18},{18,10},{11,19},{19,11},{12,20... | collective-permute-start | bytes 393224 | tf_op jit(solution)/shard_map/ppermute | solution.py:528
  22.8 0.0 copy-done.10
  22.8 0.0 copy-done.11
  22.8 0.0 copy-done.13
  22.9 0.0 copy-done.14
  22.9 1.0 %shard_map.152 = (f32[32,8,8,256]{3,2,1,0:T(8,128)S(1)}, bf16[4,128,256]{2,1,0:T(8,128)(2,1)S(1)}, bf16[4,128,256]{2,1,0:T(8,128)(2,1)S(1)}) custom-call(f32[8,256,128]{2,1,0:T(8,128)S(1)} %get-tuple-element.54.products, bf16[3,128,256]{2,1,0:T(8,128)(2,1)S(1)} %copy-done.10, bf16[3,128,256]{2,1,0:T(8,128)(2,1)S(1)} %copy-done.11, ...), custom_call_target="tpu_custom_call" | custom-call | flops 500000000 | bytes 1048576 | tf_op jit(solution)/shard_map/pallas_call | solution.py:533
  23.8 0.0 collective-permute-done.5.got_a
  23.9 0.0 collective-permute-done.6.got_b
  23.9 0.0 copy-done.6
  23.9 0.0 copy-done.7
  23.9 0.0 copy-done.9
  23.9 1.3 %shard_map.153 = (f32[32,8,8,256]{3,2,1,0:T(8,128)S(1)}, f32[136,8,128]{2,1,0:T(8,128)S(1)}, f32[136,8,128]{2,1,0:T(8,128)S(1)}, f32[8,8,128]{2,1,0:T(8,128)S(1)}) custom-call(f32[32,8,8,256]{3,2,1,0:T(8,128)S(1)} %get-tuple-element.55.partial, f32[256,128]{1,0:T(8,128)S(1)} %get-tuple-element.56.own_a, f32[256,128]{1,0:T(8,128)S(1)} %get-tuple-element.57.own_b, ...), custom_call_target="tpu_custom_call" | custom-call | flops 500000000 | bytes 1048576 | tf_op jit(solution)/shard_map/pallas_call | solution.py:533
  25.2 0.1 collective-permute-start.7
  25.3 2.8 %collective-permute-start.8 = (f32[136,8,128]{2,1,0:T(8,128)S(1)}, f32[136,8,128]{2,1,0:T(8,128)S(1)}, u32[]{:S(2)}, u32[]{:S(2)}) collective-permute-start(f32[136,8,128]{2,1,0:T(8,128)S(1)} %get-tuple-element.64), channel_id=1, source_target_pairs={{1,2},{2,1},{3,4},{4,3},{5,6},{6,5},{9,10},{10,9},{11,12},{12,11},... | collective-permute-start | bytes 1671176 | tf_op jit(solution)/shard_map/ppermute | solution.py:528
  28.0 1.0 %shard_map.147 = (f32[32,8,8,256]{3,2,1,0:T(8,128)S(1)}, bf16[4,128,256]{2,1,0:T(8,128)(2,1)S(1)}, bf16[4,128,256]{2,1,0:T(8,128)(2,1)S(1)}) custom-call(f32[8,256,128]{2,1,0:T(8,128)S(1)} %get-tuple-element.41.products, bf16[3,128,256]{2,1,0:T(8,128)(2,1)S(1)} %copy-done.10, bf16[3,128,256]{2,1,0:T(8,128)(2,1)S(1)} %copy-done.11, ...), custom_call_target="tpu_custom_call" | custom-call | flops 500000000 | bytes 1048576 | tf_op jit(solution)/shard_map/pallas_call | solution.py:533
  29.0 0.0 collective-permute-done.1.got_a
  29.0 0.0 collective-permute-done.2.got_b
  29.0 1.3 %shard_map.148 = (f32[32,8,8,256]{3,2,1,0:T(8,128)S(1)}, f32[136,8,128]{2,1,0:T(8,128)S(1)}, f32[136,8,128]{2,1,0:T(8,128)S(1)}, f32[8,8,128]{2,1,0:T(8,128)S(1)}) custom-call(f32[32,8,8,256]{3,2,1,0:T(8,128)S(1)} %get-tuple-element.42.partial, f32[256,128]{1,0:T(8,128)S(1)} %get-tuple-element.43.own_a, f32[256,128]{1,0:T(8,128)S(1)} %get-tuple-element.44.own_b, ...), custom_call_target="tpu_custom_call" | custom-call | flops 500000000 | bytes 1048576 | tf_op jit(solution)/shard_map/pallas_call | solution.py:533
  30.3 0.1 collective-permute-start.3
  30.4 2.8 %collective-permute-start.4 = (f32[136,8,128]{2,1,0:T(8,128)S(1)}, f32[136,8,128]{2,1,0:T(8,128)S(1)}, u32[]{:S(2)}, u32[]{:S(2)}) collective-permute-start(f32[136,8,128]{2,1,0:T(8,128)S(1)} %get-tuple-element.51), channel_id=1, source_target_pairs={{1,2},{2,1},{3,4},{4,3},{5,6},{6,5},{9,10},{10,9},{11,12},{12,11},... | collective-permute-start | bytes 1671176 | tf_op jit(solution)/shard_map/ppermute | solution.py:528
  33.2 0.0 copy-start.2
  33.2 0.0 copy-start.3
  33.3 0.0 copy-start.8
  33.3 1.4 %shard_map.154 = (f32[8,32,8,128]{3,2,1,0:T(8,128)S(1)}, f32[8,16,8,128]{3,2,1,0:T(8,128)S(1)}) custom-call(f32[32,8,8,256]{3,2,1,0:T(8,128)S(1)} %get-tuple-element.60.filtered), custom_call_target="tpu_custom_call" | custom-call | flops 500000000 | bytes 1048576 | tf_op jit(solution)/shard_map/pallas_call | solution.py:533
  34.7 1.4 %shard_map.149 = (f32[8,32,8,128]{3,2,1,0:T(8,128)S(1)}, f32[8,16,8,128]{3,2,1,0:T(8,128)S(1)}) custom-call(f32[32,8,8,256]{3,2,1,0:T(8,128)S(1)} %get-tuple-element.47.filtered), custom_call_target="tpu_custom_call" | custom-call | flops 500000000 | bytes 1048576 | tf_op jit(solution)/shard_map/pallas_call | solution.py:533
  36.1 0.0 collective-permute-done.7.got_a
  36.1 0.3 collective-permute-done.8.got_b
  36.4 0.0 copy-done.2
  36.4 0.0 copy-done.3
  36.4 0.0 copy-done.8
  36.4 1.8 %shard_map.155 = (f32[8,32,128]{2,1,0:T(8,128)S(1)}, f32[8,128]{1,0:T(8,128)S(1)}, f32[8,256]{1,0:T(8,128)S(1)}) custom-call(f32[8,32,8,128]{3,2,1,0:T(8,128)S(1)} %get-tuple-element.61.fine, f32[8,16,8,128]{3,2,1,0:T(8,128)S(1)} %get-tuple-element.62.coarse, f32[136,8,128]{2,1,0:T(8,128)S(1)} %collective-permute-done.7.got_a, ...), custom_call_target="tpu_custom_call" | custom-call | flops 500000000 | bytes 1048576 | tf_op jit(solution)/shard_map/pallas_call | solution.py:533
  38.2 2.1 %collective-permute-start.10 = (f32[8,256]{1,0:T(8,128)S(1)}, f32[8,256]{1,0:T(8,128)S(1)}, u32[]{:S(2)}, u32[]{:S(2)}) collective-permute-start(f32[8,256]{1,0:T(8,128)S(1)} %get-tuple-element.70), channel_id=1, source_target_pairs={{1,0},{2,1},{3,2},{4,3},{5,4},{6,5},{7,6},{9,8},{10,9},{11,10},{12... | collective-permute-start | bytes 24584 | tf_op jit(solution)/shard_map/ppermute | solution.py:627
  40.3 0.0 collective-permute-done.3.got_a
  40.3 1.8 %collective-permute-done.4.got_b = f32[136,8,128]{2,1,0:T(8,128)S(1)} collective-permute-done((f32[136,8,128]{2,1,0:T(8,128)S(1)}, f32[136,8,128]{2,1,0:T(8,128)S(1)}, u32[]{:S(2)}, u32[]{:S(2)}) %collective-permute-start.4) | collective-permute-done | bytes 557088 | tf_op jit(solution)/shard_map/ppermute | solution.py:528
  42.2 1.8 %shard_map.150 = (f32[8,32,128]{2,1,0:T(8,128)S(1)}, f32[8,128]{1,0:T(8,128)S(1)}, f32[8,256]{1,0:T(8,128)S(1)}) custom-call(f32[8,32,8,128]{3,2,1,0:T(8,128)S(1)} %get-tuple-element.48.fine, f32[8,16,8,128]{3,2,1,0:T(8,128)S(1)} %get-tuple-element.49.coarse, f32[136,8,128]{2,1,0:T(8,128)S(1)} %collective-permute-done.3.got_a, ...), custom_call_target="tpu_custom_call" | custom-call | flops 500000000 | bytes 1048576 | tf_op jit(solution)/shard_map/pallas_call | solution.py:533
  44.0 2.3 %collective-permute-start.9 = (f32[8,256]{1,0:T(8,128)S(1)}, f32[8,256]{1,0:T(8,128)S(1)}, u32[]{:S(2)}, u32[]{:S(2)}) collective-permute-start(f32[8,256]{1,0:T(8,128)S(1)} %get-tuple-element.69), channel_id=1, source_target_pairs={{1,0},{2,1},{3,2},{4,3},{5,4},{6,5},{7,6},{9,8},{10,9},{11,10},{12... | collective-permute-start | bytes 24584 | tf_op jit(solution)/shard_map/ppermute | solution.py:627
  46.3 0.0 collective-permute-done.10.refs_5_
  46.3 2.6 %collective-permute-done.9.refs_4_ = f32[8,256]{1,0:T(8,128)S(1)} collective-permute-done((f32[8,256]{1,0:T(8,128)S(1)}, f32[8,256]{1,0:T(8,128)S(1)}, u32[]{:S(2)}, u32[]{:S(2)}) %collective-permute-start.9) | collective-permute-done | bytes 8224 | tf_op jit(solution)/shard_map/ppermute | solution.py:627
  48.9 0.0 copy-done.12
  48.9 2.2 %shard_map.156 = f32[16,64,256]{2,1,0:T(8,128)} custom-call(f32[8,32,128]{2,1,0:T(8,128)S(1)} %get-tuple-element.53.refs_0_, f32[8,32,128]{2,1,0:T(8,128)S(1)} %get-tuple-element.66.refs_1_, f32[8,128]{1,0:T(8,128)S(1)} %get-tuple-element.67.refs_2_, f32[8,128]{1,0:T(8,128)S(1)} %get-tuple-element.68.refs_3_, f32[8,256]{1,0:T(8,128)S(1)} %collective-permute-done.9.refs_4_, ...), custom_call_target="tpu_custom_call" | custom-call | flops 500000000 | bytes 1048576 | tf_op jit(solution)/shard_map/pallas_call | solution.py:533
  (2 shorter events, 0.0 us)
Async XLA Ops:
  0.9 11.5 %collective-permute-start = (f32[16,256]{1,0:T(8,128)S(1)}, f32[16,256]{1,0:T(8,128)S(1)}, u32[]{:S(2)}, u32[]{:S(2)}) collective-permute-start(f32[16,256]{1,0:T(8,128)S(1)} %bitcast.3), channel_id=1, source_target_pairs={{0,1},{1,2},{2,3},{3,4},{4,5},{5,6},{6,7},{8,9},{9,10},{10,11},{11... | collective-permute-start | bytes 49160 | tf_op jit(solution)/shard_map/ppermute | solution.py:559
  4.7 1.6 %copy-start = (f32[8,16,32,128]{3,2,1,0:T(8,128)S(1)}, f32[8,16,32,128]{3,2,1,0:T(8,128)}, u32[]{:S(2)}) copy-start(f32[8,16,32,128]{3,2,1,0:T(8,128)} %members.1) | copy-start | bytes 6291460
  6.3 0.9 %copy-start.4 = (bf16[256,256]{1,0:T(8,128)(2,1)S(1)}, bf16[256,256]{1,0:T(8,128)(2,1)}, u32[]{:S(2)}) copy-start(bf16[256,256]{1,0:T(8,128)(2,1)} %constant.30.clone.restrict) | copy-start | bytes 393220
  7.2 1.2 %copy-start.5 = (f32[16,64,256]{2,1,0:T(8,128)S(1)}, f32[16,64,256]{2,1,0:T(8,128)}, u32[]{:S(2)}) copy-start(f32[16,64,256]{2,1,0:T(8,128)} %gradient.1) | copy-start | bytes 3145732
  8.4 4.0 %copy-start.1 = (bf16[1024,256]{1,0:T(8,128)(2,1)S(1)}, bf16[1024,256]{1,0:T(8,128)(2,1)}, u32[]{:S(2)}) copy-start(bf16[1024,256]{1,0:T(8,128)(2,1)} %constant.39.packing) | copy-start | bytes 1572868
  13.8 10.1 %collective-permute-start.5 = (f32[256,128]{1,0:T(8,128)S(1)}, f32[256,128]{1,0:T(8,128)S(1)}, u32[]{:S(2)}, u32[]{:S(2)}) collective-permute-start(f32[256,128]{1,0:T(8,128)S(1)} %get-tuple-element.56.own_a), channel_id=1, source_target_pairs={{0,8},{8,0},{16,24},{24,16},{1,9},{9,1},{17,25},{25,17},{2,10},{10... | collective-permute-start | bytes 393224 | tf_op jit(solution)/shard_map/ppermute | solution.py:528
  15.0 7.8 %copy-start.10 = (bf16[3,128,256]{2,1,0:T(8,128)(2,1)S(1)}, bf16[3,128,256]{2,1,0:T(8,128)(2,1)}, u32[]{:S(2)}) copy-start(bf16[3,128,256]{2,1,0:T(8,128)(2,1)} %constant.26.clone.high_tables) | copy-start | bytes 589828
  15.0 7.8 %copy-start.11 = (bf16[3,128,256]{2,1,0:T(8,128)(2,1)S(1)}, bf16[3,128,256]{2,1,0:T(8,128)(2,1)}, u32[]{:S(2)}) copy-start(bf16[3,128,256]{2,1,0:T(8,128)(2,1)} %constant.27.clone.low_tables) | copy-start | bytes 589828
  15.0 7.8 %copy-start.13 = (bf16[3,2,32,256]{3,2,1,0:T(8,128)(2,1)S(1)}, bf16[3,2,32,256]{3,2,1,0:T(8,128)(2,1)}, u32[]{:S(2)}) copy-start(bf16[3,2,32,256]{3,2,1,0:T(8,128)(2,1)} %constant.28.clone.halo_highs) | copy-start | bytes 294916
  15.0 7.8 %copy-start.14 = (bf16[3,2,32,256]{3,2,1,0:T(8,128)(2,1)S(1)}, bf16[3,2,32,256]{3,2,1,0:T(8,128)(2,1)}, u32[]{:S(2)}) copy-start(bf16[3,2,32,256]{3,2,1,0:T(8,128)(2,1)} %constant.29.clone.halo_lows) | copy-start | bytes 294916
  15.1 8.8 %copy-start.6 = (bf16[256,128]{1,0:T(8,128)(2,1)S(1)}, bf16[256,128]{1,0:T(8,128)(2,1)}, u32[]{:S(2)}) copy-start(bf16[256,128]{1,0:T(8,128)(2,1)} %constant.34.clone.beyond_high) | copy-start | bytes 196612
  15.1 8.8 %copy-start.7 = (bf16[256,128]{1,0:T(8,128)(2,1)S(1)}, bf16[256,128]{1,0:T(8,128)(2,1)}, u32[]{:S(2)}) copy-start(bf16[256,128]{1,0:T(8,128)(2,1)} %constant.35.clone.beyond_low) | copy-start | bytes 196612
  15.1 8.8 %copy-start.9 = (bf16[128,128]{1,0:T(8,128)(2,1)S(1)}, bf16[128,128]{1,0:T(8,128)(2,1)}, u32[]{:S(2)}) copy-start(bf16[128,128]{1,0:T(8,128)(2,1)} %constant.38.clone.choice) | copy-start | bytes 98308
  15.1 8.8 %collective-permute-start.6 = (f32[256,128]{1,0:T(8,128)S(1)}, f32[256,128]{1,0:T(8,128)S(1)}, u32[]{:S(2)}, u32[]{:S(2)}) collective-permute-start(f32[256,128]{1,0:T(8,128)S(1)} %get-tuple-element.57.own_b), channel_id=1, source_target_pairs={{8,16},{16,8},{9,17},{17,9},{10,18},{18,10},{11,19},{19,11},{12,20... | collective-permute-start | bytes 393224 | tf_op jit(solution)/shard_map/ppermute | solution.py:528
  18.7 10.4 %collective-permute-start.1 = (f32[256,128]{1,0:T(8,128)S(1)}, f32[256,128]{1,0:T(8,128)S(1)}, u32[]{:S(2)}, u32[]{:S(2)}) collective-permute-start(f32[256,128]{1,0:T(8,128)S(1)} %get-tuple-element.43.own_a), channel_id=1, source_target_pairs={{0,8},{8,0},{16,24},{24,16},{1,9},{9,1},{17,25},{25,17},{2,10},{10... | collective-permute-start | bytes 393224 | tf_op jit(solution)/shard_map/ppermute | solution.py:528
  18.7 10.3 %collective-permute-start.2 = (f32[256,128]{1,0:T(8,128)S(1)}, f32[256,128]{1,0:T(8,128)S(1)}, u32[]{:S(2)}, u32[]{:S(2)}) collective-permute-start(f32[256,128]{1,0:T(8,128)S(1)} %get-tuple-element.44.own_b), channel_id=1, source_target_pairs={{8,16},{16,8},{9,17},{17,9},{10,18},{18,10},{11,19},{19,11},{12,20... | collective-permute-start | bytes 393224 | tf_op jit(solution)/shard_map/ppermute | solution.py:528
  25.2 10.9 %collective-permute-start.7 = (f32[136,8,128]{2,1,0:T(8,128)S(1)}, f32[136,8,128]{2,1,0:T(8,128)S(1)}, u32[]{:S(2)}, u32[]{:S(2)}) collective-permute-start(f32[136,8,128]{2,1,0:T(8,128)S(1)} %get-tuple-element.63.own_rows), channel_id=1, source_target_pairs={{0,1},{1,0},{2,3},{3,2},{4,5},{5,4},{6,7},{7,6},{8,9},{9,8},{10,11... | collective-permute-start | bytes 1671176 | tf_op jit(solution)/shard_map/ppermute | solution.py:528
  25.3 11.1 %collective-permute-start.8 = (f32[136,8,128]{2,1,0:T(8,128)S(1)}, f32[136,8,128]{2,1,0:T(8,128)S(1)}, u32[]{:S(2)}, u32[]{:S(2)}) collective-permute-start(f32[136,8,128]{2,1,0:T(8,128)S(1)} %get-tuple-element.64), channel_id=1, source_target_pairs={{1,2},{2,1},{3,4},{4,3},{5,6},{6,5},{9,10},{10,9},{11,12},{12,11},... | collective-permute-start | bytes 1671176 | tf_op jit(solution)/shard_map/ppermute | solution.py:528
  30.3 10.0 %collective-permute-start.3 = (f32[136,8,128]{2,1,0:T(8,128)S(1)}, f32[136,8,128]{2,1,0:T(8,128)S(1)}, u32[]{:S(2)}, u32[]{:S(2)}) collective-permute-start(f32[136,8,128]{2,1,0:T(8,128)S(1)} %get-tuple-element.50.own_rows), channel_id=1, source_target_pairs={{0,1},{1,0},{2,3},{3,2},{4,5},{5,4},{6,7},{7,6},{8,9},{9,8},{10,11... | collective-permute-start | bytes 1671176 | tf_op jit(solution)/shard_map/ppermute | solution.py:528
  30.4 11.8 %collective-permute-start.4 = (f32[136,8,128]{2,1,0:T(8,128)S(1)}, f32[136,8,128]{2,1,0:T(8,128)S(1)}, u32[]{:S(2)}, u32[]{:S(2)}) collective-permute-start(f32[136,8,128]{2,1,0:T(8,128)S(1)} %get-tuple-element.51), channel_id=1, source_target_pairs={{1,2},{2,1},{3,4},{4,3},{5,6},{6,5},{9,10},{10,9},{11,12},{12,11},... | collective-permute-start | bytes 1671176 | tf_op jit(solution)/shard_map/ppermute | solution.py:528
  33.2 3.2 %copy-start.2 = (bf16[3,3,128,128]{3,2,1,0:T(8,128)(2,1)S(1)}, bf16[3,3,128,128]{3,2,1,0:T(8,128)(2,1)}, u32[]{:S(2)}) copy-start(bf16[3,3,128,128]{3,2,1,0:T(8,128)(2,1)} %constant.36.clone.row_highs) | copy-start | bytes 884740
  33.2 3.2 %copy-start.3 = (bf16[3,3,128,128]{3,2,1,0:T(8,128)(2,1)S(1)}, bf16[3,3,128,128]{3,2,1,0:T(8,128)(2,1)}, u32[]{:S(2)}) copy-start(bf16[3,3,128,128]{3,2,1,0:T(8,128)(2,1)} %constant.37.clone.row_lows) | copy-start | bytes 884740
  33.3 3.2 %copy-start.8 = (bf16[128,128]{1,0:T(8,128)(2,1)S(1)}, bf16[128,128]{1,0:T(8,128)(2,1)}, u32[]{:S(2)}) copy-start(bf16[128,128]{1,0:T(8,128)(2,1)} %constant.32.clone.refining) | copy-start | bytes 98308
  38.2 8.1 %collective-permute-start.10 = (f32[8,256]{1,0:T(8,128)S(1)}, f32[8,256]{1,0:T(8,128)S(1)}, u32[]{:S(2)}, u32[]{:S(2)}) collective-permute-start(f32[8,256]{1,0:T(8,128)S(1)} %get-tuple-element.70), channel_id=1, source_target_pairs={{1,0},{2,1},{3,2},{4,3},{5,4},{6,5},{7,6},{9,8},{10,9},{11,10},{12... | collective-permute-start | bytes 24584 | tf_op jit(solution)/shard_map/ppermute | solution.py:627
  42.2 6.8 %copy-start.12 = (bf16[256,256]{1,0:T(8,128)(2,1)S(1)}, bf16[256,256]{1,0:T(8,128)(2,1)}, u32[]{:S(2)}) copy-start(bf16[256,256]{1,0:T(8,128)(2,1)} %constant.33.clone.refs_6_) | copy-start | bytes 393220
  44.0 5.0 %collective-permute-start.9 = (f32[8,256]{1,0:T(8,128)S(1)}, f32[8,256]{1,0:T(8,128)S(1)}, u32[]{:S(2)}, u32[]{:S(2)}) collective-permute-start(f32[8,256]{1,0:T(8,128)S(1)} %get-tuple-element.69), channel_id=1, source_target_pairs={{1,0},{2,1},{3,2},{4,3},{5,4},{6,5},{7,6},{9,8},{10,9},{11,10},{12... | collective-permute-start | bytes 24584 | tf_op jit(solution)/shard_map/ppermute | solution.py:627

commit v3 on v2

--- a/solution.py
+++ b/solution.py
@@ -197,7 +197,9 @@
     return pl.ds(pl.multiple_of(index * 8, 8), 8)
 
 
-def prepare_kernel(height, gradient, members, restrict, across, turned, edges, fine, raw, table, sems):
+def prepare_kernel(height, gradient, members, restrict, own_tables, halo_tables, across, turned, edges, high_weights, low_weights,
+                   fine, raw, table, own_case, halo_case, sems):
+    case = column_case()
     blocks = height // GROUP
     levels = members.shape[1]
     part = levels // 4
@@ -208,6 +210,8 @@
     for i in range(4):
         span = pl.ds(i * part, part)
         copies.append(pltpu.make_async_copy(members.at[:, span], raw.at[:, span], sems.at[4 + i]))
+    copies.append(pltpu.make_async_copy(own_tables.at[case], own_case, sems.at[9]))
+    copies.append(pltpu.make_async_copy(halo_tables.at[case], halo_case, sems.at[10]))
     for copy in copies:
         copy.start()
     copies[0].wait()
@@ -219,6 +223,15 @@
         value = value.reshape(part, 2 * height, 2 * LANES)
         for half in range(2):
             across[half, i * part:(i + 1) * part, 8:, :] = value[:, :, half * LANES:(half + 1) * LANES]
+    copies[9].wait()
+    copies[10].wait()
+    for part_of, target in ((0, high_weights), (1, low_weights)):
+        for variant in range(4):
+            target[variant, :LANES, :] = own_case[part_of]
+            target[variant, LANES:, :] = jnp.zeros((LANES, 2 * LANES), BF16)
+            for side in range(2):
+                start = LANES + side * 64 + variant * SLOT
+                target[variant, start:start + SLOT, :] = halo_case[part_of, variant % 2, side * SLOT:(side + 1) * SLOT, :]
     rows = raw.reshape(8 * levels * height, LANES)
     lane = lax.broadcasted_iota(jnp.int32, (GROUP, LANES), 1)
 
@@ -278,21 +291,7 @@
     message_b[...] = jnp.where(even, to_west, to_east)
 
 
-def own_columns_kernel(levels, height, products, high_tables, low_tables, halo_highs, halo_lows, filtered, halo_high, halo_low):
-    groups = levels * height // GROUP
-    case = column_case()
-    for variant in range(4):
-        for source, target in ((halo_highs, halo_high), (halo_lows, halo_low)):
-            target[variant] = jnp.zeros((LANES, 2 * LANES), BF16)
-            kind = variant % 2
-            target[variant, variant * SLOT:(variant + 1) * SLOT, :] = source[case, kind, :SLOT, :]
-            target[variant, 64 + variant * SLOT:64 + (variant + 1) * SLOT, :] = source[case, kind, SLOT:, :]
-    high, low = high_tables[case], low_tables[case]
-    for line in range(GROUP):
-        filtered[:, line] = three_dots(products[line], high, low).reshape(groups, 8, 2 * LANES)
-
-
-def columns_kernel(levels, height, partial, own_a, own_b, got_a, got_b, halo_high, halo_low, beyond_high, beyond_low, choice,
+def columns_kernel(levels, height, products, own_a, own_b, got_a, got_b, high_weights, low_weights, beyond_high, beyond_low, choice,
                    filtered, message_a, message_b, factors):
     blocks = height // GROUP
     groups = levels * blocks
@@ -321,9 +320,10 @@
         split(jnp.where(lane < 64, pltpu.roll(west, 64, 1), east)),
     ]
     for line in range(GROUP):
-        high, low = halves[line // 4]
-        value = mul(high, halo_high[line % 4]) + mul(low, halo_high[line % 4]) + mul(high, halo_low[line % 4])
-        filtered[:, line] = partial[:, line] + value.reshape(groups, 8, 2 * LANES)
+        high, low = (jnp.concatenate(pair, axis=1) for pair in zip(split(products[line]), halves[line // 4]))
+        weights = high_weights[line % 4]
+        value = mul(high, weights) + mul(low, weights) + mul(high, low_weights[line % 4])
+        filtered[:, line] = value.reshape(groups, 8, 2 * LANES)
     small = lax.broadcasted_iota(jnp.int32, (8, LANES), 1)
     second = small < 64
     up_a = lax.axis_index("gy") % 2 == 0
@@ -410,8 +410,8 @@
     lax.fori_loop(0, levels, level_step, 0)
 
 
-def combine_kernel(chunk, levels, height, fine, coarse, got_a, got_b, own_rows, factors, turned, refining,
-                   row_highs, row_lows, combined, beyond, first_row, stacked, refined, weighted):
+def combine_kernel(chunk, levels, height, fine, coarse, got_a, got_b, own_rows, factors, turned, refining, row_highs, row_lows, *refs):
+    earlier, (combined, beyond, first_row, stacked, refined, weighted) = refs[:-6], refs[-6:]
     blocks = height // GROUP
     half, quarter = height // 2, height // 4
     first = chunk * levels
@@ -483,38 +483,48 @@
         return 0
 
     lax.fori_loop(0, levels, level_step, 0)
+    for rows in earlier:
+        first_row[:first, :] = rows[...]
     for level in range(levels):
-        first_row[level:level + 1, :LANES] = combined[level, 0:1, :]
-    first_row[:, LANES:] = beyond[...]
+        first_row[first + level:first + level + 1, :LANES] = combined[level, 0:1, :]
+    first_row[first:, LANES:] = beyond[...]
 
 
 def interpolate_kernel(height, *refs):
-    chunks = (len(refs) - 4) // 3
-    interpolation, out, extended, rows = refs[-4:]
+    chunks = (len(refs) - 7) // 2
+    north, interpolation, out, extended, rows, ready, sems = refs[-7:]
     levels = refs[0].shape[0]
+    part = levels // 2
     lane = lax.broadcasted_iota(jnp.int32, (height, LANES), 1)
     line = lax.broadcasted_iota(jnp.int32, (height, LANES), 0)
     row_lane = lax.broadcasted_iota(jnp.int32, (1, LANES), 1)
-    for chunk in range(chunks):
-        combined, beyond, north = refs[chunk], refs[chunks + chunk], refs[2 * chunks + chunk]
-        for level in range(levels):
-            here = combined[level]
-            last = jnp.broadcast_to(beyond[level:level + 1, :], (height, LANES))
+    copies = []
+    for start in range(0, chunks * levels, part):
+        combined, beyond = refs[start // levels], refs[chunks + start // levels]
+        for i in range(part):
+            level = start + i
+            here = combined[level % levels]
+            last = jnp.broadcast_to(beyond[level % levels:level % levels + 1, :], (height, LANES))
             last = jnp.sum(jnp.where(lane == line, last, 0.0), axis=1, keepdims=True)
             after = north[level:level + 1, :LANES]
             corner = jnp.broadcast_to(north[level:level + 1, LANES:LANES + 1], (1, LANES))
-            extended[0, 0:height, :] = here
-            extended[0, height:height + 1, :] = after
-            extended[1, 0:height, :] = jnp.where(lane == LANES - 1, last, pltpu.roll(here, LANES - 1, 1))
-            extended[1, height:height + 1, :] = jnp.where(row_lane == LANES - 1, corner, pltpu.roll(after, LANES - 1, 1))
+            extended[0, i, 0:height, :] = here
+            extended[0, i, height:height + 1, :] = after
+            extended[1, i, 0:height, :] = jnp.where(lane == LANES - 1, last, pltpu.roll(here, LANES - 1, 1))
+            extended[1, i, height:height + 1, :] = jnp.where(row_lane == LANES - 1, corner, pltpu.roll(after, LANES - 1, 1))
             for half in range(2):
-                value = extended[half, 0:height, :]
-                rows[half, level, pl.ds(0, height, 2), :] = value
-                rows[half, level, pl.ds(1, height, 2), :] = 0.5 * (value + extended[half, 1:height + 1, :])
+                value = extended[half, i, 0:height, :]
+                rows[half, i, pl.ds(0, height, 2), :] = value
+                rows[half, i, pl.ds(1, height, 2), :] = 0.5 * (value + extended[half, i, 1:height + 1, :])
         value = exact_dot(
-            jnp.concatenate([rows[half].reshape(levels * 2 * height, LANES) for half in range(2)], axis=1), interpolation[...]
+            jnp.concatenate([rows[half].reshape(part * 2 * height, LANES) for half in range(2)], axis=1), interpolation[...]
         )
-        out[chunk * levels:(chunk + 1) * levels] = value.reshape(levels, 2 * height, out.shape[2])
+        span = pl.ds(start, part)
+        ready[span] = value.reshape(part, 2 * height, ready.shape[2])
+        copies.append(pltpu.make_async_copy(ready.at[span], out.at[span], sems.at[start // part]))
+        copies[-1].start()
+    for copy in copies:
+        copy.wait()
 
 
 def partner(index, size, second):
@@ -528,13 +538,13 @@
     return lax.ppermute(value, axis, [(i, j) for i, j in pairs if j is not None])
 
 
-def call(kernel, outs, scratch, cost, *args, in_hbm=0):
+def call(kernel, outs, scratch, cost, *args, in_hbm=0, out_hbm=False):
     vmem = pl.BlockSpec(memory_space=pltpu.VMEM)
     return pl.pallas_call(
         kernel,
         out_shape=tuple(jax.ShapeDtypeStruct(*out) if isinstance(out[0], tuple) else jax.ShapeDtypeStruct(out, F32) for out in outs),
         in_specs=[pl.BlockSpec(memory_space=pltpu.HBM) if i < in_hbm else vmem for i in range(len(args))],
-        out_specs=tuple(vmem for _ in outs),
+        out_specs=tuple(pl.BlockSpec(memory_space=pltpu.HBM) if out_hbm else vmem for _ in outs),
         scratch_shapes=[pltpu.VMEM(shape, F32) if isinstance(shape, tuple) else shape for shape in scratch],
         compiler_params=pltpu.CompilerParams(vmem_limit_bytes=VMEM_LIMIT),
         cost_estimate=pl.CostEstimate(flops=cost, bytes_accessed=2**20, transcendentals=0),
@@ -543,7 +553,7 @@
 
 def halves_of(table):
     high = table.astype(np.float32).astype(BF16)
-    return jnp.asarray(high), jnp.asarray((table.astype(np.float32) - high.astype(np.float32)).astype(BF16))
+    return high, (table.astype(np.float32) - high.astype(np.float32)).astype(BF16)
 
 
 def shards(gradient, members):
@@ -559,23 +569,26 @@
     south = lax.ppermute(gradient[:, -1, :], "gy", up)
 
     columns = [column_table(width, i == 0, i == 2) for i in range(3)]
-    high_tables, low_tables = halves_of(np.stack([table[:width] for table in columns]))
-    halo_highs, halo_lows = halves_of(np.stack([halo_table(table, width) for table in columns]))
+    own_tables = np.stack(halves_of(np.stack([table[:width] for table in columns])), axis=1)
+    halo_tables = np.stack(halves_of(np.stack([halo_table(table, width) for table in columns])), axis=1)
     restrict = jnp.asarray(restriction_table(width), BF16)
     packing = jnp.asarray(packing_table(width), BF16).reshape(GROUP * width, 2 * LANES)
     refining = jnp.asarray(refining_table(width), BF16)
     interpolation = jnp.asarray(interpolation_table(width), BF16)
-    beyond_high, beyond_low = halves_of(column_filter_table(width))
-    row_highs, row_lows = halves_of(np.stack([column_rows_table(height, i == 0, i == 2) for i in range(3)]))
+    beyond_high, beyond_low = map(jnp.asarray, halves_of(column_filter_table(width)))
+    row_highs, row_lows = map(jnp.asarray, halves_of(np.stack([column_rows_table(height, i == 0, i == 2) for i in range(3)])))
     choice = jnp.asarray(edge_choice_table(), BF16)
     flops = 10**9 // CHUNKS
     far_rows = (levels * 17, 8, LANES)
 
-    across, turned, edges = call(
+    constants = (restrict, jnp.asarray(own_tables), jnp.asarray(halo_tables))
+    across, turned, edges, high_weights, low_weights = call(
         functools.partial(prepare_kernel, height),
-        [(2, all_levels, 8 + 2 * height, LANES), (all_levels, height, 8, LANES), (all_levels * height, LANES)],
-        [gradient.shape, members.shape, pltpu.VMEM(restrict.shape, BF16), pltpu.SemaphoreType.DMA((9,))],
-        flops, gradient, members, restrict, in_hbm=3,
+        [(2, all_levels, 8 + 2 * height, LANES), (all_levels, height, 8, LANES), (all_levels * height, LANES),
+         ((4, 2 * LANES, 2 * LANES), BF16), ((4, 2 * LANES, 2 * LANES), BF16)],
+        [gradient.shape, members.shape, pltpu.VMEM(restrict.shape, BF16), pltpu.VMEM(own_tables.shape[1:], BF16),
+         pltpu.VMEM(halo_tables.shape[1:], BF16), pltpu.SemaphoreType.DMA((11,))],
+        flops, *(pltpu.with_memory_space_constraint(a, pltpu.HBM) for a in (gradient, members) + constants), in_hbm=5,
     )
     packed = [
         call(
@@ -587,21 +600,12 @@
         for chunk in range(CHUNKS)
     ]
     got = [(swap(own_a, "gx", False), swap(own_b, "gx", True)) for _, own_a, own_b in packed]
-    partials = [
-        call(
-            functools.partial(own_columns_kernel, levels, height),
-            [(groups, GROUP, 8, 2 * LANES), ((4, LANES, 2 * LANES), BF16), ((4, LANES, 2 * LANES), BF16)],
-            [],
-            flops, products, high_tables, low_tables, halo_highs, halo_lows,
-        )
-        for products, _, _ in packed
-    ]
     filtered = [
         call(
             functools.partial(columns_kernel, levels, height),
             [(groups, GROUP, 8, 2 * LANES), far_rows, far_rows, (levels, 8, LANES)],
             [],
-            flops, partials[chunk][0], *packed[chunk][1:], *got[chunk], *partials[chunk][1:], beyond_high, beyond_low, choice,
+            flops, *packed[chunk], *got[chunk], high_weights, low_weights, beyond_high, beyond_low, choice,
         )
         for chunk in range(CHUNKS)
     ]
@@ -615,21 +619,25 @@
         )
         for chunk in range(CHUNKS)
     ]
-    combined, beyond, first_rows = zip(*(
-        call(
+    combined, beyond, first_rows = [], [], []
+    for chunk in range(CHUNKS):
+        results = call(
             functools.partial(combine_kernel, chunk, levels, height),
-            [(levels, height, LANES), (levels, LANES), (levels, 2 * LANES)],
+            [(levels, height, LANES), (levels, LANES), ((chunk + 1) * levels, 2 * LANES)],
             [(height // 2 * 8, LANES), (height // 2 * 8, LANES), (64, LANES)],
             flops, *own[chunk], *far[chunk], filtered[chunk][1], filtered[chunk][3], turned, refining, row_highs, row_lows,
+            *first_rows[-1:],
         )
-        for chunk in range(CHUNKS)
-    ))
-    norths = [lax.ppermute(row, "gy", [(j, i) for i, j in up]) for row in first_rows]
+        for result, into in zip(results, (combined, beyond, first_rows)):
+            into.append(result)
+    north = lax.ppermute(first_rows[-1], "gy", [(j, i) for i, j in up])
+    part = levels // 2
     (out,) = call(
         functools.partial(interpolate_kernel, height),
         [(all_levels, fine_height, fine_width)],
-        [(2, height + 8, LANES), (2, levels, 2 * height, LANES)],
-        flops, *combined, *beyond, *norths, interpolation,
+        [(2, part, height + 8, LANES), (2, part, 2 * height, LANES), (all_levels, fine_height, fine_width),
+         pltpu.SemaphoreType.DMA((2 * CHUNKS,))],
+        flops, *combined, *beyond, north, interpolation, out_hbm=True,
     )
     return out
 

time: 51.5 us -> 47.6 us (0.924)
  local copies, waits for them, and re-layouts: 4.7 us -> 1.03 us
  waiting for transfers between devices: 4.83 us -> 8.47 us
  starting transfers between devices: 21.5 us -> 19.4 us
  Pallas kernels: 19.7 us -> 18.2 us
    unnamed x31 -> x19, local copies, waits for them, and re-layouts: 3.78 us -> 0.05 us
    ppermute x8, waiting for transfers between devices: 2.18 us -> 5.72 us  [swap(): lax.ppermute(value, axis, [(i, j) for i, j in pairs if j is not None])]
    ppermute x2 -> x1, starting transfers between devices: 4.4 us -> 2.3 us  [shards(): north = lax.ppermute(first_rows[-1], 'gy', [(j, i) for i, j in up])]
    pallas_call x12 -> x10, Pallas kernels: 19.7 us -> 18.2 us  [call(): pl.pallas_call(kernel, out_shape=tuple((jax.ShapeDtypeStruct(*out) if isi...]
    ppermute x2 -> x1, waiting for transfers between devices: 2.65 us -> 2.75 us  [shards(): north = lax.ppermute(first_rows[-1], 'gy', [(j, i) for i, j in up])]
  transfers between devices with their start and end apart: 11 -> 10, of which waited for: 3 -> 5; matrix products, arithmetic and copies ran while one was open for 0% -> 0% of each run, Pallas kernels for 32% -> 28%
where the time goes in v3:
time: 47.6 us; the launch traced here: 47.3 us
  starting transfers between devices  19.4 us (41%)
  Pallas kernels  18.2 us (38%)
  waiting for transfers between devices  8.47 us (18%)
  local copies, waits for them, and re-layouts  1.03 us (2%)
    pallas_call x10, Pallas kernels, call(): pl.pallas_call(kernel, out_shape=tuple((jax.ShapeDtypeStruct(*out) if isi...  18.2 us
    ppermute x8, starting transfers between devices, swap(): lax.ppermute(value, axis, [(i, j) for i, j in pairs if j is not None])  13.3 us
    ppermute x8, waiting for transfers between devices, swap(): lax.ppermute(value, axis, [(i, j) for i, j in pairs if j is not None])  5.72 us
    ppermute x1, starting transfers between devices, shards(): south = lax.ppermute(gradient[:, -1, :], 'gy', up)  3.77 us
    ppermute x1, waiting for transfers between devices, shards(): north = lax.ppermute(first_rows[-1], 'gy', [(j, i) for i, j in up])  2.75 us
    ppermute x1, starting transfers between devices, shards(): north = lax.ppermute(first_rows[-1], 'gy', [(j, i) for i, j in up])  2.3 us
    slice x1, local copies, waits for them, and re-layouts, shards(): south = lax.ppermute(gradient[:, -1, :], 'gy', up)  0.99 us
  transfers between devices with their start and end apart: 10, of which 5 were waited for; matrix products, arithmetic and copies ran while one was open for 0% of the time, Pallas kernels for 28%

profile of v3, /device:TPU:21, one launch (start us, length us, event | category | flops | bytes accessed | tf_op | source)
XLA Modules:
  0.0 47.3 jit_solution(6924124581542710587)
XLA Ops:
  0.0 0.0 copy-start.3
  0.0 0.0 copy-start
  0.0 1.0 %slice.3 = f32[16,1,256]{2,1,0:T(1,128)S(1)} slice(f32[16,64,256]{2,1,0:T(8,128)} %gradient.1), slice={[0:16], [63:64], [0:256]} | slice | bytes 32768 | tf_op jit(solution)/shard_map/slice | solution.py:569
  1.0 3.8 %collective-permute-start = (f32[16,256]{1,0:T(8,128)S(1)}, f32[16,256]{1,0:T(8,128)S(1)}, u32[]{:S(2)}, u32[]{:S(2)}) collective-permute-start(f32[16,256]{1,0:T(8,128)S(1)} %bitcast.3), channel_id=1, source_target_pairs={{0,1},{1,2},{2,3},{3,4},{4,5},{5,6},{6,7},{8,9},{9,10},{10,11},{11... | collective-permute-start | bytes 49160 | tf_op jit(solution)/shard_map/ppermute | solution.py:569
  4.8 4.7 %shard_map.127 = (f32[2,16,72,128]{3,2,1,0:T(8,128)S(1)}, f32[16,32,8,128]{3,2,1,0:T(8,128)S(1)}, f32[512,128]{1,0:T(8,128)S(1)}, bf16[4,256,256]{2,1,0:T(8,128)(2,1)S(1)}, bf16[4,256,256]{2,1,0:T(8,128)(2,1)S(1)}) custom-call(f32[16,64,256]{2,1,0:T(8,128)} %gradient.1, f32[8,16,32,128]{3,2,1,0:T(8,128)} %members.1, ...), custom_call_target="tpu_custom_call" | custom-call | flops 500000000 | bytes 1048576 | tf_op jit(solution)/shard_map/pallas_call | solution.py:543
  9.5 0.0 collective-permute-done.south
  9.5 0.0 copy-done.3
  9.5 0.0 copy-done
  9.5 1.3 %shard_map.128 = (f32[8,256,128]{2,1,0:T(8,128)S(1)}, f32[256,128]{1,0:T(8,128)S(1)}, f32[256,128]{1,0:T(8,128)S(1)}) custom-call(f32[2,16,72,128]{3,2,1,0:T(8,128)S(1)} %get-tuple-element.34.across, f32[16,32,8,128]{3,2,1,0:T(8,128)S(1)} %get-tuple-element.35.turned, f32[512,128]{1,0:T(8,128)S(1)} %get-tuple-element.36.edges, ...), custom_call_target="tpu_custom_call" | custom-call | flops 500000000 | bytes 1048576 | tf_op jit(solution)/shard_map/pallas_call | solution.py:543
  10.9 1.3 %collective-permute-start.1 = (f32[256,128]{1,0:T(8,128)S(1)}, f32[256,128]{1,0:T(8,128)S(1)}, u32[]{:S(2)}, u32[]{:S(2)}) collective-permute-start(f32[256,128]{1,0:T(8,128)S(1)} %get-tuple-element.38.own_a), channel_id=1, source_target_pairs={{0,8},{8,0},{16,24},{24,16},{1,9},{9,1},{17,25},{25,17},{2,10},{10... | collective-permute-start | bytes 393224 | tf_op jit(solution)/shard_map/ppermute | solution.py:538
  12.1 0.0 copy-start.4
  12.1 0.0 copy-start.5
  12.1 0.0 copy-start.7
  12.2 2.2 %collective-permute-start.2 = (f32[256,128]{1,0:T(8,128)S(1)}, f32[256,128]{1,0:T(8,128)S(1)}, u32[]{:S(2)}, u32[]{:S(2)}) collective-permute-start(f32[256,128]{1,0:T(8,128)S(1)} %get-tuple-element.39.own_b), channel_id=1, source_target_pairs={{8,16},{16,8},{9,17},{17,9},{10,18},{18,10},{11,19},{19,11},{12,20... | collective-permute-start | bytes 393224 | tf_op jit(solution)/shard_map/ppermute | solution.py:538
  14.4 1.3 %shard_map.132 = (f32[8,256,128]{2,1,0:T(8,128)S(1)}, f32[256,128]{1,0:T(8,128)S(1)}, f32[256,128]{1,0:T(8,128)S(1)}) custom-call(f32[2,16,72,128]{3,2,1,0:T(8,128)S(1)} %get-tuple-element.34.across, f32[16,32,8,128]{3,2,1,0:T(8,128)S(1)} %get-tuple-element.35.turned, f32[512,128]{1,0:T(8,128)S(1)} %get-tuple-element.36.edges, ...), custom_call_target="tpu_custom_call" | custom-call | flops 500000000 | bytes 1048576 | tf_op jit(solution)/shard_map/pallas_call | solution.py:543
  15.7 0.1 collective-permute-start.5
  15.8 4.1 %collective-permute-start.6 = (f32[256,128]{1,0:T(8,128)S(1)}, f32[256,128]{1,0:T(8,128)S(1)}, u32[]{:S(2)}, u32[]{:S(2)}) collective-permute-start(f32[256,128]{1,0:T(8,128)S(1)} %get-tuple-element.51.own_b), channel_id=1, source_target_pairs={{8,16},{16,8},{9,17},{17,9},{10,18},{18,10},{11,19},{19,11},{12,20... | collective-permute-start | bytes 393224 | tf_op jit(solution)/shard_map/ppermute | solution.py:538
  19.9 0.0 collective-permute-done.1.got_a
  19.9 0.4 collective-permute-done.2.got_b
  20.3 0.0 copy-done.4
  20.3 0.0 copy-done.5
  20.3 0.0 copy-done.7
  20.3 1.3 %shard_map.129 = (f32[32,8,8,256]{3,2,1,0:T(8,128)S(1)}, f32[136,8,128]{2,1,0:T(8,128)S(1)}, f32[136,8,128]{2,1,0:T(8,128)S(1)}, f32[8,8,128]{2,1,0:T(8,128)S(1)}) custom-call(f32[8,256,128]{2,1,0:T(8,128)S(1)} %get-tuple-element.37.products, f32[256,128]{1,0:T(8,128)S(1)} %get-tuple-element.38.own_a, f32[256,128]{1,0:T(8,128)S(1)} %get-tuple-element.39.own_b, ...), custom_call_target="tpu_custom_call" | custom-call | flops 500000000 | bytes 1048576 | tf_op jit(solution)/shard_map/pallas_call | solution.py:543
  21.6 0.1 collective-permute-start.3
  21.7 3.4 %collective-permute-start.4 = (f32[136,8,128]{2,1,0:T(8,128)S(1)}, f32[136,8,128]{2,1,0:T(8,128)S(1)}, u32[]{:S(2)}, u32[]{:S(2)}) collective-permute-start(f32[136,8,128]{2,1,0:T(8,128)S(1)} %get-tuple-element.46), channel_id=1, source_target_pairs={{1,2},{2,1},{3,4},{4,3},{5,6},{6,5},{9,10},{10,9},{11,12},{12,11},... | collective-permute-start | bytes 1671176 | tf_op jit(solution)/shard_map/ppermute | solution.py:538
  25.1 0.0 collective-permute-done.5.got_a
  25.1 0.4 collective-permute-done.6.got_b
  25.5 1.3 %shard_map.133 = (f32[32,8,8,256]{3,2,1,0:T(8,128)S(1)}, f32[136,8,128]{2,1,0:T(8,128)S(1)}, f32[136,8,128]{2,1,0:T(8,128)S(1)}, f32[8,8,128]{2,1,0:T(8,128)S(1)}) custom-call(f32[8,256,128]{2,1,0:T(8,128)S(1)} %get-tuple-element.49.products, f32[256,128]{1,0:T(8,128)S(1)} %get-tuple-element.50.own_a, f32[256,128]{1,0:T(8,128)S(1)} %get-tuple-element.51.own_b, ...), custom_call_target="tpu_custom_call" | custom-call | flops 500000000 | bytes 1048576 | tf_op jit(solution)/shard_map/pallas_call | solution.py:543
  26.8 0.3 collective-permute-start.7
  27.1 1.9 %collective-permute-start.8 = (f32[136,8,128]{2,1,0:T(8,128)S(1)}, f32[136,8,128]{2,1,0:T(8,128)S(1)}, u32[]{:S(2)}, u32[]{:S(2)}) collective-permute-start(f32[136,8,128]{2,1,0:T(8,128)S(1)} %get-tuple-element.56), channel_id=1, source_target_pairs={{1,2},{2,1},{3,4},{4,3},{5,6},{6,5},{9,10},{10,9},{11,12},{12,11},... | collective-permute-start | bytes 1671176 | tf_op jit(solution)/shard_map/ppermute | solution.py:538
  29.0 0.0 copy-start.1
  29.0 0.0 copy-start.2
  29.0 0.0 copy-start.6
  29.1 1.4 %shard_map.130 = (f32[8,32,8,128]{3,2,1,0:T(8,128)S(1)}, f32[8,16,8,128]{3,2,1,0:T(8,128)S(1)}) custom-call(f32[32,8,8,256]{3,2,1,0:T(8,128)S(1)} %get-tuple-element.42.filtered), custom_call_target="tpu_custom_call" | custom-call | flops 500000000 | bytes 1048576 | tf_op jit(solution)/shard_map/pallas_call | solution.py:543
  30.5 1.4 %shard_map.134 = (f32[8,32,8,128]{3,2,1,0:T(8,128)S(1)}, f32[8,16,8,128]{3,2,1,0:T(8,128)S(1)}) custom-call(f32[32,8,8,256]{3,2,1,0:T(8,128)S(1)} %get-tuple-element.52.filtered), custom_call_target="tpu_custom_call" | custom-call | flops 500000000 | bytes 1048576 | tf_op jit(solution)/shard_map/pallas_call | solution.py:543
  31.9 0.0 collective-permute-done.3.got_a
  31.9 1.0 %collective-permute-done.4.got_b = f32[136,8,128]{2,1,0:T(8,128)S(1)} collective-permute-done((f32[136,8,128]{2,1,0:T(8,128)S(1)}, f32[136,8,128]{2,1,0:T(8,128)S(1)}, u32[]{:S(2)}, u32[]{:S(2)}) %collective-permute-start.4) | collective-permute-done | bytes 557088 | tf_op jit(solution)/shard_map/ppermute | solution.py:538
  32.8 0.0 copy-done.1
  32.8 0.0 copy-done.2
  32.8 0.0 copy-done.6
  32.8 1.8 %shard_map.131 = (f32[8,32,128]{2,1,0:T(8,128)S(1)}, f32[8,128]{1,0:T(8,128)S(1)}, f32[8,256]{1,0:T(8,128)S(1)}) custom-call(f32[8,32,8,128]{3,2,1,0:T(8,128)S(1)} %get-tuple-element.43.fine, f32[8,16,8,128]{3,2,1,0:T(8,128)S(1)} %get-tuple-element.44.coarse, f32[136,8,128]{2,1,0:T(8,128)S(1)} %collective-permute-done.3.got_a, ...), custom_call_target="tpu_custom_call" | custom-call | flops 500000000 | bytes 1048576 | tf_op jit(solution)/shard_map/pallas_call | solution.py:543
  34.6 0.0 collective-permute-done.7.got_a
  34.7 3.9 %collective-permute-done.8.got_b = f32[136,8,128]{2,1,0:T(8,128)S(1)} collective-permute-done((f32[136,8,128]{2,1,0:T(8,128)S(1)}, f32[136,8,128]{2,1,0:T(8,128)S(1)}, u32[]{:S(2)}, u32[]{:S(2)}) %collective-permute-start.8) | collective-permute-done | bytes 557088 | tf_op jit(solution)/shard_map/ppermute | solution.py:538
  38.6 0.0 copy-start.8
  38.6 1.8 %shard_map.135 = (f32[8,32,128]{2,1,0:T(8,128)S(1)}, f32[8,128]{1,0:T(8,128)S(1)}, f32[16,256]{1,0:T(8,128)S(1)}) custom-call(f32[8,32,8,128]{3,2,1,0:T(8,128)S(1)} %get-tuple-element.53.fine, f32[8,16,8,128]{3,2,1,0:T(8,128)S(1)} %get-tuple-element.54.coarse, f32[136,8,128]{2,1,0:T(8,128)S(1)} %collective-permute-done.7.got_a, ...), custom_call_target="tpu_custom_call" | custom-call | flops 500000000 | bytes 1048576 | tf_op jit(solution)/shard_map/pallas_call | solution.py:543
  40.4 2.3 %collective-permute-start.9 = (f32[16,256]{1,0:T(8,128)S(1)}, f32[16,256]{1,0:T(8,128)S(1)}, u32[]{:S(2)}, u32[]{:S(2)}) collective-permute-start(f32[16,256]{1,0:T(8,128)S(1)} %get-tuple-element.62), channel_id=1, source_target_pairs={{1,0},{2,1},{3,2},{4,3},{5,4},{6,5},{7,6},{9,8},{10,9},{11,10},{12... | collective-permute-start | bytes 49160 | tf_op jit(solution)/shard_map/ppermute | solution.py:633
  42.7 2.7 %collective-permute-done.9.refs_4_ = f32[16,256]{1,0:T(8,128)S(1)} collective-permute-done((f32[16,256]{1,0:T(8,128)S(1)}, f32[16,256]{1,0:T(8,128)S(1)}, u32[]{:S(2)}, u32[]{:S(2)}) %collective-permute-start.9) | collective-permute-done | bytes 16416 | tf_op jit(solution)/shard_map/ppermute | solution.py:633
  45.5 0.0 copy-done.8
  45.5 1.9 %shard_map.136 = f32[16,64,256]{2,1,0:T(8,128)} custom-call(f32[8,32,128]{2,1,0:T(8,128)S(1)} %get-tuple-element.48.refs_0_, f32[8,32,128]{2,1,0:T(8,128)S(1)} %get-tuple-element.59.refs_1_, f32[8,128]{1,0:T(8,128)S(1)} %get-tuple-element.60.refs_2_, f32[8,128]{1,0:T(8,128)S(1)} %get-tuple-element.61.refs_3_, f32[16,256]{1,0:T(8,128)S(1)} %collective-permute-done.9.refs_4_, ...), custom_call_target="tpu_custom_call" | custom-call | flops 500000000 | bytes 1048576 | tf_op jit(solution)/shard_map/pallas_call | solution.py:543
  (1 shorter events, 0.0 us)
Async XLA Ops:
  0.0 9.5 %copy-start.3 = (bf16[256,256]{1,0:T(8,128)(2,1)S(1)}, bf16[256,256]{1,0:T(8,128)(2,1)}, u32[]{:S(2)}) copy-start(bf16[256,256]{1,0:T(8,128)(2,1)} %constant.22.clone.restrict) | copy-start | bytes 393220
  0.0 9.5 %copy-start = (bf16[1024,256]{1,0:T(8,128)(2,1)S(1)}, bf16[1024,256]{1,0:T(8,128)(2,1)}, u32[]{:S(2)}) copy-start(bf16[1024,256]{1,0:T(8,128)(2,1)} %constant.33.packing) | copy-start | bytes 1572868
  1.0 8.5 %collective-permute-start = (f32[16,256]{1,0:T(8,128)S(1)}, f32[16,256]{1,0:T(8,128)S(1)}, u32[]{:S(2)}, u32[]{:S(2)}) collective-permute-start(f32[16,256]{1,0:T(8,128)S(1)} %bitcast.3), channel_id=1, source_target_pairs={{0,1},{1,2},{2,3},{3,4},{4,5},{5,6},{6,7},{8,9},{9,10},{10,11},{11... | collective-permute-start | bytes 49160 | tf_op jit(solution)/shard_map/ppermute | solution.py:569
  10.9 9.0 %collective-permute-start.1 = (f32[256,128]{1,0:T(8,128)S(1)}, f32[256,128]{1,0:T(8,128)S(1)}, u32[]{:S(2)}, u32[]{:S(2)}) collective-permute-start(f32[256,128]{1,0:T(8,128)S(1)} %get-tuple-element.38.own_a), channel_id=1, source_target_pairs={{0,8},{8,0},{16,24},{24,16},{1,9},{9,1},{17,25},{25,17},{2,10},{10... | collective-permute-start | bytes 393224 | tf_op jit(solution)/shard_map/ppermute | solution.py:538
  12.1 8.1 %copy-start.4 = (bf16[256,128]{1,0:T(8,128)(2,1)S(1)}, bf16[256,128]{1,0:T(8,128)(2,1)}, u32[]{:S(2)}) copy-start(bf16[256,128]{1,0:T(8,128)(2,1)} %constant.26.clone.beyond_high) | copy-start | bytes 196612
  12.1 8.1 %copy-start.5 = (bf16[256,128]{1,0:T(8,128)(2,1)S(1)}, bf16[256,128]{1,0:T(8,128)(2,1)}, u32[]{:S(2)}) copy-start(bf16[256,128]{1,0:T(8,128)(2,1)} %constant.27.clone.beyond_low) | copy-start | bytes 196612
  12.1 8.1 %copy-start.7 = (bf16[128,128]{1,0:T(8,128)(2,1)S(1)}, bf16[128,128]{1,0:T(8,128)(2,1)}, u32[]{:S(2)}) copy-start(bf16[128,128]{1,0:T(8,128)(2,1)} %constant.30.clone.choice) | copy-start | bytes 98308
  12.2 8.1 %collective-permute-start.2 = (f32[256,128]{1,0:T(8,128)S(1)}, f32[256,128]{1,0:T(8,128)S(1)}, u32[]{:S(2)}, u32[]{:S(2)}) collective-permute-start(f32[256,128]{1,0:T(8,128)S(1)} %get-tuple-element.39.own_b), channel_id=1, source_target_pairs={{8,16},{16,8},{9,17},{17,9},{10,18},{18,10},{11,19},{19,11},{12,20... | collective-permute-start | bytes 393224 | tf_op jit(solution)/shard_map/ppermute | solution.py:538
  15.7 9.3 %collective-permute-start.5 = (f32[256,128]{1,0:T(8,128)S(1)}, f32[256,128]{1,0:T(8,128)S(1)}, u32[]{:S(2)}, u32[]{:S(2)}) collective-permute-start(f32[256,128]{1,0:T(8,128)S(1)} %get-tuple-element.50.own_a), channel_id=1, source_target_pairs={{0,8},{8,0},{16,24},{24,16},{1,9},{9,1},{17,25},{25,17},{2,10},{10... | collective-permute-start | bytes 393224 | tf_op jit(solution)/shard_map/ppermute | solution.py:538
  15.8 9.7 %collective-permute-start.6 = (f32[256,128]{1,0:T(8,128)S(1)}, f32[256,128]{1,0:T(8,128)S(1)}, u32[]{:S(2)}, u32[]{:S(2)}) collective-permute-start(f32[256,128]{1,0:T(8,128)S(1)} %get-tuple-element.51.own_b), channel_id=1, source_target_pairs={{8,16},{16,8},{9,17},{17,9},{10,18},{18,10},{11,19},{19,11},{12,20... | collective-permute-start | bytes 393224 | tf_op jit(solution)/shard_map/ppermute | solution.py:538
  21.6 10.3 %collective-permute-start.3 = (f32[136,8,128]{2,1,0:T(8,128)S(1)}, f32[136,8,128]{2,1,0:T(8,128)S(1)}, u32[]{:S(2)}, u32[]{:S(2)}) collective-permute-start(f32[136,8,128]{2,1,0:T(8,128)S(1)} %get-tuple-element.45.own_rows), channel_id=1, source_target_pairs={{0,1},{1,0},{2,3},{3,2},{4,5},{5,4},{6,7},{7,6},{8,9},{9,8},{10,11... | collective-permute-start | bytes 1671176 | tf_op jit(solution)/shard_map/ppermute | solution.py:538
  21.7 11.1 %collective-permute-start.4 = (f32[136,8,128]{2,1,0:T(8,128)S(1)}, f32[136,8,128]{2,1,0:T(8,128)S(1)}, u32[]{:S(2)}, u32[]{:S(2)}) collective-permute-start(f32[136,8,128]{2,1,0:T(8,128)S(1)} %get-tuple-element.46), channel_id=1, source_target_pairs={{1,2},{2,1},{3,4},{4,3},{5,6},{6,5},{9,10},{10,9},{11,12},{12,11},... | collective-permute-start | bytes 1671176 | tf_op jit(solution)/shard_map/ppermute | solution.py:538
  26.8 7.9 %collective-permute-start.7 = (f32[136,8,128]{2,1,0:T(8,128)S(1)}, f32[136,8,128]{2,1,0:T(8,128)S(1)}, u32[]{:S(2)}, u32[]{:S(2)}) collective-permute-start(f32[136,8,128]{2,1,0:T(8,128)S(1)} %get-tuple-element.55.own_rows), channel_id=1, source_target_pairs={{0,1},{1,0},{2,3},{3,2},{4,5},{5,4},{6,7},{7,6},{8,9},{9,8},{10,11... | collective-permute-start | bytes 1671176 | tf_op jit(solution)/shard_map/ppermute | solution.py:538
  27.1 11.5 %collective-permute-start.8 = (f32[136,8,128]{2,1,0:T(8,128)S(1)}, f32[136,8,128]{2,1,0:T(8,128)S(1)}, u32[]{:S(2)}, u32[]{:S(2)}) collective-permute-start(f32[136,8,128]{2,1,0:T(8,128)S(1)} %get-tuple-element.56), channel_id=1, source_target_pairs={{1,2},{2,1},{3,4},{4,3},{5,6},{6,5},{9,10},{10,9},{11,12},{12,11},... | collective-permute-start | bytes 1671176 | tf_op jit(solution)/shard_map/ppermute | solution.py:538
  29.0 3.8 %copy-start.1 = (bf16[3,3,128,128]{3,2,1,0:T(8,128)(2,1)S(1)}, bf16[3,3,128,128]{3,2,1,0:T(8,128)(2,1)}, u32[]{:S(2)}) copy-start(bf16[3,3,128,128]{3,2,1,0:T(8,128)(2,1)} %constant.28.clone.row_highs) | copy-start | bytes 884740
  29.0 3.8 %copy-start.2 = (bf16[3,3,128,128]{3,2,1,0:T(8,128)(2,1)S(1)}, bf16[3,3,128,128]{3,2,1,0:T(8,128)(2,1)}, u32[]{:S(2)}) copy-start(bf16[3,3,128,128]{3,2,1,0:T(8,128)(2,1)} %constant.29.clone.row_lows) | copy-start | bytes 884740
  29.0 3.8 %copy-start.6 = (bf16[128,128]{1,0:T(8,128)(2,1)S(1)}, bf16[128,128]{1,0:T(8,128)(2,1)}, u32[]{:S(2)}) copy-start(bf16[128,128]{1,0:T(8,128)(2,1)} %constant.24.clone.refining) | copy-start | bytes 98308
  38.6 6.9 %copy-start.8 = (bf16[256,256]{1,0:T(8,128)(2,1)S(1)}, bf16[256,256]{1,0:T(8,128)(2,1)}, u32[]{:S(2)}) copy-start(bf16[256,256]{1,0:T(8,128)(2,1)} %constant.25.clone.refs_5_) | copy-start | bytes 393220
  40.4 5.1 %collective-permute-start.9 = (f32[16,256]{1,0:T(8,128)S(1)}, f32[16,256]{1,0:T(8,128)S(1)}, u32[]{:S(2)}, u32[]{:S(2)}) collective-permute-start(f32[16,256]{1,0:T(8,128)S(1)} %get-tuple-element.62), channel_id=1, source_target_pairs={{1,0},{2,1},{3,2},{4,3},{5,4},{6,5},{7,6},{9,8},{10,9},{11,10},{12... | collective-permute-start | bytes 49160 | tf_op jit(solution)/shard_map/ppermute | solution.py:633

commit v4 on v3

--- a/solution.py
+++ b/solution.py
@@ -18,6 +18,7 @@
 EDGE = 15
 COLUMN = 32
 CHUNKS = 2
+PER_LEVEL = 14
 VMEM_LIMIT = 20 * 2**20
 BF16, F32 = jnp.bfloat16, jnp.float32
 double_taps = [
@@ -89,13 +90,13 @@
     return table
 
 
-def halo_table(columns, width):
+def halo_table(columns, width, first):
     table = np.zeros((2, 2 * SLOT, 2 * LANES))
     outer = columns[width:]
     for side, lane, compact, factor, line in message_lanes():
         if line < 2 and lane < 2 * SLOT:
             table[lane // SLOT, side * SLOT + lane % SLOT] = outer[compact]
-    table[:, EDGE] = columns[0]
+    table[:, EDGE] = 0.0 if first else columns[0]
     table[:, SLOT + EDGE] = outer[16]
     return table
 
@@ -232,16 +233,16 @@
             for side in range(2):
                 start = LANES + side * 64 + variant * SLOT
                 target[variant, start:start + SLOT, :] = halo_case[part_of, variant % 2, side * SLOT:(side + 1) * SLOT, :]
-    rows = raw.reshape(8 * levels * height, LANES)
     lane = lax.broadcasted_iota(jnp.int32, (GROUP, LANES), 1)
 
     def level_step(level, _):
         for block in range(blocks):
             edge = jnp.zeros((GROUP, LANES), F32)
+            span = slice(block * GROUP, (block + 1) * GROUP)
+            block_rows = jnp.swapaxes(raw[:, level, span, :], 0, 1)
+            turned[level, span] = block_rows
             for line in range(GROUP):
-                y = block * GROUP + line
-                member = rows[pl.ds(level * height + y, 8, levels * height), :]
-                turned[level, y] = member
+                member = block_rows[line]
                 spot = line * SLOT + EDGE
                 edge = jnp.where(lane == spot, pltpu.roll(member, spot, 1), edge)
             edges[tile(level * blocks + block), :] = edge
@@ -255,7 +256,7 @@
 def pack_kernel(chunk, levels, height, across, turned, edges, south, restrict, packing, products, message_a, message_b, coarse, below):
     blocks = height // GROUP
     first = chunk * levels
-    value = exact_dot(south[...], restrict[...])
+    value = exact_dot(south[...], restrict[...]) * jnp.where(lax.axis_index("gy") == 0, 0.0, 1.0).astype(F32)
     for half in range(2):
         below[half] = value[:, half * LANES:(half + 1) * LANES]
     lane = lax.broadcasted_iota(jnp.int32, (GROUP, LANES), 1)
@@ -286,9 +287,8 @@
         total = total + exact_dot(value, packing[line * LANES:(line + 2) * LANES, :])
     to_east = total[:, :LANES] + message_a[...]
     to_west = total[:, LANES:] + edges[first * blocks * 8:(first + levels) * blocks * 8, :]
-    even = lax.axis_index("gx") % 2 == 0
-    message_a[...] = jnp.where(even, to_east, to_west)
-    message_b[...] = jnp.where(even, to_west, to_east)
+    message_a[...] = to_east
+    message_b[...] = to_west
 
 
 def columns_kernel(levels, height, products, own_a, own_b, got_a, got_b, high_weights, low_weights, beyond_high, beyond_low, choice,
@@ -296,9 +296,7 @@
     blocks = height // GROUP
     groups = levels * blocks
     lane = lax.broadcasted_iota(jnp.int32, (groups * 8, LANES), 1)
-    even = lax.axis_index("gx") % 2 == 0
-    own_east, own_west = jnp.where(even, own_a[...], own_b[...]), jnp.where(even, own_b[...], own_a[...])
-    west, east = jnp.where(even, got_b[...], got_a[...]), jnp.where(even, got_a[...], got_b[...])
+    own_east, own_west, west, east = own_a[...], own_b[...], got_a[...], got_b[...]
     spot = lane % SLOT == EDGE
     chosen = exact_dot(east, choice[...]).reshape(levels, blocks, 8, LANES)
     total = chosen[:, 0]
@@ -314,7 +312,7 @@
     for block in range(1, blocks):
         total = total + pltpu.roll(beyond[:, block], block * COLUMN, 2)
     for message in (message_a, message_b):
-        message[levels * 16:] = total
+        message[levels * PER_LEVEL:] = total
     halves = [
         split(jnp.where(lane < 64, west, pltpu.roll(east, 64, 1))),
         split(jnp.where(lane < 64, pltpu.roll(west, 64, 1), east)),
@@ -339,11 +337,15 @@
             for half in range(2):
                 fourth.append(sum(at(block, half * 4 + k) for k in range(1, 4)) + at(block, half * 4))
         for message, start, coarse in ((message_a, start_a, coarse_a), (message_b, start_b, coarse_b)):
+            rows = []
             for line in range(GROUP):
-                message[level * 16 + line] = filtered[level * blocks + start, line, :, :LANES]
+                message[level * PER_LEVEL + line] = filtered[level * blocks + start, line, :, :LANES]
                 block, pair = coarse + line // 4, line % 4
                 pairs = at(block, 2 * pair) + at(block, 2 * pair + 1)
-                message[level * 16 + 8 + line] = jnp.where(second, pairs, fourth[line])
+                rows.append(jnp.where(second, pairs, fourth[line]))
+            for i in range(6):
+                spare = pltpu.roll(rows[6 + i // 3], 96 - 32 * (i % 3), 1)
+                message[level * PER_LEVEL + 8 + i] = jnp.where(small < 96, rows[i], spare)
         return 0
 
     lax.fori_loop(0, levels, level_step, 0)
@@ -410,48 +412,98 @@
     lax.fori_loop(0, levels, level_step, 0)
 
 
-def combine_kernel(chunk, levels, height, fine, coarse, got_a, got_b, own_rows, factors, turned, refining, row_highs, row_lows, *refs):
-    earlier, (combined, beyond, first_row, stacked, refined, weighted) = refs[:-6], refs[-6:]
+def outside(load):
+    values = [load(j) for j in range(8)]
+    result = []
+    for i in range(8):
+        total = double_taps[i + 1] * values[0]
+        for j in range(1, 8 - i):
+            total = total + double_taps[i + 1 + j] * values[j]
+        result.append(total)
+    return result
+
+
+def coarse_rows(packed, lane):
+    rows = list(packed)
+    for i in range(2):
+        pieces = [pltpu.roll(packed[3 * i + k], 32 + 32 * k, 1) for k in range(3)]
+        rows.append(jnp.where(lane < 32, pieces[0], jnp.where(lane < 64, pieces[1], pieces[2])))
+    return rows
+
+
+def coarse_scale(lane):
+    return jnp.where(lane < 64, jnp.float32(generations[1][1]), jnp.float32(generations[2][1]))
+
+
+def first_row_kernel(chunk, levels, height, fine, coarse, got_a, got_b, own_rows, factors, turned, refining, row_highs, row_lows, *refs):
+    earlier, (beyond, first_row, packed) = refs[:1] if chunk else (), refs[-3:]
+    first = chunk * levels
+    up_a = lax.axis_index("gy") % 2 == 0
+    gy, ny = lax.axis_index("gy"), lax.axis_size("gy")
+
+    def side(value):
+        return value.reshape(levels * 8, LANES)
+
+    case = jnp.where(gy == 0, 0, jnp.where(gy == ny - 1, 2, 1))
+    extra = slice(levels * PER_LEVEL, levels * (PER_LEVEL + 1))
+    far_a, far_b = side(got_a[extra]), side(got_b[extra])
+    value = three_dots(side(own_rows[extra]), row_highs[case, 0], row_lows[case, 0])
+    value = value + three_dots(jnp.where(up_a, far_b, far_a), row_highs[case, 1], row_lows[case, 1])
+    value = value + three_dots(jnp.where(up_a, far_a, far_b), row_highs[case, 2], row_lows[case, 2])
+    beyond[...] = jnp.sum(value.reshape(levels, 8, LANES) * factors[...], axis=1) * (1.0 / 7.0)
+
+    lane = lax.broadcasted_iota(jnp.int32, (8, LANES), 1)
+    second = lane < 64
+    weight = jnp.float32(generations[0][1])
+    keep = jnp.where((gy == 0) | (gy == ny - 1), 0.0, 1.0).astype(F32)
+    for level in range(levels):
+        base = level * PER_LEVEL
+        value = coarse[level, 0]
+        below = [jnp.where(up_a, keep * got_b[base + 8 + r], got_a[base + 8 + r]) for r in range(6)]
+        below = coarse_rows(below, lane)
+        for j in range(8):
+            value = value + double_taps[j + 1] * below[7 - j]
+        above = jnp.where(up_a, got_a[base + 8], keep * got_b[base + 8])
+        value = value + jnp.where(second, 0.0, double_taps[8] * above)
+        packed[level * 8:level * 8 + 8, :] = value * coarse_scale(lane)
+    refined = exact_dot(packed[...], refining[...])
+    for rows in earlier:
+        first_row[:first, :] = rows[...]
+    for level in range(levels):
+        base = level * PER_LEVEL
+        value = fine[level, 0]
+        for j in range(8):
+            value = value + double_taps[j + 1] * jnp.where(up_a, keep * got_b[base + 7 - j], got_a[base + 7 - j])
+        value = turned[first + level, 0] * (weight * value + refined[level * 8:level * 8 + 8, :])
+        first_row[first + level:first + level + 1, :LANES] = jnp.sum(value, axis=0, keepdims=True) * (1.0 / 7.0)
+    first_row[first:, LANES:] = beyond[...]
+
+
+def combine_kernel(chunk, levels, height, fine, coarse, got_a, got_b, turned, refining, combined, stacked, refined):
     blocks = height // GROUP
     half, quarter = height // 2, height // 4
     first = chunk * levels
     up_a = lax.axis_index("gy") % 2 == 0
+    lane = lax.broadcasted_iota(jnp.int32, (8, LANES), 1)
+    second = lane < 64
+    scale = coarse_scale(lane)
+    weight = jnp.float32(generations[0][1])
     gy, ny = lax.axis_index("gy"), lax.axis_size("gy")
-    second = lax.broadcasted_iota(jnp.int32, (8, LANES), 1) < 64
-    scale = jnp.where(second, jnp.float32(generations[1][1]), jnp.float32(generations[2][1]))
-    weight = jnp.float32(generations[0][1])
-
-    def side(value):
-        return value.reshape(levels * 8, LANES)
-
-    case = jnp.where(gy == 0, 0, jnp.where(gy == ny - 1, 2, 1))
-    far_a, far_b = side(got_a[levels * 16:]), side(got_b[levels * 16:])
-    value = three_dots(side(own_rows[levels * 16:]), row_highs[case, 0], row_lows[case, 0])
-    value = value + three_dots(jnp.where(up_a, far_b, far_a), row_highs[case, 1], row_lows[case, 1])
-    value = value + three_dots(jnp.where(up_a, far_a, far_b), row_highs[case, 2], row_lows[case, 2])
-    beyond[...] = jnp.sum(value.reshape(levels, 8, LANES) * factors[...], axis=1) * (1.0 / 7.0)
-
-    def outside(load):
-        values = [load(j) for j in range(8)]
-        result = []
-        for i in range(8):
-            total = double_taps[i + 1] * values[0]
-            for j in range(1, 8 - i):
-                total = total + double_taps[i + 1 + j] * values[j]
-            result.append(total)
-        return result
+    keep = jnp.where((gy == 0) | (gy == ny - 1), 0.0, 1.0).astype(F32)
 
     def level_step(level, _):
         def north(r):
-            return jnp.where(up_a, got_a[level * 16 + r], got_b[level * 16 + r])
+            return jnp.where(up_a, got_a[level * PER_LEVEL + r], keep * got_b[level * PER_LEVEL + r])
 
         def south(r):
-            return jnp.where(up_a, got_b[level * 16 + r], got_a[level * 16 + r])
-
+            return jnp.where(up_a, keep * got_b[level * PER_LEVEL + r], got_a[level * PER_LEVEL + r])
+
+        below = coarse_rows([south(8 + r) for r in range(6)], lane)
+        above = coarse_rows([north(8 + r) for r in range(6)], lane)
         fine_south = outside(lambda j: south(7 - j))
-        coarse_south = outside(lambda j: south(15 - j))
+        coarse_south = outside(lambda j: below[7 - j])
         fine_north = outside(north)
-        coarse_north = outside(lambda j: north(8 + j))
+        coarse_north = outside(lambda j: above[j])
         parts = []
         for r in range(half):
             value = coarse[level, r]
@@ -467,6 +519,7 @@
             stacked[r * 8:r * 8 + 8, :] = jnp.where(second, parts[r], parts[r // 2])
         refined[...] = exact_dot(stacked[...], refining[...])
         for block in range(blocks):
+            weighted = []
             for line in range(GROUP):
                 y = block * GROUP + line
                 value = fine[level, y]
@@ -475,76 +528,103 @@
                 if y >= height - 8:
                     value = value + fine_north[height - 1 - y]
                 value = weight * value + refined[y // 2 * 8:y // 2 * 8 + 8, :]
-                weighted[line * 8:line * 8 + 8, :] = turned[first + level, y] * value
-            total = weighted[pl.ds(0, 8, 8), :]
-            for m in range(1, 8):
-                total = total + weighted[pl.ds(m, 8, 8), :]
+                weighted.append(turned[first + level, y] * value)
+            total = jnp.sum(jnp.swapaxes(jnp.stack(weighted), 0, 1), axis=0)
             combined[level, block * GROUP:(block + 1) * GROUP, :] = total * (1.0 / 7.0)
         return 0
 
     lax.fori_loop(0, levels, level_step, 0)
-    for rows in earlier:
-        first_row[:first, :] = rows[...]
-    for level in range(levels):
-        first_row[first + level:first + level + 1, :LANES] = combined[level, 0:1, :]
-    first_row[first:, LANES:] = beyond[...]
-
-
-def interpolate_kernel(height, *refs):
-    chunks = (len(refs) - 7) // 2
-    north, interpolation, out, extended, rows, ready, sems = refs[-7:]
-    levels = refs[0].shape[0]
-    part = levels // 2
+
+
+def interpolate_levels(combined, beyond, north, first, start, part, interpolation, extended, rows):
+    height = combined.shape[1]
     lane = lax.broadcasted_iota(jnp.int32, (height, LANES), 1)
     line = lax.broadcasted_iota(jnp.int32, (height, LANES), 0)
-    row_lane = lax.broadcasted_iota(jnp.int32, (1, LANES), 1)
+    for i in range(part):
+        level = start + i
+        here = combined[level]
+        last = jnp.broadcast_to(beyond[level:level + 1, :], (height, LANES))
+        last = jnp.sum(jnp.where(lane == line, last, 0.0), axis=1, keepdims=True)
+        extended[0, i, 0:height, :] = here
+        extended[1, i, 0:height, :] = jnp.where(lane == LANES - 1, last, pltpu.roll(here, LANES - 1, 1))
+        for half in range(2):
+            if north is None:
+                extended[half, i, height:height + 1, :] = jnp.zeros((1, LANES), F32)
+            else:
+                extended[half, i, height:height + 1, :] = north[half][first + level:first + level + 1, :]
+            value = extended[half, i, 0:height, :]
+            rows[half, i, pl.ds(0, height, 2), :] = value
+            rows[half, i, pl.ds(1, height, 2), :] = 0.5 * (value + extended[half, i, 1:height + 1, :])
+    value = exact_dot(
+        jnp.concatenate([rows[half].reshape(part * 2 * height, LANES) for half in range(2)], axis=1), interpolation[...]
+    )
+    return value.reshape(part, 2 * height, interpolation.shape[1])
+
+
+def early_kernel(combined, beyond, interpolation, out, tails, extended, rows, ready, sems):
+    levels = combined.shape[0]
+    part = levels // 2
+    done = ready.shape[1] - 8
     copies = []
-    for start in range(0, chunks * levels, part):
-        combined, beyond = refs[start // levels], refs[chunks + start // levels]
-        for i in range(part):
-            level = start + i
-            here = combined[level % levels]
-            last = jnp.broadcast_to(beyond[level % levels:level % levels + 1, :], (height, LANES))
-            last = jnp.sum(jnp.where(lane == line, last, 0.0), axis=1, keepdims=True)
-            after = north[level:level + 1, :LANES]
-            corner = jnp.broadcast_to(north[level:level + 1, LANES:LANES + 1], (1, LANES))
-            extended[0, i, 0:height, :] = here
-            extended[0, i, height:height + 1, :] = after
-            extended[1, i, 0:height, :] = jnp.where(lane == LANES - 1, last, pltpu.roll(here, LANES - 1, 1))
-            extended[1, i, height:height + 1, :] = jnp.where(row_lane == LANES - 1, corner, pltpu.roll(after, LANES - 1, 1))
-            for half in range(2):
-                value = extended[half, i, 0:height, :]
-                rows[half, i, pl.ds(0, height, 2), :] = value
-                rows[half, i, pl.ds(1, height, 2), :] = 0.5 * (value + extended[half, i, 1:height + 1, :])
-        value = exact_dot(
-            jnp.concatenate([rows[half].reshape(part * 2 * height, LANES) for half in range(2)], axis=1), interpolation[...]
-        )
+    for start in range(0, levels, part):
         span = pl.ds(start, part)
-        ready[span] = value.reshape(part, 2 * height, ready.shape[2])
-        copies.append(pltpu.make_async_copy(ready.at[span], out.at[span], sems.at[start // part]))
+        ready[span] = interpolate_levels(combined, beyond, None, 0, start, part, interpolation, extended, rows)
+        copies.append(pltpu.make_async_copy(ready.at[span, pl.ds(0, done)], out.at[span, pl.ds(0, done)], sems.at[start // part]))
+        copies[-1].start()
+    tails[...] = ready[:, done:, :]
+    for copy in copies:
+        copy.wait()
+
+
+def late_kernel(first, before, combined, beyond, north, interpolation, tails, out, extended, rows, ready, ends, kept, shifted, sems):
+    levels = combined.shape[0]
+    part = levels // 2
+    lane = lax.broadcasted_iota(jnp.int32, shifted.shape, 1)
+    inside = jnp.where(lax.axis_index("gy") == lax.axis_size("gy") - 1, 0.0, 1.0).astype(F32)
+    corner = jnp.broadcast_to(north[:, LANES:LANES + 1], shifted.shape) * inside
+    after = north[:, :LANES] * inside
+    kept[...] = after
+    shifted[...] = jnp.where(lane == LANES - 1, corner, pltpu.roll(after, LANES - 1, 1))
+    copies = []
+    row = 0.5 * exact_dot(jnp.concatenate([after, shifted[...]], axis=1), interpolation[...])
+    ends[...] = tails[...]
+    for level in range(first):
+        ends[level, 7:8, :] = ends[level, 7:8, :] + row[level:level + 1, :]
+    done = ready.shape[1] - 8
+    copies.append(pltpu.make_async_copy(ends, out.at[pl.ds(0, first), pl.ds(done, 8)], sems.at[2]))
+    copies[-1].start()
+    for start in range(0, levels, part):
+        span = pl.ds(start, part)
+        rows_north = (kept, shifted)
+        ready[span] = interpolate_levels(combined, beyond, rows_north, first, start, part, interpolation, extended, rows)
+        copies.append(pltpu.make_async_copy(ready.at[span], out.at[pl.ds(first + start, part)], sems.at[start // part]))
         copies[-1].start()
     for copy in copies:
         copy.wait()
 
 
-def partner(index, size, second):
-    other = ((index + 1) ^ 1) - 1 if second else index ^ 1
-    return other if 0 <= other < size else None
-
-
-def swap(value, axis, second):
+def around(value, axis, step):
     size = lax.axis_size(axis)
-    pairs = [(i, partner(i, size, second)) for i in range(size)]
-    return lax.ppermute(value, axis, [(i, j) for i, j in pairs if j is not None])
-
-
-def call(kernel, outs, scratch, cost, *args, in_hbm=0, out_hbm=False):
+    return lax.ppermute(value, axis, [(i, (i + step) % size) for i in range(size)])
+
+
+def swap(value, second):
+    nx, ny = lax.axis_size("gx"), lax.axis_size("gy")
+    pairs = []
+    for x in range(nx):
+        for y in range(ny):
+            other = ((y + 1) ^ 1) - 1 if second else y ^ 1
+            pairs.append((x * ny + y, x * ny + other if 0 <= other < ny else (x ^ 1) * ny + y))
+    return lax.ppermute(value, ("gx", "gy"), pairs)
+
+
+def call(kernel, outs, scratch, cost, *args, in_hbm=0):
     vmem = pl.BlockSpec(memory_space=pltpu.VMEM)
     return pl.pallas_call(
         kernel,
         out_shape=tuple(jax.ShapeDtypeStruct(*out) if isinstance(out[0], tuple) else jax.ShapeDtypeStruct(out, F32) for out in outs),
         in_specs=[pl.BlockSpec(memory_space=pltpu.HBM) if i < in_hbm else vmem for i in range(len(args))],
-        out_specs=tuple(pl.BlockSpec(memory_space=pltpu.HBM) if out_hbm else vmem for _ in outs),
+        out_specs=tuple(vmem for _ in outs),
         scratch_shapes=[pltpu.VMEM(shape, F32) if isinstance(shape, tuple) else shape for shape in scratch],
         compiler_params=pltpu.CompilerParams(vmem_limit_bytes=VMEM_LIMIT),
         cost_estimate=pl.CostEstimate(flops=cost, bytes_accessed=2**20, transcendentals=0),
@@ -559,18 +639,16 @@
 def shards(gradient, members):
     all_levels, fine_height, fine_width = gradient.shape
     count, _, height, width = members.shape
-    assert count == 8 and width == LANES and height == 32 and lax.axis_size("gx") > 1
+    assert count == 8 and width == LANES and height == 32 and lax.axis_size("gx") % 2 == 0 and lax.axis_size("gy") % 2 == 0
     assert all_levels % CHUNKS == 0
     levels = all_levels // CHUNKS
     groups = levels * height // GROUP
-    ny = lax.axis_size("gy")
-
-    up = [(i, i + 1) for i in range(ny - 1)]
-    south = lax.ppermute(gradient[:, -1, :], "gy", up)
+
+    south = around(gradient[:, -1, :], "gy", 1)
 
     columns = [column_table(width, i == 0, i == 2) for i in range(3)]
     own_tables = np.stack(halves_of(np.stack([table[:width] for table in columns])), axis=1)
-    halo_tables = np.stack(halves_of(np.stack([halo_table(table, width) for table in columns])), axis=1)
+    halo_tables = np.stack(halves_of(np.stack([halo_table(table, width, i == 0) for i, table in enumerate(columns)])), axis=1)
     restrict = jnp.asarray(restriction_table(width), BF16)
     packing = jnp.asarray(packing_table(width), BF16).reshape(GROUP * width, 2 * LANES)
     refining = jnp.asarray(refining_table(width), BF16)
@@ -579,7 +657,7 @@
     row_highs, row_lows = map(jnp.asarray, halves_of(np.stack([column_rows_table(height, i == 0, i == 2) for i in range(3)])))
     choice = jnp.asarray(edge_choice_table(), BF16)
     flops = 10**9 // CHUNKS
-    far_rows = (levels * 17, 8, LANES)
+    far_rows = (levels * (PER_LEVEL + 1), 8, LANES)
 
     constants = (restrict, jnp.asarray(own_tables), jnp.asarray(halo_tables))
     across, turned, edges, high_weights, low_weights = call(
@@ -599,7 +677,7 @@
         )
         for chunk in range(CHUNKS)
     ]
-    got = [(swap(own_a, "gx", False), swap(own_b, "gx", True)) for _, own_a, own_b in packed]
+    got = [(around(to_east, "gx", 1), around(to_west, "gx", -1)) for _, to_east, to_west in packed]
     filtered = [
         call(
             functools.partial(columns_kernel, levels, height),
@@ -609,7 +687,7 @@
         )
         for chunk in range(CHUNKS)
     ]
-    far = [(swap(rows_a, "gy", False), swap(rows_b, "gy", True)) for _, rows_a, rows_b, _ in filtered]
+    far = [(swap(rows_a, False), swap(rows_b, True)) for _, rows_a, rows_b, _ in filtered]
     own = [
         call(
             functools.partial(own_rows_kernel, levels, height),
@@ -619,26 +697,48 @@
         )
         for chunk in range(CHUNKS)
     ]
-    combined, beyond, first_rows = [], [], []
-    for chunk in range(CHUNKS):
-        results = call(
+    part = levels // 2
+    buffers = [(2, part, height + 8, LANES), (2, part, 2 * height, LANES), (levels, fine_height, fine_width)]
+    vmem, hbm = pl.BlockSpec(memory_space=pltpu.VMEM), pl.BlockSpec(memory_space=pltpu.HBM)
+    out_shape = jax.ShapeDtypeStruct(gradient.shape, F32)
+    params = pltpu.CompilerParams(vmem_limit_bytes=VMEM_LIMIT)
+    cost = pl.CostEstimate(flops=flops, bytes_accessed=2**20, transcendentals=0)
+
+    def first_rows_of(chunk, *earlier):
+        return call(
+            functools.partial(first_row_kernel, chunk, levels, height),
+            [(levels, LANES), ((chunk + 1) * levels, 2 * LANES)],
+            [(levels * 8, LANES)],
+            flops, *own[chunk], *far[chunk], filtered[chunk][1], filtered[chunk][3], turned, refining, row_highs, row_lows, *earlier,
+        )
+
+    def combined_of(chunk):
+        return call(
             functools.partial(combine_kernel, chunk, levels, height),
-            [(levels, height, LANES), (levels, LANES), ((chunk + 1) * levels, 2 * LANES)],
-            [(height // 2 * 8, LANES), (height // 2 * 8, LANES), (64, LANES)],
-            flops, *own[chunk], *far[chunk], filtered[chunk][1], filtered[chunk][3], turned, refining, row_highs, row_lows,
-            *first_rows[-1:],
-        )
-        for result, into in zip(results, (combined, beyond, first_rows)):
-            into.append(result)
-    north = lax.ppermute(first_rows[-1], "gy", [(j, i) for i, j in up])
-    part = levels // 2
-    (out,) = call(
-        functools.partial(interpolate_kernel, height),
-        [(all_levels, fine_height, fine_width)],
-        [(2, part, height + 8, LANES), (2, part, 2 * height, LANES), (all_levels, fine_height, fine_width),
-         pltpu.SemaphoreType.DMA((2 * CHUNKS,))],
-        flops, *combined, *beyond, north, interpolation, out_hbm=True,
-    )
+            [(levels, height, LANES)],
+            [(height // 2 * 8, LANES), (height // 2 * 8, LANES)],
+            flops, *own[chunk], *far[chunk], turned, refining,
+        )[0]
+
+    early_beyond, early_rows = first_rows_of(0)
+    out, tails = pl.pallas_call(
+        early_kernel,
+        out_shape=(out_shape, jax.ShapeDtypeStruct((levels, 8, fine_width), F32)),
+        in_specs=[vmem] * 3, out_specs=(hbm, vmem),
+        scratch_shapes=[pltpu.VMEM(shape, F32) for shape in buffers] + [pltpu.SemaphoreType.DMA((2,))],
+        compiler_params=params, cost_estimate=cost,
+    )(combined_of(0), early_beyond, interpolation)
+    beyond, rows = first_rows_of(1, early_rows, tails)
+    north = around(rows, "gy", -1)
+    out = pl.pallas_call(
+        functools.partial(late_kernel, levels),
+        out_shape=out_shape,
+        in_specs=[hbm] + [vmem] * 5, out_specs=hbm,
+        scratch_shapes=[pltpu.VMEM(shape, F32) for shape in buffers + [(levels, 8, fine_width), (all_levels, LANES), (all_levels, LANES)]]
+        + [pltpu.SemaphoreType.DMA((3,))],
+        input_output_aliases={0: 0},
+        compiler_params=params, cost_estimate=cost,
+    )(out, combined_of(1), beyond, north, interpolation, tails)
     return out
 
 

time: 47.6 us -> 41.5 us (0.87)
  the two profiles are of different devices: /device:TPU:21 before, /device:TPU:0 now
where the time goes in v4:
time: 41.5 us; the launch traced here: 41.3 us
  Pallas kernels  20.8 us (50%)
  starting transfers between devices  12 us (29%)
  waiting for transfers between devices  6.72 us (16%)
  local copies, waits for them, and re-layouts  1.63 us (4%)
    pallas_call x11, Pallas kernels, call(): pl.pallas_call(kernel, out_shape=tuple((jax.ShapeDtypeStruct(*out) if isi...  18 us
    ppermute x6, starting transfers between devices, around(): lax.ppermute(value, axis, [(i, (i + step) % size) for i in range(size)])  8.73 us
    ppermute x6, waiting for transfers between devices, around(): lax.ppermute(value, axis, [(i, (i + step) % size) for i in range(size)])  6.71 us
    ppermute x4, starting transfers between devices, swap(): return lax.ppermute(value, ('gx', 'gy'), pairs)  3.25 us
    pallas_call x1, Pallas kernels, shards(): pl.pallas_call(functools.partial(late_kernel, levels), out_shape=out_shap...  1.42 us
    pallas_call x1, Pallas kernels, shards(): pl.pallas_call(early_kernel, out_shape=(out_shape, jax.ShapeDtypeStruct((...  1.34 us
    slice x1, local copies, waits for them, and re-layouts, shards(): south = around(gradient[:, -1, :], 'gy', 1)  0.99 us
  transfers between devices with their start and end apart: 10, of which 3 were waited for; matrix products, arithmetic and copies ran while one was open for 0% of the time, Pallas kernels for 43%

profile of v4, /device:TPU:0, one launch (start us, length us, event | category | flops | bytes accessed | tf_op | source)
XLA Modules:
  0.0 41.3 jit_solution(9178283996009416813)
XLA Ops:
  0.0 0.0 copy-start.3
  0.0 0.0 copy-start
  0.0 1.0 %slice.3 = f32[16,1,256]{2,1,0:T(1,128)S(1)} slice(f32[16,64,256]{2,1,0:T(8,128)} %gradient.1), slice={[0:16], [63:64], [0:256]} | slice | bytes 32768 | tf_op jit(solution)/shard_map/slice | solution.py:647
  1.0 0.5 %collective-permute-start = (f32[16,256]{1,0:T(8,128)S(1)}, f32[16,256]{1,0:T(8,128)S(1)}, u32[]{:S(2)}, u32[]{:S(2)}) collective-permute-start(f32[16,256]{1,0:T(8,128)S(1)} %bitcast.3), channel_id=1, source_target_pairs={{0,1},{1,2},{2,3},{3,4},{4,5},{5,6},{6,7},{7,0},{8,9},{9,10},{10,1... | collective-permute-start | bytes 49160 | tf_op jit(solution)/shard_map/ppermute | solution.py:608
  1.5 4.1 %shard_map.127 = (f32[2,16,72,128]{3,2,1,0:T(8,128)S(1)}, f32[16,32,8,128]{3,2,1,0:T(8,128)S(1)}, f32[512,128]{1,0:T(8,128)S(1)}, bf16[4,256,256]{2,1,0:T(8,128)(2,1)S(1)}, bf16[4,256,256]{2,1,0:T(8,128)(2,1)S(1)}) custom-call(f32[16,64,256]{2,1,0:T(8,128)} %gradient.1, f32[8,16,32,128]{3,2,1,0:T(8,128)} %members.1, ...), custom_call_target="tpu_custom_call" | custom-call | flops 500000000 | bytes 1048576 | tf_op jit(solution)/shard_map/pallas_call | solution.py:623
  5.7 1.3 %collective-permute-done.south = f32[16,256]{1,0:T(8,128)S(1)} collective-permute-done((f32[16,256]{1,0:T(8,128)S(1)}, f32[16,256]{1,0:T(8,128)S(1)}, u32[]{:S(2)}, u32[]{:S(2)}) %collective-permute-start) | collective-permute-done | bytes 16416 | tf_op jit(solution)/shard_map/ppermute | solution.py:608
  7.0 0.0 copy-done.3
  7.0 0.0 copy-done
  7.0 1.3 %shard_map.128 = (f32[8,256,128]{2,1,0:T(8,128)S(1)}, f32[256,128]{1,0:T(8,128)S(1)}, f32[256,128]{1,0:T(8,128)S(1)}) custom-call(f32[2,16,72,128]{3,2,1,0:T(8,128)S(1)} %get-tuple-element.34.across, f32[16,32,8,128]{3,2,1,0:T(8,128)S(1)} %get-tuple-element.35.turned, f32[512,128]{1,0:T(8,128)S(1)} %get-tuple-element.36.edges, ...), custom_call_target="tpu_custom_call" | custom-call | flops 500000000 | bytes 1048576 | tf_op jit(solution)/shard_map/pallas_call | solution.py:623
  8.3 2.0 %collective-permute-start.1 = (f32[256,128]{1,0:T(8,128)S(1)}, f32[256,128]{1,0:T(8,128)S(1)}, u32[]{:S(2)}, u32[]{:S(2)}) collective-permute-start(f32[256,128]{1,0:T(8,128)S(1)} %get-tuple-element.38.own_a), channel_id=1, source_target_pairs={{0,8},{8,16},{16,24},{24,0},{1,9},{9,17},{17,25},{25,1},{2,10},{10... | collective-permute-start | bytes 393224 | tf_op jit(solution)/shard_map/ppermute | solution.py:608
  10.4 0.0 copy-start.5
  10.4 0.0 copy-start.6
  10.4 0.0 copy-start.7
  10.4 1.1 %collective-permute-start.2 = (f32[256,128]{1,0:T(8,128)S(1)}, f32[256,128]{1,0:T(8,128)S(1)}, u32[]{:S(2)}, u32[]{:S(2)}) collective-permute-start(f32[256,128]{1,0:T(8,128)S(1)} %get-tuple-element.39.own_b), channel_id=1, source_target_pairs={{0,24},{8,0},{16,8},{24,16},{1,25},{9,1},{17,9},{25,17},{2,26},{10... | collective-permute-start | bytes 393224 | tf_op jit(solution)/shard_map/ppermute | solution.py:608
  11.4 1.3 %shard_map.134 = (f32[8,256,128]{2,1,0:T(8,128)S(1)}, f32[256,128]{1,0:T(8,128)S(1)}, f32[256,128]{1,0:T(8,128)S(1)}) custom-call(f32[2,16,72,128]{3,2,1,0:T(8,128)S(1)} %get-tuple-element.34.across, f32[16,32,8,128]{3,2,1,0:T(8,128)S(1)} %get-tuple-element.35.turned, f32[512,128]{1,0:T(8,128)S(1)} %get-tuple-element.36.edges, ...), custom_call_target="tpu_custom_call" | custom-call | flops 500000000 | bytes 1048576 | tf_op jit(solution)/shard_map/pallas_call | solution.py:623
  12.8 1.0 %collective-permute-start.5 = (f32[256,128]{1,0:T(8,128)S(1)}, f32[256,128]{1,0:T(8,128)S(1)}, u32[]{:S(2)}, u32[]{:S(2)}) collective-permute-start(f32[256,128]{1,0:T(8,128)S(1)} %get-tuple-element.51.own_a), channel_id=1, source_target_pairs={{0,8},{8,16},{16,24},{24,0},{1,9},{9,17},{17,25},{25,1},{2,10},{10... | collective-permute-start | bytes 393224 | tf_op jit(solution)/shard_map/ppermute | solution.py:608
  13.8 1.9 %collective-permute-start.6 = (f32[256,128]{1,0:T(8,128)S(1)}, f32[256,128]{1,0:T(8,128)S(1)}, u32[]{:S(2)}, u32[]{:S(2)}) collective-permute-start(f32[256,128]{1,0:T(8,128)S(1)} %get-tuple-element.52.own_b), channel_id=1, source_target_pairs={{0,24},{8,0},{16,8},{24,16},{1,25},{9,1},{17,9},{25,17},{2,26},{10... | collective-permute-start | bytes 393224 | tf_op jit(solution)/shard_map/ppermute | solution.py:608
  15.7 0.0 collective-permute-done.1.got_a
  15.7 3.3 %collective-permute-done.2.got_b = f32[256,128]{1,0:T(8,128)S(1)} collective-permute-done((f32[256,128]{1,0:T(8,128)S(1)}, f32[256,128]{1,0:T(8,128)S(1)}, u32[]{:S(2)}, u32[]{:S(2)}) %collective-permute-start.2) | collective-permute-done | bytes 131104 | tf_op jit(solution)/shard_map/ppermute | solution.py:608
  19.0 0.0 copy-done.5
  19.0 0.0 copy-done.6
  19.0 0.0 copy-done.7
  19.0 1.8 %shard_map.129 = (f32[32,8,8,256]{3,2,1,0:T(8,128)S(1)}, f32[120,8,128]{2,1,0:T(8,128)S(1)}, f32[120,8,128]{2,1,0:T(8,128)S(1)}, f32[8,8,128]{2,1,0:T(8,128)S(1)}) custom-call(f32[8,256,128]{2,1,0:T(8,128)S(1)} %get-tuple-element.37.products, f32[256,128]{1,0:T(8,128)S(1)} %get-tuple-element.38.own_a, f32[256,128]{1,0:T(8,128)S(1)} %get-tuple-element.39.own_b, ...), custom_call_target="tpu_custom_call" | custom-call | flops 500000000 | bytes 1048576 | tf_op jit(solution)/shard_map/pallas_call | solution.py:623
  20.8 0.1 collective-permute-start.3
  20.9 1.6 %collective-permute-start.4 = (f32[120,8,128]{2,1,0:T(8,128)S(1)}, f32[120,8,128]{2,1,0:T(8,128)S(1)}, u32[]{:S(2)}, u32[]{:S(2)}) collective-permute-start(f32[120,8,128]{2,1,0:T(8,128)S(1)} %get-tuple-element.46), channel_id=1, source_target_pairs={{0,8},{1,2},{2,1},{3,4},{4,3},{5,6},{6,5},{7,15},{8,0},{9,10},{10,... | collective-permute-start | bytes 1474568 | tf_op jit(solution)/shard_map/ppermute | solution.py:618
  22.4 0.0 collective-permute-done.5.got_a
  22.4 2.1 %collective-permute-done.6.got_b = f32[256,128]{1,0:T(8,128)S(1)} collective-permute-done((f32[256,128]{1,0:T(8,128)S(1)}, f32[256,128]{1,0:T(8,128)S(1)}, u32[]{:S(2)}, u32[]{:S(2)}) %collective-permute-start.6) | collective-permute-done | bytes 131104 | tf_op jit(solution)/shard_map/ppermute | solution.py:608
  24.5 1.8 %shard_map.135 = (f32[32,8,8,256]{3,2,1,0:T(8,128)S(1)}, f32[120,8,128]{2,1,0:T(8,128)S(1)}, f32[120,8,128]{2,1,0:T(8,128)S(1)}, f32[8,8,128]{2,1,0:T(8,128)S(1)}) custom-call(f32[8,256,128]{2,1,0:T(8,128)S(1)} %get-tuple-element.50.products, f32[256,128]{1,0:T(8,128)S(1)} %get-tuple-element.51.own_a, f32[256,128]{1,0:T(8,128)S(1)} %get-tuple-element.52.own_b, ...), custom_call_target="tpu_custom_call" | custom-call | flops 500000000 | bytes 1048576 | tf_op jit(solution)/shard_map/pallas_call | solution.py:623
  26.3 0.1 collective-permute-start.7
  26.4 1.5 %collective-permute-start.8 = (f32[120,8,128]{2,1,0:T(8,128)S(1)}, f32[120,8,128]{2,1,0:T(8,128)S(1)}, u32[]{:S(2)}, u32[]{:S(2)}) collective-permute-start(f32[120,8,128]{2,1,0:T(8,128)S(1)} %get-tuple-element.57), channel_id=1, source_target_pairs={{0,8},{1,2},{2,1},{3,4},{4,3},{5,6},{6,5},{7,15},{8,0},{9,10},{10,... | collective-permute-start | bytes 1474568 | tf_op jit(solution)/shard_map/ppermute | solution.py:618
  28.0 0.0 copy-start.4
  28.0 1.4 %shard_map.130 = (f32[8,32,8,128]{3,2,1,0:T(8,128)S(1)}, f32[8,16,8,128]{3,2,1,0:T(8,128)S(1)}) custom-call(f32[32,8,8,256]{3,2,1,0:T(8,128)S(1)} %get-tuple-element.42.filtered), custom_call_target="tpu_custom_call" | custom-call | flops 500000000 | bytes 1048576 | tf_op jit(solution)/shard_map/pallas_call | solution.py:623
  29.4 1.4 %shard_map.136 = (f32[8,32,8,128]{3,2,1,0:T(8,128)S(1)}, f32[8,16,8,128]{3,2,1,0:T(8,128)S(1)}) custom-call(f32[32,8,8,256]{3,2,1,0:T(8,128)S(1)} %get-tuple-element.53.filtered), custom_call_target="tpu_custom_call" | custom-call | flops 500000000 | bytes 1048576 | tf_op jit(solution)/shard_map/pallas_call | solution.py:623
  30.8 0.0 collective-permute-done.3.got_a
  30.8 0.0 collective-permute-done.4.got_b
  30.8 0.0 copy-done.4
  30.8 0.0 copy-start.1
  30.8 0.0 copy-start.2
  30.8 2.2 %shard_map.131.combined = f32[8,32,128]{2,1,0:T(8,128)S(1)} custom-call(f32[8,32,8,128]{3,2,1,0:T(8,128)S(1)} %get-tuple-element.43.fine, f32[8,16,8,128]{3,2,1,0:T(8,128)S(1)} %get-tuple-element.44.coarse, f32[120,8,128]{2,1,0:T(8,128)S(1)} %collective-permute-done.3.got_a, f32[120,8,128]{2,1,0:T(8,128)S(1)} %collective-permute-done.4.got_b, ...), custom_call_target="tpu_custom_call" | custom-call | flops 500000000 | bytes 1048576 | tf_op jit(solution)/shard_map/pallas_call | solution.py:623
  33.0 0.0 copy-done.1
  33.0 0.0 copy-done.2
  33.0 0.0 copy-start.8
  33.0 0.3 shard_map.132
  33.3 0.6 %copy-done.8 = bf16[256,256]{1,0:T(8,128)(2,1)S(1)} copy-done((bf16[256,256]{1,0:T(8,128)(2,1)S(1)}, bf16[256,256]{1,0:T(8,128)(2,1)}, u32[]{:S(2)}) %copy-start.8) | copy-done | bytes 131096
  33.9 1.3 %shard_map.133 = (f32[16,64,256]{2,1,0:T(8,128)}, f32[8,8,256]{2,1,0:T(8,128)S(1)}) custom-call(f32[8,32,128]{2,1,0:T(8,128)S(1)} %shard_map.131.combined, f32[8,128]{1,0:T(8,128)S(1)} %get-tuple-element.48.beyond, bf16[256,256]{1,0:T(8,128)(2,1)S(1)} %copy-done.8), custom_call_target="tpu_custom_call" | custom-call | flops 500000000 | bytes 1048576 | tf_op jit(solution)/shard_map/pallas_call | solution.py:724
  35.3 0.0 collective-permute-done.7.got_a
  35.3 0.0 collective-permute-done.8.got_b
  35.3 0.3 shard_map.138
  35.6 2.1 %collective-permute-start.9 = (f32[16,256]{1,0:T(8,128)S(1)}, f32[16,256]{1,0:T(8,128)S(1)}, u32[]{:S(2)}, u32[]{:S(2)}) collective-permute-start(f32[16,256]{1,0:T(8,128)S(1)} %get-tuple-element.62), channel_id=1, source_target_pairs={{0,7},{1,0},{2,1},{3,2},{4,3},{5,4},{6,5},{7,6},{8,15},{9,8},{10,9... | collective-permute-start | bytes 49160 | tf_op jit(solution)/shard_map/ppermute | solution.py:608
  37.7 2.2 %shard_map.137.combined = f32[8,32,128]{2,1,0:T(8,128)S(1)} custom-call(f32[8,32,8,128]{3,2,1,0:T(8,128)S(1)} %get-tuple-element.54.fine, f32[8,16,8,128]{3,2,1,0:T(8,128)S(1)} %get-tuple-element.55.coarse, f32[120,8,128]{2,1,0:T(8,128)S(1)} %collective-permute-done.7.got_a, f32[120,8,128]{2,1,0:T(8,128)S(1)} %collective-permute-done.8.got_b, ...), custom_call_target="tpu_custom_call" | custom-call | flops 500000000 | bytes 1048576 | tf_op jit(solution)/shard_map/pallas_call | solution.py:623
  39.9 0.0 collective-permute-done.9.north
  39.9 1.4 %shard_map.139 = f32[16,64,256]{2,1,0:T(8,128)} custom-call(f32[16,64,256]{2,1,0:T(8,128)} %get-tuple-element.49.before, f32[8,32,128]{2,1,0:T(8,128)S(1)} %shard_map.137.combined, f32[8,128]{1,0:T(8,128)S(1)} %get-tuple-element.61.beyond, f32[16,256]{1,0:T(8,128)S(1)} %collective-permute-done.9.north, ...), custom_call_target="tpu_custom_call", output_to_operand_aliasing={{}: (0, {})} | custom-call | flops 500000000 | bytes 1048576 | tf_op jit(solution)/shard_map/pallas_call | solution.py:733
  (1 shorter events, 0.0 us)
Async XLA Ops:
  0.0 7.0 %copy-start.3 = (bf16[256,256]{1,0:T(8,128)(2,1)S(1)}, bf16[256,256]{1,0:T(8,128)(2,1)}, u32[]{:S(2)}) copy-start(bf16[256,256]{1,0:T(8,128)(2,1)} %constant.22.clone.restrict) | copy-start | bytes 393220
  0.0 7.0 %copy-start = (bf16[1024,256]{1,0:T(8,128)(2,1)S(1)}, bf16[1024,256]{1,0:T(8,128)(2,1)}, u32[]{:S(2)}) copy-start(bf16[1024,256]{1,0:T(8,128)(2,1)} %constant.33.packing) | copy-start | bytes 1572868
  1.0 6.0 %collective-permute-start = (f32[16,256]{1,0:T(8,128)S(1)}, f32[16,256]{1,0:T(8,128)S(1)}, u32[]{:S(2)}, u32[]{:S(2)}) collective-permute-start(f32[16,256]{1,0:T(8,128)S(1)} %bitcast.3), channel_id=1, source_target_pairs={{0,1},{1,2},{2,3},{3,4},{4,5},{5,6},{6,7},{7,0},{8,9},{9,10},{10,1... | collective-permute-start | bytes 49160 | tf_op jit(solution)/shard_map/ppermute | solution.py:608
  8.3 7.4 %collective-permute-start.1 = (f32[256,128]{1,0:T(8,128)S(1)}, f32[256,128]{1,0:T(8,128)S(1)}, u32[]{:S(2)}, u32[]{:S(2)}) collective-permute-start(f32[256,128]{1,0:T(8,128)S(1)} %get-tuple-element.38.own_a), channel_id=1, source_target_pairs={{0,8},{8,16},{16,24},{24,0},{1,9},{9,17},{17,25},{25,1},{2,10},{10... | collective-permute-start | bytes 393224 | tf_op jit(solution)/shard_map/ppermute | solution.py:608
  10.4 8.6 %copy-start.5 = (bf16[256,128]{1,0:T(8,128)(2,1)S(1)}, bf16[256,128]{1,0:T(8,128)(2,1)}, u32[]{:S(2)}) copy-start(bf16[256,128]{1,0:T(8,128)(2,1)} %constant.26.clone.beyond_high) | copy-start | bytes 196612
  10.4 8.6 %copy-start.6 = (bf16[256,128]{1,0:T(8,128)(2,1)S(1)}, bf16[256,128]{1,0:T(8,128)(2,1)}, u32[]{:S(2)}) copy-start(bf16[256,128]{1,0:T(8,128)(2,1)} %constant.27.clone.beyond_low) | copy-start | bytes 196612
  10.4 8.6 %copy-start.7 = (bf16[128,128]{1,0:T(8,128)(2,1)S(1)}, bf16[128,128]{1,0:T(8,128)(2,1)}, u32[]{:S(2)}) copy-start(bf16[128,128]{1,0:T(8,128)(2,1)} %constant.30.clone.choice) | copy-start | bytes 98308
  10.4 8.6 %collective-permute-start.2 = (f32[256,128]{1,0:T(8,128)S(1)}, f32[256,128]{1,0:T(8,128)S(1)}, u32[]{:S(2)}, u32[]{:S(2)}) collective-permute-start(f32[256,128]{1,0:T(8,128)S(1)} %get-tuple-element.39.own_b), channel_id=1, source_target_pairs={{0,24},{8,0},{16,8},{24,16},{1,25},{9,1},{17,9},{25,17},{2,26},{10... | collective-permute-start | bytes 393224 | tf_op jit(solution)/shard_map/ppermute | solution.py:608
  12.8 9.7 %collective-permute-start.5 = (f32[256,128]{1,0:T(8,128)S(1)}, f32[256,128]{1,0:T(8,128)S(1)}, u32[]{:S(2)}, u32[]{:S(2)}) collective-permute-start(f32[256,128]{1,0:T(8,128)S(1)} %get-tuple-element.51.own_a), channel_id=1, source_target_pairs={{0,8},{8,16},{16,24},{24,0},{1,9},{9,17},{17,25},{25,1},{2,10},{10... | collective-permute-start | bytes 393224 | tf_op jit(solution)/shard_map/ppermute | solution.py:608
  13.8 10.8 %collective-permute-start.6 = (f32[256,128]{1,0:T(8,128)S(1)}, f32[256,128]{1,0:T(8,128)S(1)}, u32[]{:S(2)}, u32[]{:S(2)}) collective-permute-start(f32[256,128]{1,0:T(8,128)S(1)} %get-tuple-element.52.own_b), channel_id=1, source_target_pairs={{0,24},{8,0},{16,8},{24,16},{1,25},{9,1},{17,9},{25,17},{2,26},{10... | collective-permute-start | bytes 393224 | tf_op jit(solution)/shard_map/ppermute | solution.py:608
  20.8 10.0 %collective-permute-start.3 = (f32[120,8,128]{2,1,0:T(8,128)S(1)}, f32[120,8,128]{2,1,0:T(8,128)S(1)}, u32[]{:S(2)}, u32[]{:S(2)}) collective-permute-start(f32[120,8,128]{2,1,0:T(8,128)S(1)} %get-tuple-element.45.own_rows), channel_id=1, source_target_pairs={{0,1},{1,0},{2,3},{3,2},{4,5},{5,4},{6,7},{7,6},{8,9},{9,8},{10,11... | collective-permute-start | bytes 1474568 | tf_op jit(solution)/shard_map/ppermute | solution.py:618
  20.9 9.9 %collective-permute-start.4 = (f32[120,8,128]{2,1,0:T(8,128)S(1)}, f32[120,8,128]{2,1,0:T(8,128)S(1)}, u32[]{:S(2)}, u32[]{:S(2)}) collective-permute-start(f32[120,8,128]{2,1,0:T(8,128)S(1)} %get-tuple-element.46), channel_id=1, source_target_pairs={{0,8},{1,2},{2,1},{3,4},{4,3},{5,6},{6,5},{7,15},{8,0},{9,10},{10,... | collective-permute-start | bytes 1474568 | tf_op jit(solution)/shard_map/ppermute | solution.py:618
  26.3 9.0 %collective-permute-start.7 = (f32[120,8,128]{2,1,0:T(8,128)S(1)}, f32[120,8,128]{2,1,0:T(8,128)S(1)}, u32[]{:S(2)}, u32[]{:S(2)}) collective-permute-start(f32[120,8,128]{2,1,0:T(8,128)S(1)} %get-tuple-element.56.own_rows), channel_id=1, source_target_pairs={{0,1},{1,0},{2,3},{3,2},{4,5},{5,4},{6,7},{7,6},{8,9},{9,8},{10,11... | collective-permute-start | bytes 1474568 | tf_op jit(solution)/shard_map/ppermute | solution.py:618
  26.4 8.9 %collective-permute-start.8 = (f32[120,8,128]{2,1,0:T(8,128)S(1)}, f32[120,8,128]{2,1,0:T(8,128)S(1)}, u32[]{:S(2)}, u32[]{:S(2)}) collective-permute-start(f32[120,8,128]{2,1,0:T(8,128)S(1)} %get-tuple-element.57), channel_id=1, source_target_pairs={{0,8},{1,2},{2,1},{3,4},{4,3},{5,6},{6,5},{7,15},{8,0},{9,10},{10,... | collective-permute-start | bytes 1474568 | tf_op jit(solution)/shard_map/ppermute | solution.py:618
  28.0 2.8 %copy-start.4 = (bf16[128,128]{1,0:T(8,128)(2,1)S(1)}, bf16[128,128]{1,0:T(8,128)(2,1)}, u32[]{:S(2)}) copy-start(bf16[128,128]{1,0:T(8,128)(2,1)} %constant.24.clone.refining) | copy-start | bytes 98308
  30.8 2.2 %copy-start.1 = (bf16[3,3,128,128]{3,2,1,0:T(8,128)(2,1)S(1)}, bf16[3,3,128,128]{3,2,1,0:T(8,128)(2,1)}, u32[]{:S(2)}) copy-start(bf16[3,3,128,128]{3,2,1,0:T(8,128)(2,1)} %constant.28.clone.row_highs) | copy-start | bytes 884740
  30.8 2.2 %copy-start.2 = (bf16[3,3,128,128]{3,2,1,0:T(8,128)(2,1)S(1)}, bf16[3,3,128,128]{3,2,1,0:T(8,128)(2,1)}, u32[]{:S(2)}) copy-start(bf16[3,3,128,128]{3,2,1,0:T(8,128)(2,1)} %constant.29.clone.row_lows) | copy-start | bytes 884740
  33.0 0.9 %copy-start.8 = (bf16[256,256]{1,0:T(8,128)(2,1)S(1)}, bf16[256,256]{1,0:T(8,128)(2,1)}, u32[]{:S(2)}) copy-start(bf16[256,256]{1,0:T(8,128)(2,1)} %constant.25.clone.interpolation) | copy-start | bytes 393220
  35.6 4.3 %collective-permute-start.9 = (f32[16,256]{1,0:T(8,128)S(1)}, f32[16,256]{1,0:T(8,128)S(1)}, u32[]{:S(2)}, u32[]{:S(2)}) collective-permute-start(f32[16,256]{1,0:T(8,128)S(1)} %get-tuple-element.62), channel_id=1, source_target_pairs={{0,7},{1,0},{2,1},{3,2},{4,3},{5,4},{6,5},{7,6},{8,15},{9,8},{10,9... | collective-permute-start | bytes 49160 | tf_op jit(solution)/shard_map/ppermute | solution.py:608

commit v5 on v4

--- a/solution.py
+++ b/solution.py
@@ -14,8 +14,10 @@
 
 LANES = 128
 GROUP = 8
-SLOT = 16
-EDGE = 15
+SLOTS = (12, 14)
+FREE = (8, 9)
+USED = (8 * 12, 8 * 14)
+COMPACT = 64
 COLUMN = 32
 CHUNKS = 2
 PER_LEVEL = 14
@@ -66,17 +68,21 @@
     return np.stack(rows)
 
 
+def edge_lane(side, line):
+    return SLOTS[side] * (line // 4 * 4 + 3) + FREE[side] + line % 4
+
+
 def message_lanes():
     places = []
     for line in range(GROUP):
-        places += [(0, line * SLOT + c, c, 1, line) for c in range(8)]
-        places += [(1, line * SLOT + c, 16 + c, 1, line) for c in range(9)]
-        if line % 2 == 0:
-            places += [(0, line * SLOT + 8 + c, 8 + c, 2, line) for c in range(4)]
-            places += [(1, line * SLOT + 9 + c, 25 + c, 2, line) for c in range(5)]
-        if line % 4 == 1:
-            places += [(0, line * SLOT + 8 + c, 12 + c, 4, line - 1) for c in range(4)]
-            places += [(1, line * SLOT + 9 + c, 30 + c, 4, line - 1) for c in range(5)]
+        for side, (first, second, fourth) in enumerate(((0, 8, 12), (16, 25, 30))):
+            start = line * SLOTS[side]
+            places += [(side, start + c, first + c, 1, line, line) for c in range(FREE[side])]
+            rest = [start + c for c in range(FREE[side], SLOTS[side])]
+            if line % 2 == 0:
+                places += [(side, lane, second + c, 2, line, line) for c, lane in enumerate(rest)]
+            if line % 4 == 1:
+                places += [(side, lane, fourth + c, 4, line - 1, line) for c, lane in enumerate(rest)]
     return places
 
 
@@ -84,20 +90,27 @@
     table = np.zeros((GROUP, width, 2 * LANES), np.float32)
     east = list(range(width - 8, width)) + [width // 2 - 8 + c for c in range(4)] + [width // 4 - 8 + c for c in range(4)]
     west = list(range(9)) + [4 + c for c in range(5)] + [4 + c for c in range(5)]
-    for side, lane, compact, factor, line in message_lanes():
+    for side, lane, compact, factor, line, _ in message_lanes():
         start = (west[compact - 16] if side else east[compact]) * factor
         table[line:line + factor, start:start + factor, side * LANES + lane] = 1.0
     return table
 
 
 def halo_table(columns, width, first):
-    table = np.zeros((2, 2 * SLOT, 2 * LANES))
-    outer = columns[width:]
-    for side, lane, compact, factor, line in message_lanes():
-        if line < 2 and lane < 2 * SLOT:
-            table[lane // SLOT, side * SLOT + lane % SLOT] = outer[compact]
-    table[:, EDGE] = 0.0 if first else columns[0]
-    table[:, SLOT + EDGE] = outer[16]
+    table = np.zeros((COMPACT, 2 * LANES))
+    table[:35] = columns[width:]
+    table[35] = 0.0 if first else columns[0]
+    return table
+
+
+def halo_places():
+    table = np.zeros((4, LANES, COMPACT), np.float32)
+    for side, lane, compact, _, _, line in message_lanes():
+        if line < 4:
+            table[line, side * 64 + lane, compact] = 1.0
+    for line in range(4):
+        table[line, edge_lane(0, line), 35] = 1.0
+        table[line, 64 + edge_lane(1, line), 16] = 1.0
     return table
 
 
@@ -129,7 +142,7 @@
     low = [width - 8 + c for c in range(8)] + [width // 2 - 8 + c for c in range(4)] + [width // 4 - 8 + c for c in range(4)]
     high = [width + c for c in range(9)] + [width // 2 + 4 + c for c in range(5)] + [width // 4 + 4 + c for c in range(5)]
     ends = {(1, 16 + 8): 1, (2, 25 + 4): 2}
-    for side, lane, compact, factor, line in message_lanes():
+    for side, lane, compact, factor, line, _ in message_lanes():
         place = (high[compact - 16] if side else low[compact]) * factor
         for generation, _ in generations:
             if generation >= factor and generation <= ends.get((factor, compact), 4):
@@ -138,7 +151,7 @@
     for line in range(GROUP):
         for generation, _ in generations:
             weight = filters[generation][width // generation + 8]
-            table[LANES + line * SLOT + EDGE, column_lane(generation, line // generation)] += weight
+            table[LANES + edge_lane(1, line), column_lane(generation, line // generation)] += weight
     return table
 
 
@@ -157,7 +170,7 @@
 def edge_choice_table():
     table = np.zeros((LANES, LANES), np.float32)
     for line in range(GROUP):
-        table[line * SLOT + EDGE, line] = 1.0
+        table[edge_lane(1, line), line] = 1.0
     return table
 
 
@@ -198,41 +211,38 @@
     return pl.ds(pl.multiple_of(index * 8, 8), 8)
 
 
-def prepare_kernel(height, gradient, members, restrict, own_tables, halo_tables, across, turned, edges, high_weights, low_weights,
-                   fine, raw, table, own_case, halo_case, sems):
-    case = column_case()
+def prepare_kernel(chunk, levels, height, *refs):
+    if chunk:
+        (gradient, members, restrict, _), (across, turned, edges), (fine, raw, table, sems) = refs[:4], refs[4:7], refs[7:]
+    else:
+        (gradient, members, restrict, own_tables, halo_tables, places, refine), refs = refs[:7], refs[7:]
+        across, turned, edges, high_weights, low_weights, refine_out, fine, raw, table, own_case, halo_case, placing, sems = refs
     blocks = height // GROUP
-    levels = members.shape[1]
-    part = levels // 4
-    copies = [pltpu.make_async_copy(restrict, table, sems.at[8])]
-    for i in range(4):
-        span = pl.ds(i * part, part)
-        copies.append(pltpu.make_async_copy(gradient.at[span], fine.at[span], sems.at[i]))
-    for i in range(4):
-        span = pl.ds(i * part, part)
-        copies.append(pltpu.make_async_copy(members.at[:, span], raw.at[:, span], sems.at[4 + i]))
-    copies.append(pltpu.make_async_copy(own_tables.at[case], own_case, sems.at[9]))
-    copies.append(pltpu.make_async_copy(halo_tables.at[case], halo_case, sems.at[10]))
+    first, part = chunk * levels, levels // 2
+    copies = [pltpu.make_async_copy(restrict, table, sems.at[0])]
+    for i in range(2):
+        span = pl.ds(first + i * part, part)
+        copies.append(pltpu.make_async_copy(gradient.at[span], fine.at[pl.ds(i * part, part)], sems.at[1 + i]))
+    for i in range(2):
+        span = pl.ds(first + i * part, part)
+        copies.append(pltpu.make_async_copy(members.at[:, span], raw.at[:, pl.ds(i * part, part)], sems.at[3 + i]))
+    if not chunk:
+        case = column_case()
+        copies.append(pltpu.make_async_copy(own_tables.at[case], own_case, sems.at[5]))
+        copies.append(pltpu.make_async_copy(halo_tables.at[case], halo_case, sems.at[6]))
+        copies.append(pltpu.make_async_copy(places, placing, sems.at[7]))
+        copies.append(pltpu.make_async_copy(refine, refine_out, sems.at[8]))
     for copy in copies:
         copy.start()
     copies[0].wait()
     for half in range(2):
         across[half, :, 0:8, :] = jnp.zeros((levels, 8, LANES), F32)
-    for i in range(4):
+    for i in range(2):
         copies[1 + i].wait()
         value = exact_dot(fine[i * part:(i + 1) * part].reshape(part * 2 * height, fine.shape[2]), table[...])
         value = value.reshape(part, 2 * height, 2 * LANES)
         for half in range(2):
             across[half, i * part:(i + 1) * part, 8:, :] = value[:, :, half * LANES:(half + 1) * LANES]
-    copies[9].wait()
-    copies[10].wait()
-    for part_of, target in ((0, high_weights), (1, low_weights)):
-        for variant in range(4):
-            target[variant, :LANES, :] = own_case[part_of]
-            target[variant, LANES:, :] = jnp.zeros((LANES, 2 * LANES), BF16)
-            for side in range(2):
-                start = LANES + side * 64 + variant * SLOT
-                target[variant, start:start + SLOT, :] = halo_case[part_of, variant % 2, side * SLOT:(side + 1) * SLOT, :]
     lane = lax.broadcasted_iota(jnp.int32, (GROUP, LANES), 1)
 
     def level_step(level, _):
@@ -242,18 +252,25 @@
             block_rows = jnp.swapaxes(raw[:, level, span, :], 0, 1)
             turned[level, span] = block_rows
             for line in range(GROUP):
-                member = block_rows[line]
-                spot = line * SLOT + EDGE
-                edge = jnp.where(lane == spot, pltpu.roll(member, spot, 1), edge)
+                spot = edge_lane(1, line)
+                edge = jnp.where(lane == spot, pltpu.roll(block_rows[line], spot, 1), edge)
             edges[tile(level * blocks + block), :] = edge
         return 0
 
-    for i in range(4):
-        copies[5 + i].wait()
-        lax.fori_loop(i * part, (i + 1) * part, level_step, 0)
-
-
-def pack_kernel(chunk, levels, height, across, turned, edges, south, restrict, packing, products, message_a, message_b, coarse, below):
+    for i in range(2):
+        copies[3 + i].wait()
+        lax.fori_loop(i * part, (i + 1) * part, level_step, 0, unroll=4)
+    if not chunk:
+        for copy in copies[5:]:
+            copy.wait()
+        for which, target in ((0, high_weights), (1, low_weights)):
+            for variant in range(4):
+                target[variant, :LANES, :] = own_case[which]
+                target[variant, LANES:, :] = mul(placing[variant], halo_case[which]).astype(BF16)
+
+
+def pack_kernel(chunk, levels, height, across, turned, edges, south, restrict, packing, products, own_east, own_west, to_east, to_west,
+                coarse, below):
     blocks = height // GROUP
     first = chunk * levels
     value = exact_dot(south[...], restrict[...]) * jnp.where(lax.axis_index("gy") == 0, 0.0, 1.0).astype(F32)
@@ -261,50 +278,72 @@
         below[half] = value[:, half * LANES:(half + 1) * LANES]
     lane = lax.broadcasted_iota(jnp.int32, (GROUP, LANES), 1)
     line_of = lax.broadcasted_iota(jnp.int32, (GROUP, LANES), 0)
+    spots = (line_of >> 2) * (4 * SLOTS[0]) + edge_lane(0, 0) + (line_of & 3)
     top = lax.broadcasted_iota(jnp.int32, (height, LANES), 0) == 0
 
     def level_step(level, _):
         for half in range(2):
             under = jnp.broadcast_to(below[half, pl.ds(first + level, 1), :], (height, LANES))
-            under = jnp.where(top, under, across[half, first + level, pl.ds(7, height, 2), :])
-            coarse[half] = across[half, first + level, pl.ds(8, height, 2), :] + 0.5 * (
-                across[half, first + level, pl.ds(9, height, 2), :] + under
+            under = jnp.where(top, under, across[half, level, pl.ds(7, height, 2), :])
+            coarse[half] = across[half, level, pl.ds(8, height, 2), :] + 0.5 * (
+                across[half, level, pl.ds(9, height, 2), :] + under
             )
         for block in range(blocks):
             place_rows = tile(level * blocks + block)
             for line in range(GROUP):
                 y = block * GROUP + line
-                products[line, place_rows, :] = turned[first + level, y] * coarse[0, y:y + 1, :]
+                products[line, place_rows, :] = turned[level, y] * coarse[0, y:y + 1, :]
             column = jnp.broadcast_to(coarse[1, block * GROUP:(block + 1) * GROUP, 0:1], (GROUP, LANES))
-            column = jnp.sum(jnp.where(lane == line_of * SLOT + EDGE, column, 0.0), axis=0, keepdims=True)
-            message_a[place_rows, :] = jnp.broadcast_to(column, (GROUP, LANES))
+            column = jnp.sum(jnp.where(lane == spots, column, 0.0), axis=0, keepdims=True)
+            own_east[place_rows, :] = jnp.broadcast_to(column, (GROUP, LANES))
         return 0
 
-    lax.fori_loop(0, levels, level_step, 0)
+    lax.fori_loop(0, levels, level_step, 0, unroll=4)
     total = jnp.zeros((levels * blocks * 8, 2 * LANES), F32)
     for line in range(0, GROUP, 2):
         value = jnp.concatenate([products[line], products[line + 1]], axis=1)
         total = total + exact_dot(value, packing[line * LANES:(line + 2) * LANES, :])
-    to_east = total[:, :LANES] + message_a[...]
-    to_west = total[:, LANES:] + edges[first * blocks * 8:(first + levels) * blocks * 8, :]
-    message_a[...] = to_east
-    message_b[...] = to_west
-
-
-def columns_kernel(levels, height, products, own_a, own_b, got_a, got_b, high_weights, low_weights, beyond_high, beyond_low, choice,
+    own_east[...] = own_east[...] + total[:, :LANES]
+    own_west[...] = total[:, LANES:] + edges[...]
+    lane = lax.broadcasted_iota(jnp.int32, (levels, 8, LANES), 2)
+    groups = [own_east[...].reshape(levels, 4, 8, LANES)[:, i] for i in range(4)]
+    for i in range(3):
+        to_east[i] = jnp.where(lane < USED[0], groups[i], pltpu.roll(groups[3], USED[0] - 32 * i, 2))
+    lane = lane[:levels // 2]
+    groups = [own_west[...].reshape(levels // 2, 8, 8, LANES)[:, i] for i in range(8)]
+    for i in range(7):
+        to_west[i] = jnp.where(lane < USED[1], groups[i], pltpu.roll(groups[7], USED[1] - 16 * i, 2))
+
+
+def columns_kernel(levels, height, products, own_a, own_b, from_west, from_east, high_weights, low_weights, beyond_high, beyond_low, choice,
                    filtered, message_a, message_b, factors):
     blocks = height // GROUP
     groups = levels * blocks
     lane = lax.broadcasted_iota(jnp.int32, (groups * 8, LANES), 1)
-    own_east, own_west, west, east = own_a[...], own_b[...], got_a[...], got_b[...]
-    spot = lane % SLOT == EDGE
+    own_east, own_west = own_a[...], own_b[...]
+    whole = lax.broadcasted_iota(jnp.int32, (levels, 8, LANES), 2)
+    parts = [from_west[i] for i in range(3)]
+    last = pltpu.roll(parts[2], 96, 2)
+    for i in range(2):
+        last = jnp.where((whole >= 32 * i) & (whole < 32 * i + 32), pltpu.roll(parts[i], 32 * i + 32, 2), last)
+    west = jnp.stack(parts + [last], axis=1).reshape(groups * 8, LANES)
+    whole = whole[:levels // 2]
+    parts = [from_east[i] for i in range(7)]
+    last = pltpu.roll(parts[6], 112, 2)
+    for i in range(6):
+        last = jnp.where((whole >= 16 * i) & (whole < 16 * i + 16), pltpu.roll(parts[i], 16 * i + 16, 2), last)
+    east = jnp.stack(parts + [last], axis=1).reshape(groups * 8, LANES)
     chosen = exact_dot(east, choice[...]).reshape(levels, blocks, 8, LANES)
     total = chosen[:, 0]
     for block in range(1, blocks):
         total = total + pltpu.roll(chosen[:, block], block * GROUP, 2)
     factors[...] = total
-    west = jnp.where(spot, west * own_west, west)
-    east = jnp.where(spot, east * own_east, east)
+    shifts = [edge_lane(1, line) - edge_lane(0, line) for line in (0, 4)]
+    for line, shift in zip((0, 4), shifts):
+        spot = (lane >= edge_lane(0, line)) & (lane < edge_lane(0, line) + 4)
+        west = jnp.where(spot, west * pltpu.roll(own_west, LANES - shift, 1), west)
+        spot = (lane >= edge_lane(1, line)) & (lane < edge_lane(1, line) + 4)
+        east = jnp.where(spot, east * pltpu.roll(own_east, shift, 1), east)
     inside = jnp.where(lax.axis_index("gx") == lax.axis_size("gx") - 1, 0.0, 1.0).astype(F32)
     beyond = three_dots(jnp.concatenate([own_east, east], axis=1), beyond_high[...], beyond_low[...])
     beyond = (beyond * inside).reshape(levels, blocks, 8, LANES)
@@ -315,7 +354,7 @@
         message[levels * PER_LEVEL:] = total
     halves = [
         split(jnp.where(lane < 64, west, pltpu.roll(east, 64, 1))),
-        split(jnp.where(lane < 64, pltpu.roll(west, 64, 1), east)),
+        split(jnp.where(lane < 64, pltpu.roll(west, LANES - USED[0] // 2, 1), pltpu.roll(east, 64 - USED[1] // 2, 1))),
     ]
     for line in range(GROUP):
         high, low = (jnp.concatenate(pair, axis=1) for pair in zip(split(products[line]), halves[line // 4]))
@@ -348,7 +387,7 @@
                 message[level * PER_LEVEL + 8 + i] = jnp.where(small < 96, rows[i], spare)
         return 0
 
-    lax.fori_loop(0, levels, level_step, 0)
+    lax.fori_loop(0, levels, level_step, 0, unroll=4)
 
 
 def convolve_own(load, count, low_edges, high_edges, store):
@@ -409,7 +448,7 @@
         convolve_own(load_coarse, half, low, [(high_second, half), (high_fourth, quarter)], store_to(coarse))
         return 0
 
-    lax.fori_loop(0, levels, level_step, 0)
+    lax.fori_loop(0, levels, level_step, 0, unroll=4)
 
 
 def outside(load):
@@ -474,7 +513,7 @@
         value = fine[level, 0]
         for j in range(8):
             value = value + double_taps[j + 1] * jnp.where(up_a, keep * got_b[base + 7 - j], got_a[base + 7 - j])
-        value = turned[first + level, 0] * (weight * value + refined[level * 8:level * 8 + 8, :])
+        value = turned[level, 0] * (weight * value + refined[level * 8:level * 8 + 8, :])
         first_row[first + level:first + level + 1, :LANES] = jnp.sum(value, axis=0, keepdims=True) * (1.0 / 7.0)
     first_row[first:, LANES:] = beyond[...]
 
@@ -528,12 +567,12 @@
                 if y >= height - 8:
                     value = value + fine_north[height - 1 - y]
                 value = weight * value + refined[y // 2 * 8:y // 2 * 8 + 8, :]
-                weighted.append(turned[first + level, y] * value)
+                weighted.append(turned[level, y] * value)
             total = jnp.sum(jnp.swapaxes(jnp.stack(weighted), 0, 1), axis=0)
             combined[level, block * GROUP:(block + 1) * GROUP, :] = total * (1.0 / 7.0)
         return 0
 
-    lax.fori_loop(0, levels, level_step, 0)
+    lax.fori_loop(0, levels, level_step, 0, unroll=4)
 
 
 def interpolate_levels(combined, beyond, north, first, start, part, interpolation, extended, rows):
@@ -649,6 +688,7 @@
     columns = [column_table(width, i == 0, i == 2) for i in range(3)]
     own_tables = np.stack(halves_of(np.stack([table[:width] for table in columns])), axis=1)
     halo_tables = np.stack(halves_of(np.stack([halo_table(table, width, i == 0) for i, table in enumerate(columns)])), axis=1)
+    places = halo_places()
     restrict = jnp.asarray(restriction_table(width), BF16)
     packing = jnp.asarray(packing_table(width), BF16).reshape(GROUP * width, 2 * LANES)
     refining = jnp.asarray(refining_table(width), BF16)
@@ -659,31 +699,35 @@
     flops = 10**9 // CHUNKS
     far_rows = (levels * (PER_LEVEL + 1), 8, LANES)
 
-    constants = (restrict, jnp.asarray(own_tables), jnp.asarray(halo_tables))
-    across, turned, edges, high_weights, low_weights = call(
-        functools.partial(prepare_kernel, height),
-        [(2, all_levels, 8 + 2 * height, LANES), (all_levels, height, 8, LANES), (all_levels * height, LANES),
-         ((4, 2 * LANES, 2 * LANES), BF16), ((4, 2 * LANES, 2 * LANES), BF16)],
-        [gradient.shape, members.shape, pltpu.VMEM(restrict.shape, BF16), pltpu.VMEM(own_tables.shape[1:], BF16),
-         pltpu.VMEM(halo_tables.shape[1:], BF16), pltpu.SemaphoreType.DMA((11,))],
-        flops, *(pltpu.with_memory_space_constraint(a, pltpu.HBM) for a in (gradient, members) + constants), in_hbm=5,
-    )
-    packed = [
-        call(
+    hbm_of = functools.partial(pltpu.with_memory_space_constraint, memory_space=pltpu.HBM)
+    constants = tuple(map(hbm_of, (jnp.asarray(own_tables), jnp.asarray(halo_tables), jnp.asarray(places, BF16), interpolation)))
+    gradient, members, far_restrict = map(hbm_of, (gradient, members, restrict))
+    prepared, packed = [], []
+    for chunk in range(CHUNKS):
+        outs = [(2, levels, 8 + 2 * height, LANES), (levels, height, 8, LANES), (levels * height, LANES)]
+        scratch = [(levels, fine_height, fine_width), (8, levels, height, LANES), pltpu.VMEM(restrict.shape, BF16)]
+        if chunk == 0:
+            outs += [((4, 2 * LANES, 2 * LANES), BF16), ((4, 2 * LANES, 2 * LANES), BF16), (interpolation.shape, BF16)]
+            scratch += [pltpu.VMEM(shape, BF16) for shape in (own_tables.shape[1:], halo_tables.shape[1:], places.shape)]
+        extra = constants if chunk == 0 else (packed[-1][3],)
+        prepared.append(call(
+            functools.partial(prepare_kernel, chunk, levels, height), outs, scratch + [pltpu.SemaphoreType.DMA((9,))],
+            flops, gradient, members, far_restrict, *extra, in_hbm=3 if chunk else 7,
+        ))
+        packed.append(call(
             functools.partial(pack_kernel, chunk, levels, height),
-            [(GROUP, groups * 8, LANES), (groups * 8, LANES), (groups * 8, LANES)],
+            [(GROUP, groups * 8, LANES), (groups * 8, LANES), (groups * 8, LANES), (3, levels, 8, LANES), (7, levels // 2, 8, LANES)],
             [(2, height, LANES), (2, all_levels, LANES)],
-            flops, across, turned, edges, south, restrict, packing,
-        )
-        for chunk in range(CHUNKS)
-    ]
-    got = [(around(to_east, "gx", 1), around(to_west, "gx", -1)) for _, to_east, to_west in packed]
+            flops, *prepared[-1][:3], south, restrict, packing,
+        ))
+    high_weights, low_weights, interpolation = prepared[0][3:]
+    got = [(around(to_east, "gx", 1), around(to_west, "gx", -1)) for *_, to_east, to_west in packed]
     filtered = [
         call(
             functools.partial(columns_kernel, levels, height),
             [(groups, GROUP, 8, 2 * LANES), far_rows, far_rows, (levels, 8, LANES)],
             [],
-            flops, *packed[chunk], *got[chunk], high_weights, low_weights, beyond_high, beyond_low, choice,
+            flops, *packed[chunk][:3], *got[chunk], high_weights, low_weights, beyond_high, beyond_low, choice,
         )
         for chunk in range(CHUNKS)
     ]
@@ -709,7 +753,7 @@
             functools.partial(first_row_kernel, chunk, levels, height),
             [(levels, LANES), ((chunk + 1) * levels, 2 * LANES)],
             [(levels * 8, LANES)],
-            flops, *own[chunk], *far[chunk], filtered[chunk][1], filtered[chunk][3], turned, refining, row_highs, row_lows, *earlier,
+            flops, *own[chunk], *far[chunk], filtered[chunk][1], filtered[chunk][3], prepared[chunk][1], refining, row_highs, row_lows, *earlier,
         )
 
     def combined_of(chunk):
@@ -717,7 +761,7 @@
             functools.partial(combine_kernel, chunk, levels, height),
             [(levels, height, LANES)],
             [(height // 2 * 8, LANES), (height // 2 * 8, LANES)],
-            flops, *own[chunk], *far[chunk], turned, refining,
+            flops, *own[chunk], *far[chunk], prepared[chunk][1], refining,
         )[0]
 
     early_beyond, early_rows = first_rows_of(0)

time: 41.5 us -> 36.4 us (0.88)
  Pallas kernels: 20.8 us -> 17.2 us
  starting transfers between devices: 12 us -> 10 us
  waiting for transfers between devices: 6.72 us -> 7.76 us
  local copies, waits for them, and re-layouts: 1.63 us -> 1.03 us
    pallas_call x11 -> x12, Pallas kernels: 18 us -> 14.5 us  [call(): pl.pallas_call(kernel, out_shape=tuple((jax.ShapeDtypeStruct(*out) if isi...]
    ppermute x4, waiting for transfers between devices: 0.02 us -> 2.99 us  [swap(): return lax.ppermute(value, ('gx', 'gy'), pairs)]
    ppermute x6, waiting for transfers between devices: 6.71 us -> 4.77 us  [around(): lax.ppermute(value, axis, [(i, (i + step) % size) for i in range(size)])]
    ppermute x6, starting transfers between devices: 8.73 us -> 6.85 us  [around(): lax.ppermute(value, axis, [(i, (i + step) % size) for i in range(size)])]
    unnamed x19, local copies, waits for them, and re-layouts: 0.65 us -> 0.05 us
  transfers between devices with their start and end apart: 10 -> 10, of which waited for: 3 -> 6; matrix products, arithmetic and copies ran while one was open for 0% -> 0% of each run, Pallas kernels for 43% -> 40%
where the time goes in v5:
time: 36.4 us; the launch traced here: 36.2 us
  Pallas kernels  17.2 us (47%)
  starting transfers between devices  10 us (27%)
  waiting for transfers between devices  7.76 us (21%)
  local copies, waits for them, and re-layouts  1.03 us (3%)
    pallas_call x12, Pallas kernels, call(): pl.pallas_call(kernel, out_shape=tuple((jax.ShapeDtypeStruct(*out) if isi...  14.5 us
    ppermute x6, starting transfers between devices, around(): lax.ppermute(value, axis, [(i, (i + step) % size) for i in range(size)])  6.85 us
    ppermute x6, waiting for transfers between devices, around(): lax.ppermute(value, axis, [(i, (i + step) % size) for i in range(size)])  4.77 us
    ppermute x4, starting transfers between devices, swap(): return lax.ppermute(value, ('gx', 'gy'), pairs)  3.15 us
    ppermute x4, waiting for transfers between devices, swap(): return lax.ppermute(value, ('gx', 'gy'), pairs)  2.99 us
    pallas_call x1, Pallas kernels, shards(): pl.pallas_call(functools.partial(late_kernel, levels), out_shape=out_shap...  1.41 us
    pallas_call x1, Pallas kernels, shards(): pl.pallas_call(early_kernel, out_shape=(out_shape, jax.ShapeDtypeStruct((...  1.35 us
    slice x1, local copies, waits for them, and re-layouts, shards(): south = around(gradient[:, -1, :], 'gy', 1)  0.98 us
  transfers between devices with their start and end apart: 10, of which 6 were waited for; matrix products, arithmetic and copies ran while one was open for 0% of the time, Pallas kernels for 40%

profile of v5, /device:TPU:0, one launch (start us, length us, event | category | flops | bytes accessed | tf_op | source)
XLA Modules:
  0.0 36.2 jit_solution(5988188957522832613)
XLA Ops:
  0.0 0.0 copy-start
  0.0 0.0 copy-start.1
  0.0 1.0 %slice.3 = f32[16,1,256]{2,1,0:T(1,128)S(1)} slice(f32[16,64,256]{2,1,0:T(8,128)} %refs_0_.3), slice={[0:16], [63:64], [0:256]} | slice | bytes 32768 | tf_op jit(solution)/shard_map/slice | solution.py:686
  1.0 0.5 %collective-permute-start = (f32[16,256]{1,0:T(8,128)S(1)}, f32[16,256]{1,0:T(8,128)S(1)}, u32[]{:S(2)}, u32[]{:S(2)}) collective-permute-start(f32[16,256]{1,0:T(8,128)S(1)} %bitcast.3), channel_id=1, source_target_pairs={{0,1},{1,2},{2,3},{3,4},{4,5},{5,6},{6,7},{7,0},{8,9},{9,10},{10,1... | collective-permute-start | bytes 49160 | tf_op jit(solution)/shard_map/ppermute | solution.py:647
  1.5 2.4 %shard_map.136 = (f32[2,8,72,128]{3,2,1,0:T(8,128)S(1)}, f32[8,32,8,128]{3,2,1,0:T(8,128)S(1)}, f32[256,128]{1,0:T(8,128)S(1)}, bf16[4,256,256]{2,1,0:T(8,128)(2...) custom-call(f32[16,64,256]{2,1,0:T(8,128)} %refs_0_.3, f32[8,16,32,128]{3,2,1,0:T(8,128)} %refs_1_.3, ...), custom_call_target="tpu_custom_call" | custom-call | flops 500000000 | bytes 1048576 | tf_op jit(solution)/shard_map/pallas_call | solution.py:662
  4.0 3.0 %collective-permute-done.south = f32[16,256]{1,0:T(8,128)S(1)} collective-permute-done((f32[16,256]{1,0:T(8,128)S(1)}, f32[16,256]{1,0:T(8,128)S(1)}, u32[]{:S(2)}, u32[]{:S(2)}) %collective-permute-start) | collective-permute-done | bytes 16416 | tf_op jit(solution)/shard_map/ppermute | solution.py:647
  7.0 0.0 copy-done
  7.0 0.0 copy-done.1
  7.0 1.0 %shard_map.137 = (f32[8,256,128]{2,1,0:T(8,128)S(1)}, f32[256,128]{1,0:T(8,128)S(1)}, f32[256,128]{1,0:T(8,128)S(1)}, f32[3,8,8,128]{3,2,1,0:T(8,128)S(1)}, f32[7,4,8,128]{3,2,1,0:T(8,128)S(1)}) custom-call(f32[2,8,72,128]{3,2,1,0:T(8,128)S(1)} %get-tuple-element.42.across, f32[8,32,8,128]{3,2,1,0:T(8,128)S(1)} %get-tuple-element.43.turned, ...), custom_call_target="tpu_custom_call" | custom-call | flops 500000000 | bytes 1048576 | tf_op jit(solution)/shard_map/pallas_call | solution.py:662
  8.0 0.0 copy-start.2
  8.0 3.0 %collective-permute-start.2 = (f32[7,4,8,128]{3,2,1,0:T(8,128)S(1)}, f32[7,4,8,128]{3,2,1,0:T(8,128)S(1)}, u32[]{:S(2)}, u32[]{:S(2)}) collective-permute-start(f32[7,4,8,128]{3,2,1,0:T(8,128)S(1)} %get-tuple-element.49), channel_id=1, source_target_pairs={{0,24},{8,0},{16,8},{24,16},{1,25},{9,1},{17,9},{25,17},{2,26},{10... | collective-permute-start | bytes 344072 | tf_op jit(solution)/shard_map/ppermute | solution.py:647
  11.0 0.0 copy-start.6
  11.0 0.0 copy-start.7
  11.0 0.0 copy-start.8
  11.0 0.0 collective-permute-start.1
  11.0 2.1 %shard_map.143 = (f32[2,8,72,128]{3,2,1,0:T(8,128)S(1)}, f32[8,32,8,128]{3,2,1,0:T(8,128)S(1)}, f32[256,128]{1,0:T(8,128)S(1)}) custom-call(f32[16,64,256]{2,1,0:T(8,128)} %refs_0_.3, f32[8,16,32,128]{3,2,1,0:T(8,128)} %refs_1_.3, bf16[256,256]{1,0:T(8,128)(2,1)} %constant.24.clone.refs_2_.restrict, f32[3,8,8,128]{3,2,1,0:T(8,128)S(1)} %get-tuple-element.48.refs_3_), custom_call_target="tpu_custom_call" | custom-call | flops 500000000 | bytes 1048576 | tf_op jit(solution)/shard_map/pallas_call | solution.py:662
  13.1 0.0 copy-done.2
  13.2 1.0 %shard_map.144 = (f32[8,256,128]{2,1,0:T(8,128)S(1)}, f32[256,128]{1,0:T(8,128)S(1)}, f32[256,128]{1,0:T(8,128)S(1)}, f32[3,8,8,128]{3,2,1,0:T(8,128)S(1)}, f32[7,4,8,128]{3,2,1,0:T(8,128)S(1)}) custom-call(f32[2,8,72,128]{3,2,1,0:T(8,128)S(1)} %get-tuple-element.61.across, f32[8,32,8,128]{3,2,1,0:T(8,128)S(1)} %get-tuple-element.62.turned, ...), custom_call_target="tpu_custom_call" | custom-call | flops 500000000 | bytes 1048576 | tf_op jit(solution)/shard_map/pallas_call | solution.py:662
  14.1 2.0 %collective-permute-start.5 = (f32[3,8,8,128]{3,2,1,0:T(8,128)S(1)}, f32[3,8,8,128]{3,2,1,0:T(8,128)S(1)}, u32[]{:S(2)}, u32[]{:S(2)}) collective-permute-start(f32[3,8,8,128]{3,2,1,0:T(8,128)S(1)} %get-tuple-element.67), channel_id=1, source_target_pairs={{0,8},{8,16},{16,24},{24,0},{1,9},{9,17},{17,25},{25,1},{2,10},{10... | collective-permute-start | bytes 294920 | tf_op jit(solution)/shard_map/ppermute | solution.py:647
  16.1 1.0 %collective-permute-start.6 = (f32[7,4,8,128]{3,2,1,0:T(8,128)S(1)}, f32[7,4,8,128]{3,2,1,0:T(8,128)S(1)}, u32[]{:S(2)}, u32[]{:S(2)}) collective-permute-start(f32[7,4,8,128]{3,2,1,0:T(8,128)S(1)} %get-tuple-element.68), channel_id=1, source_target_pairs={{0,24},{8,0},{16,8},{24,16},{1,25},{9,1},{17,9},{25,17},{2,26},{10... | collective-permute-start | bytes 344072 | tf_op jit(solution)/shard_map/ppermute | solution.py:647
  17.1 0.0 collective-permute-done.1.from_west
  17.1 0.0 collective-permute-done.2.from_east
  17.1 0.0 copy-done.6
  17.1 0.0 copy-done.7
  17.2 0.0 copy-done.8
  17.2 1.4 %shard_map.138 = (f32[32,8,8,256]{3,2,1,0:T(8,128)S(1)}, f32[120,8,128]{2,1,0:T(8,128)S(1)}, f32[120,8,128]{2,1,0:T(8,128)S(1)}, f32[8,8,128]{2,1,0:T(8,128)S(1)}) custom-call(f32[8,256,128]{2,1,0:T(8,128)S(1)} %get-tuple-element.45.products, f32[256,128]{1,0:T(8,128)S(1)} %get-tuple-element.46.own_a, f32[256,128]{1,0:T(8,128)S(1)} %get-tuple-element.47.own_b, ...), custom_call_target="tpu_custom_call" | custom-call | flops 500000000 | bytes 1048576 | tf_op jit(solution)/shard_map/pallas_call | solution.py:662
  18.6 1.1 %collective-permute-start.4 = (f32[120,8,128]{2,1,0:T(8,128)S(1)}, f32[120,8,128]{2,1,0:T(8,128)S(1)}, u32[]{:S(2)}, u32[]{:S(2)}) collective-permute-start(f32[120,8,128]{2,1,0:T(8,128)S(1)} %get-tuple-element.56), channel_id=1, source_target_pairs={{0,8},{1,2},{2,1},{3,4},{4,3},{5,6},{6,5},{7,15},{8,0},{9,10},{10,... | collective-permute-start | bytes 1474568 | tf_op jit(solution)/shard_map/ppermute | solution.py:657
  19.7 0.0 collective-permute-start.3
  19.7 0.6 %collective-permute-done.5.from_west = f32[3,8,8,128]{3,2,1,0:T(8,128)S(1)} collective-permute-done((f32[3,8,8,128]{3,2,1,0:T(8,128)S(1)}, f32[3,8,8,128]{3,2,1,0:T(8,128)S(1)}, u32[]{:S(2)}, u32[]{:S(2)}) %collective-permute-start.5) | collective-permute-done | bytes 98336 | tf_op jit(solution)/shard_map/ppermute | solution.py:647
  20.3 0.6 %collective-permute-done.6.from_east = f32[7,4,8,128]{3,2,1,0:T(8,128)S(1)} collective-permute-done((f32[7,4,8,128]{3,2,1,0:T(8,128)S(1)}, f32[7,4,8,128]{3,2,1,0:T(8,128)S(1)}, u32[]{:S(2)}, u32[]{:S(2)}) %collective-permute-start.6) | collective-permute-done | bytes 114720 | tf_op jit(solution)/shard_map/ppermute | solution.py:647
  20.9 1.4 %shard_map.145 = (f32[32,8,8,256]{3,2,1,0:T(8,128)S(1)}, f32[120,8,128]{2,1,0:T(8,128)S(1)}, f32[120,8,128]{2,1,0:T(8,128)S(1)}, f32[8,8,128]{2,1,0:T(8,128)S(1)}) custom-call(f32[8,256,128]{2,1,0:T(8,128)S(1)} %get-tuple-element.64.products, f32[256,128]{1,0:T(8,128)S(1)} %get-tuple-element.65.own_a, f32[256,128]{1,0:T(8,128)S(1)} %get-tuple-element.66.own_b, ...), custom_call_target="tpu_custom_call" | custom-call | flops 500000000 | bytes 1048576 | tf_op jit(solution)/shard_map/pallas_call | solution.py:662
  22.3 2.1 %collective-permute-start.8 = (f32[120,8,128]{2,1,0:T(8,128)S(1)}, f32[120,8,128]{2,1,0:T(8,128)S(1)}, u32[]{:S(2)}, u32[]{:S(2)}) collective-permute-start(f32[120,8,128]{2,1,0:T(8,128)S(1)} %get-tuple-element.73), channel_id=1, source_target_pairs={{0,8},{1,2},{2,1},{3,4},{4,3},{5,6},{6,5},{7,15},{8,0},{9,10},{10,... | collective-permute-start | bytes 1474568 | tf_op jit(solution)/shard_map/ppermute | solution.py:657
  24.4 0.0 collective-permute-start.7
  24.4 0.0 copy-start.5
  24.4 1.3 %shard_map.139 = (f32[8,32,8,128]{3,2,1,0:T(8,128)S(1)}, f32[8,16,8,128]{3,2,1,0:T(8,128)S(1)}) custom-call(f32[32,8,8,256]{3,2,1,0:T(8,128)S(1)} %get-tuple-element.52.filtered), custom_call_target="tpu_custom_call" | custom-call | flops 500000000 | bytes 1048576 | tf_op jit(solution)/shard_map/pallas_call | solution.py:662
  25.8 1.4 %shard_map.146 = (f32[8,32,8,128]{3,2,1,0:T(8,128)S(1)}, f32[8,16,8,128]{3,2,1,0:T(8,128)S(1)}) custom-call(f32[32,8,8,256]{3,2,1,0:T(8,128)S(1)} %get-tuple-element.69.filtered), custom_call_target="tpu_custom_call" | custom-call | flops 500000000 | bytes 1048576 | tf_op jit(solution)/shard_map/pallas_call | solution.py:662
  27.1 0.0 copy-start.3
  27.2 0.0 copy-start.4
  27.2 0.3 collective-permute-done.4.got_b
  27.5 0.0 collective-permute-done.3.got_a
  27.5 0.0 copy-done.5
  27.5 0.9 %shard_map.140.combined = f32[8,32,128]{2,1,0:T(8,128)S(1)} custom-call(f32[8,32,8,128]{3,2,1,0:T(8,128)S(1)} %get-tuple-element.53.fine, f32[8,16,8,128]{3,2,1,0:T(8,128)S(1)} %get-tuple-element.54.coarse, f32[120,8,128]{2,1,0:T(8,128)S(1)} %collective-permute-done.3.got_a, f32[120,8,128]{2,1,0:T(8,128)S(1)} %collective-permute-done.4.got_b, ...), custom_call_target="tpu_custom_call" | custom-call | flops 500000000 | bytes 1048576 | tf_op jit(solution)/shard_map/pallas_call | solution.py:662
  28.5 0.0 copy-done.3
  28.5 0.0 copy-done.4
  28.5 0.3 shard_map.141
  28.8 1.3 %shard_map.142 = (f32[16,64,256]{2,1,0:T(8,128)}, f32[8,8,256]{2,1,0:T(8,128)S(1)}) custom-call(f32[8,32,128]{2,1,0:T(8,128)S(1)} %shard_map.140.combined, f32[8,128]{1,0:T(8,128)S(1)} %get-tuple-element.58.beyond, bf16[256,256]{1,0:T(8,128)(2,1)S(1)} %get-tuple-element.59.interpolation), custom_call_target="tpu_custom_call" | custom-call | flops 500000000 | bytes 1048576 | tf_op jit(solution)/shard_map/pallas_call | solution.py:768
  30.1 2.6 %collective-permute-done.8.got_b = f32[120,8,128]{2,1,0:T(8,128)S(1)} collective-permute-done((f32[120,8,128]{2,1,0:T(8,128)S(1)}, f32[120,8,128]{2,1,0:T(8,128)S(1)}, u32[]{:S(2)}, u32[]{:S(2)}) %collective-permute-start.8) | collective-permute-done | bytes 491552 | tf_op jit(solution)/shard_map/ppermute | solution.py:657
  32.8 0.0 collective-permute-done.7.got_a
  32.8 0.3 shard_map.148
  33.1 0.3 collective-permute-start.9
  33.4 0.9 %shard_map.147.combined = f32[8,32,128]{2,1,0:T(8,128)S(1)} custom-call(f32[8,32,8,128]{3,2,1,0:T(8,128)S(1)} %get-tuple-element.70.fine, f32[8,16,8,128]{3,2,1,0:T(8,128)S(1)} %get-tuple-element.71.coarse, f32[120,8,128]{2,1,0:T(8,128)S(1)} %collective-permute-done.7.got_a, f32[120,8,128]{2,1,0:T(8,128)S(1)} %collective-permute-done.8.got_b, ...), custom_call_target="tpu_custom_call" | custom-call | flops 500000000 | bytes 1048576 | tf_op jit(solution)/shard_map/pallas_call | solution.py:662
  34.3 0.5 %collective-permute-done.9.north = f32[16,256]{1,0:T(8,128)S(1)} collective-permute-done((f32[16,256]{1,0:T(8,128)S(1)}, f32[16,256]{1,0:T(8,128)S(1)}, u32[]{:S(2)}, u32[]{:S(2)}) %collective-permute-start.9) | collective-permute-done | bytes 16416 | tf_op jit(solution)/shard_map/ppermute | solution.py:647
  34.8 1.4 %shard_map.149 = f32[16,64,256]{2,1,0:T(8,128)} custom-call(f32[16,64,256]{2,1,0:T(8,128)} %get-tuple-element.60.before, f32[8,32,128]{2,1,0:T(8,128)S(1)} %shard_map.147.combined, f32[8,128]{1,0:T(8,128)S(1)} %get-tuple-element.77.beyond, f32[16,256]{1,0:T(8,128)S(1)} %collective-permute-done.9.north, ...), custom_call_target="tpu_custom_call", output_to_operand_aliasing={{}: (0, {})} | custom-call | flops 500000000 | bytes 1048576 | tf_op jit(solution)/shard_map/pallas_call | solution.py:777
  (1 shorter events, 0.0 us)
Async XLA Ops:
  0.0 7.0 %copy-start = (bf16[1024,256]{1,0:T(8,128)(2,1)S(1)}, bf16[1024,256]{1,0:T(8,128)(2,1)}, u32[]{:S(2)}) copy-start(bf16[1024,256]{1,0:T(8,128)(2,1)} %constant.36.packing) | copy-start | bytes 1572868
  0.0 7.0 %copy-start.1 = (bf16[256,256]{1,0:T(8,128)(2,1)S(1)}, bf16[256,256]{1,0:T(8,128)(2,1)}, u32[]{:S(2)}) copy-start(bf16[256,256]{1,0:T(8,128)(2,1)} %constant.24.clone.refs_2_.restrict) | copy-start | bytes 393220
  1.0 6.0 %collective-permute-start = (f32[16,256]{1,0:T(8,128)S(1)}, f32[16,256]{1,0:T(8,128)S(1)}, u32[]{:S(2)}, u32[]{:S(2)}) collective-permute-start(f32[16,256]{1,0:T(8,128)S(1)} %bitcast.3), channel_id=1, source_target_pairs={{0,1},{1,2},{2,3},{3,4},{4,5},{5,6},{6,7},{7,0},{8,9},{9,10},{10,1... | collective-permute-start | bytes 49160 | tf_op jit(solution)/shard_map/ppermute | solution.py:647
  8.0 5.2 %copy-start.2 = (bf16[256,256]{1,0:T(8,128)(2,1)S(1)}, bf16[256,256]{1,0:T(8,128)(2,1)}, u32[]{:S(2)}) copy-start(bf16[256,256]{1,0:T(8,128)(2,1)} %constant.24.clone.refs_2_.restrict) | copy-start | bytes 393220
  8.0 9.1 %collective-permute-start.2 = (f32[7,4,8,128]{3,2,1,0:T(8,128)S(1)}, f32[7,4,8,128]{3,2,1,0:T(8,128)S(1)}, u32[]{:S(2)}, u32[]{:S(2)}) collective-permute-start(f32[7,4,8,128]{3,2,1,0:T(8,128)S(1)} %get-tuple-element.49), channel_id=1, source_target_pairs={{0,24},{8,0},{16,8},{24,16},{1,25},{9,1},{17,9},{25,17},{2,26},{10... | collective-permute-start | bytes 344072 | tf_op jit(solution)/shard_map/ppermute | solution.py:647
  11.0 6.2 %copy-start.6 = (bf16[256,128]{1,0:T(8,128)(2,1)S(1)}, bf16[256,128]{1,0:T(8,128)(2,1)}, u32[]{:S(2)}) copy-start(bf16[256,128]{1,0:T(8,128)(2,1)} %constant.29.clone.beyond_low) | copy-start | bytes 196612
  11.0 6.2 %copy-start.7 = (bf16[256,128]{1,0:T(8,128)(2,1)S(1)}, bf16[256,128]{1,0:T(8,128)(2,1)}, u32[]{:S(2)}) copy-start(bf16[256,128]{1,0:T(8,128)(2,1)} %constant.28.clone.beyond_high) | copy-start | bytes 196612
  11.0 6.2 %copy-start.8 = (bf16[128,128]{1,0:T(8,128)(2,1)S(1)}, bf16[128,128]{1,0:T(8,128)(2,1)}, u32[]{:S(2)}) copy-start(bf16[128,128]{1,0:T(8,128)(2,1)} %constant.32.clone.choice) | copy-start | bytes 98308
  11.0 6.1 %collective-permute-start.1 = (f32[3,8,8,128]{3,2,1,0:T(8,128)S(1)}, f32[3,8,8,128]{3,2,1,0:T(8,128)S(1)}, u32[]{:S(2)}, u32[]{:S(2)}) collective-permute-start(f32[3,8,8,128]{3,2,1,0:T(8,128)S(1)} %get-tuple-element.48.refs_3_), channel_id=1, source_target_pairs={{0,8},{8,16},{16,24},{24,0},{1,9},{9,17},{17,25},{25,1},{2,10},{10... | collective-permute-start | bytes 294920 | tf_op jit(solution)/shard_map/ppermute | solution.py:647
  14.1 6.1 %collective-permute-start.5 = (f32[3,8,8,128]{3,2,1,0:T(8,128)S(1)}, f32[3,8,8,128]{3,2,1,0:T(8,128)S(1)}, u32[]{:S(2)}, u32[]{:S(2)}) collective-permute-start(f32[3,8,8,128]{3,2,1,0:T(8,128)S(1)} %get-tuple-element.67), channel_id=1, source_target_pairs={{0,8},{8,16},{16,24},{24,0},{1,9},{9,17},{17,25},{25,1},{2,10},{10... | collective-permute-start | bytes 294920 | tf_op jit(solution)/shard_map/ppermute | solution.py:647
  16.1 4.8 %collective-permute-start.6 = (f32[7,4,8,128]{3,2,1,0:T(8,128)S(1)}, f32[7,4,8,128]{3,2,1,0:T(8,128)S(1)}, u32[]{:S(2)}, u32[]{:S(2)}) collective-permute-start(f32[7,4,8,128]{3,2,1,0:T(8,128)S(1)} %get-tuple-element.68), channel_id=1, source_target_pairs={{0,24},{8,0},{16,8},{24,16},{1,25},{9,1},{17,9},{25,17},{2,26},{10... | collective-permute-start | bytes 344072 | tf_op jit(solution)/shard_map/ppermute | solution.py:647
  18.6 8.9 %collective-permute-start.4 = (f32[120,8,128]{2,1,0:T(8,128)S(1)}, f32[120,8,128]{2,1,0:T(8,128)S(1)}, u32[]{:S(2)}, u32[]{:S(2)}) collective-permute-start(f32[120,8,128]{2,1,0:T(8,128)S(1)} %get-tuple-element.56), channel_id=1, source_target_pairs={{0,8},{1,2},{2,1},{3,4},{4,3},{5,6},{6,5},{7,15},{8,0},{9,10},{10,... | collective-permute-start | bytes 1474568 | tf_op jit(solution)/shard_map/ppermute | solution.py:657
  19.7 7.8 %collective-permute-start.3 = (f32[120,8,128]{2,1,0:T(8,128)S(1)}, f32[120,8,128]{2,1,0:T(8,128)S(1)}, u32[]{:S(2)}, u32[]{:S(2)}) collective-permute-start(f32[120,8,128]{2,1,0:T(8,128)S(1)} %get-tuple-element.55.own_rows), channel_id=1, source_target_pairs={{0,1},{1,0},{2,3},{3,2},{4,5},{5,4},{6,7},{7,6},{8,9},{9,8},{10,11... | collective-permute-start | bytes 1474568 | tf_op jit(solution)/shard_map/ppermute | solution.py:657
  22.3 10.4 %collective-permute-start.8 = (f32[120,8,128]{2,1,0:T(8,128)S(1)}, f32[120,8,128]{2,1,0:T(8,128)S(1)}, u32[]{:S(2)}, u32[]{:S(2)}) collective-permute-start(f32[120,8,128]{2,1,0:T(8,128)S(1)} %get-tuple-element.73), channel_id=1, source_target_pairs={{0,8},{1,2},{2,1},{3,4},{4,3},{5,6},{6,5},{7,15},{8,0},{9,10},{10,... | collective-permute-start | bytes 1474568 | tf_op jit(solution)/shard_map/ppermute | solution.py:657
  24.4 8.4 %collective-permute-start.7 = (f32[120,8,128]{2,1,0:T(8,128)S(1)}, f32[120,8,128]{2,1,0:T(8,128)S(1)}, u32[]{:S(2)}, u32[]{:S(2)}) collective-permute-start(f32[120,8,128]{2,1,0:T(8,128)S(1)} %get-tuple-element.72.own_rows), channel_id=1, source_target_pairs={{0,1},{1,0},{2,3},{3,2},{4,5},{5,4},{6,7},{7,6},{8,9},{9,8},{10,11... | collective-permute-start | bytes 1474568 | tf_op jit(solution)/shard_map/ppermute | solution.py:657
  24.4 3.1 %copy-start.5 = (bf16[128,128]{1,0:T(8,128)(2,1)S(1)}, bf16[128,128]{1,0:T(8,128)(2,1)}, u32[]{:S(2)}) copy-start(bf16[128,128]{1,0:T(8,128)(2,1)} %constant.26.clone.refining) | copy-start | bytes 98308
  27.1 1.3 %copy-start.3 = (bf16[3,3,128,128]{3,2,1,0:T(8,128)(2,1)S(1)}, bf16[3,3,128,128]{3,2,1,0:T(8,128)(2,1)}, u32[]{:S(2)}) copy-start(bf16[3,3,128,128]{3,2,1,0:T(8,128)(2,1)} %constant.31.clone.row_lows) | copy-start | bytes 884740
  27.2 1.3 %copy-start.4 = (bf16[3,3,128,128]{3,2,1,0:T(8,128)(2,1)S(1)}, bf16[3,3,128,128]{3,2,1,0:T(8,128)(2,1)}, u32[]{:S(2)}) copy-start(bf16[3,3,128,128]{3,2,1,0:T(8,128)(2,1)} %constant.30.clone.row_highs) | copy-start | bytes 884740
  33.1 1.8 %collective-permute-start.9 = (f32[16,256]{1,0:T(8,128)S(1)}, f32[16,256]{1,0:T(8,128)S(1)}, u32[]{:S(2)}, u32[]{:S(2)}) collective-permute-start(f32[16,256]{1,0:T(8,128)S(1)} %get-tuple-element.78), channel_id=1, source_target_pairs={{0,7},{1,0},{2,1},{3,2},{4,3},{5,4},{6,5},{7,6},{8,15},{9,8},{10,9... | collective-permute-start | bytes 49160 | tf_op jit(solution)/shard_map/ppermute | solution.py:647

commit v6 on v5

--- a/solution.py
+++ b/solution.py
@@ -7,6 +7,7 @@
 from jax.experimental import pallas as pl
 from jax.experimental.pallas import tpu as pltpu
 from jax.sharding import PartitionSpec as P
+
 
 beta_raw = [(1.0 - (offset - 4) ** 2 / 25.0) ** 2 for offset in range(9)]
 beta_taps = [value / sum(beta_raw) for value in beta_raw]
@@ -20,7 +21,7 @@
 COMPACT = 64
 COLUMN = 32
 CHUNKS = 2
-PER_LEVEL = 14
+PARTS = 4
 VMEM_LIMIT = 20 * 2**20
 BF16, F32 = jnp.bfloat16, jnp.float32
 double_taps = [
@@ -30,6 +31,7 @@
     [sum(beta_taps[i - k + 4] * beta_taps[k - j + 4] for k in range(-4, 0) if i - k <= 4 and j - k <= 4) for j in range(4)]
     for i in range(4)
 ]
+
 
 def twice_filter(width, first, last):
     low, high = (0 if first else -99), (width - 1 if last else width + 99)
@@ -211,62 +213,68 @@
     return pl.ds(pl.multiple_of(index * 8, 8), 8)
 
 
-def prepare_kernel(chunk, levels, height, *refs):
-    if chunk:
-        (gradient, members, restrict, _), (across, turned, edges), (fine, raw, table, sems) = refs[:4], refs[4:7], refs[7:]
-    else:
-        (gradient, members, restrict, own_tables, halo_tables, places, refine), refs = refs[:7], refs[7:]
-        across, turned, edges, high_weights, low_weights, refine_out, fine, raw, table, own_case, halo_case, placing, sems = refs
+def turn_members(height, raw, first, turned, edges, start, stop, rims=None):
     blocks = height // GROUP
-    first, part = chunk * levels, levels // 2
-    copies = [pltpu.make_async_copy(restrict, table, sems.at[0])]
-    for i in range(2):
-        span = pl.ds(first + i * part, part)
-        copies.append(pltpu.make_async_copy(gradient.at[span], fine.at[pl.ds(i * part, part)], sems.at[1 + i]))
-    for i in range(2):
-        span = pl.ds(first + i * part, part)
-        copies.append(pltpu.make_async_copy(members.at[:, span], raw.at[:, pl.ds(i * part, part)], sems.at[3 + i]))
-    if not chunk:
-        case = column_case()
-        copies.append(pltpu.make_async_copy(own_tables.at[case], own_case, sems.at[5]))
-        copies.append(pltpu.make_async_copy(halo_tables.at[case], halo_case, sems.at[6]))
-        copies.append(pltpu.make_async_copy(places, placing, sems.at[7]))
-        copies.append(pltpu.make_async_copy(refine, refine_out, sems.at[8]))
-    for copy in copies:
-        copy.start()
-    copies[0].wait()
-    for half in range(2):
-        across[half, :, 0:8, :] = jnp.zeros((levels, 8, LANES), F32)
-    for i in range(2):
-        copies[1 + i].wait()
-        value = exact_dot(fine[i * part:(i + 1) * part].reshape(part * 2 * height, fine.shape[2]), table[...])
-        value = value.reshape(part, 2 * height, 2 * LANES)
-        for half in range(2):
-            across[half, i * part:(i + 1) * part, 8:, :] = value[:, :, half * LANES:(half + 1) * LANES]
     lane = lax.broadcasted_iota(jnp.int32, (GROUP, LANES), 1)
+    up_a = lax.axis_index("gy") % 2 == 0
 
     def level_step(level, _):
+        ends = []
         for block in range(blocks):
             edge = jnp.zeros((GROUP, LANES), F32)
             span = slice(block * GROUP, (block + 1) * GROUP)
-            block_rows = jnp.swapaxes(raw[:, level, span, :], 0, 1)
+            block_rows = jnp.swapaxes(raw[:, first + level, span, :], 0, 1)
             turned[level, span] = block_rows
             for line in range(GROUP):
                 spot = edge_lane(1, line)
                 edge = jnp.where(lane == spot, pltpu.roll(block_rows[line], spot, 1), edge)
             edges[tile(level * blocks + block), :] = edge
+            ends.append(block_rows)
+        if rims:
+            rims[0][level] = jnp.where(up_a, ends[-1], ends[0])
+            rims[1][level] = jnp.where(up_a, ends[0], ends[-1])
         return 0
 
+    lax.fori_loop(start, stop, level_step, 0, unroll=4)
+
+
+def reduce_columns(fine, first, count, height, table, across, start):
+    value = exact_dot(fine[first:first + count].reshape(count * 2 * height, fine.shape[2]), table[...])
+    value = value.reshape(count, 2 * height, 2 * LANES)
+    for half in range(2):
+        across[half, start:start + count, 8:, :] = value[:, :, half * LANES:(half + 1) * LANES]
+        across[half, start:start + count, 0:8, :] = jnp.zeros((count, 8, LANES), F32)
+
+
+def prepare_kernel(levels, height, gradient, members, restrict, own_tables, halo_tables, places, refine,
+                   across, turned, edges, high_weights, low_weights, refine_out, fine, raw, table, own_case, halo_case, placing, sems):
+    part = levels // 2
+    case = column_case()
+    moves = [(restrict, table)]
+    moves += [(gradient.at[pl.ds(i * part, part)], fine.at[pl.ds(i * part, part)]) for i in range(2)]
+    moves += [(members.at[:, pl.ds(i * part, part)], raw.at[:, pl.ds(i * part, part)]) for i in range(2)]
+    moves += [(own_tables.at[case], own_case), (halo_tables.at[case], halo_case), (places, placing), (refine, refine_out)]
+    copies = [pltpu.make_async_copy(source, target, sems.at[i]) for i, (source, target) in enumerate(moves)]
+    for copy in copies:
+        copy.start()
+    copies[0].wait()
+    for i in range(2):
+        copies[1 + i].wait()
+        reduce_columns(fine, i * part, part, height, table, across, i * part)
     for i in range(2):
         copies[3 + i].wait()
-        lax.fori_loop(i * part, (i + 1) * part, level_step, 0, unroll=4)
-    if not chunk:
-        for copy in copies[5:]:
-            copy.wait()
-        for which, target in ((0, high_weights), (1, low_weights)):
-            for variant in range(4):
-                target[variant, :LANES, :] = own_case[which]
-                target[variant, LANES:, :] = mul(placing[variant], halo_case[which]).astype(BF16)
+        turn_members(height, raw, 0, turned, edges, i * part, (i + 1) * part)
+    for copy in copies[5:]:
+        copy.wait()
+    for which, target in ((0, high_weights), (1, low_weights)):
+        for variant in range(4):
+            target[variant, :LANES, :] = own_case[which]
+            target[variant, LANES:, :] = mul(placing[variant], halo_case[which]).astype(BF16)
+
+
+def prepare_more_kernel(chunk, levels, height, gradient, members, restrict, _, across, turned, edges, rim_a, rim_b):
+    reduce_columns(gradient, chunk * levels, levels, height, restrict, across, 0)
+    turn_members(height, members, chunk * levels, turned, edges, 0, levels, (rim_a, rim_b))
 
 
 def pack_kernel(chunk, levels, height, across, turned, edges, south, restrict, packing, products, own_east, own_west, to_east, to_west,
@@ -315,8 +323,29 @@
         to_west[i] = jnp.where(lane < USED[1], groups[i], pltpu.roll(groups[7], USED[1] - 16 * i, 2))
 
 
-def columns_kernel(levels, height, products, own_a, own_b, from_west, from_east, high_weights, low_weights, beyond_high, beyond_low, choice,
-                   filtered, message_a, message_b, factors):
+def outside(load):
+    values = [load(j) for j in range(8)]
+    result = []
+    for i in range(8):
+        total = double_taps[i + 1] * values[0]
+        for j in range(1, 8 - i):
+            total = total + double_taps[i + 1 + j] * values[j]
+        result.append(total)
+    return result
+
+
+def per_level_of(chunk):
+    return 7 if chunk else 14
+
+
+def columns_kernel(chunk, levels, height, products, own_a, own_b, from_west, from_east, high_weights, low_weights,
+                   beyond_high, beyond_low, choice, *refs):
+    if chunk:
+        rims, refs, weighted = refs[:2], refs[3:-1], refs[-1]
+    else:
+        refs = refs[1:]
+    filtered, message_a, message_b, factors = refs
+    per_level = per_level_of(chunk)
     blocks = height // GROUP
     groups = levels * blocks
     lane = lax.broadcasted_iota(jnp.int32, (groups * 8, LANES), 1)
@@ -351,7 +380,7 @@
     for block in range(1, blocks):
         total = total + pltpu.roll(beyond[:, block], block * COLUMN, 2)
     for message in (message_a, message_b):
-        message[levels * PER_LEVEL:] = total
+        message[levels * per_level:] = total
     halves = [
         split(jnp.where(lane < 64, west, pltpu.roll(east, 64, 1))),
         split(jnp.where(lane < 64, pltpu.roll(west, LANES - USED[0] // 2, 1), pltpu.roll(east, 64 - USED[1] // 2, 1))),
@@ -375,16 +404,27 @@
         for block in range(blocks):
             for half in range(2):
                 fourth.append(sum(at(block, half * 4 + k) for k in range(1, 4)) + at(block, half * 4))
-        for message, start, coarse in ((message_a, start_a, coarse_a), (message_b, start_b, coarse_b)):
+        sides = ((message_a, start_a, coarse_a, up_a), (message_b, start_b, coarse_b, jnp.logical_not(up_a)))
+        for side, (message, start, coarse, upward) in enumerate(sides):
+            if chunk:
+                def nearest(j):
+                    return filtered[level * blocks + start, jnp.where(upward, 7 - j, j), :, :LANES]
+
+                for i, value in enumerate(outside(nearest)):
+                    place = jnp.where(upward, i, 7 - i)
+                    weighted[side, place] = rims[side][level, place] * value
+                total = jnp.sum(jnp.swapaxes(weighted[side], 0, 1), axis=0)
+                message[level * per_level] = jnp.float32(generations[0][1]) * total
             rows = []
             for line in range(GROUP):
-                message[level * PER_LEVEL + line] = filtered[level * blocks + start, line, :, :LANES]
+                if not chunk:
+                    message[level * per_level + line] = filtered[level * blocks + start, line, :, :LANES]
                 block, pair = coarse + line // 4, line % 4
                 pairs = at(block, 2 * pair) + at(block, 2 * pair + 1)
                 rows.append(jnp.where(second, pairs, fourth[line]))
             for i in range(6):
                 spare = pltpu.roll(rows[6 + i // 3], 96 - 32 * (i % 3), 1)
-                message[level * PER_LEVEL + 8 + i] = jnp.where(small < 96, rows[i], spare)
+                message[level * per_level + per_level - 6 + i] = jnp.where(small < 96, rows[i], spare)
         return 0
 
     lax.fori_loop(0, levels, level_step, 0, unroll=4)
@@ -435,6 +475,7 @@
         def store_to(ref):
             def store(r, value):
                 ref[level, r] = value
+
             return store
 
         convolve_own(lambda r: at(r, 0), height, low, [(high, height)], store_to(fine))
@@ -449,17 +490,6 @@
         return 0
 
     lax.fori_loop(0, levels, level_step, 0, unroll=4)
-
-
-def outside(load):
-    values = [load(j) for j in range(8)]
-    result = []
-    for i in range(8):
-        total = double_taps[i + 1] * values[0]
-        for j in range(1, 8 - i):
-            total = total + double_taps[i + 1 + j] * values[j]
-        result.append(total)
-    return result
 
 
 def coarse_rows(packed, lane):
@@ -474,7 +504,7 @@
     return jnp.where(lane < 64, jnp.float32(generations[1][1]), jnp.float32(generations[2][1]))
 
 
-def first_row_kernel(chunk, levels, height, fine, coarse, got_a, got_b, own_rows, factors, turned, refining, row_highs, row_lows, *refs):
+def first_row_kernel(chunk, levels, fine, coarse, got_a, got_b, own_rows, factors, turned, refining, row_highs, row_lows, *refs):
     earlier, (beyond, first_row, packed) = refs[:1] if chunk else (), refs[-3:]
     first = chunk * levels
     up_a = lax.axis_index("gy") % 2 == 0
@@ -484,7 +514,9 @@
         return value.reshape(levels * 8, LANES)
 
     case = jnp.where(gy == 0, 0, jnp.where(gy == ny - 1, 2, 1))
-    extra = slice(levels * PER_LEVEL, levels * (PER_LEVEL + 1))
+    per_level = per_level_of(chunk)
+    skip = per_level - 6
+    extra = slice(levels * per_level, levels * (per_level + 1))
     far_a, far_b = side(got_a[extra]), side(got_b[extra])
     value = three_dots(side(own_rows[extra]), row_highs[case, 0], row_lows[case, 0])
     value = value + three_dots(jnp.where(up_a, far_b, far_a), row_highs[case, 1], row_lows[case, 1])
@@ -496,32 +528,36 @@
     weight = jnp.float32(generations[0][1])
     keep = jnp.where((gy == 0) | (gy == ny - 1), 0.0, 1.0).astype(F32)
     for level in range(levels):
-        base = level * PER_LEVEL
+        base = level * per_level
         value = coarse[level, 0]
-        below = [jnp.where(up_a, keep * got_b[base + 8 + r], got_a[base + 8 + r]) for r in range(6)]
+        below = [jnp.where(up_a, keep * got_b[base + skip + r], got_a[base + skip + r]) for r in range(6)]
         below = coarse_rows(below, lane)
         for j in range(8):
             value = value + double_taps[j + 1] * below[7 - j]
-        above = jnp.where(up_a, got_a[base + 8], keep * got_b[base + 8])
+        above = jnp.where(up_a, got_a[base + skip], keep * got_b[base + skip])
         value = value + jnp.where(second, 0.0, double_taps[8] * above)
         packed[level * 8:level * 8 + 8, :] = value * coarse_scale(lane)
     refined = exact_dot(packed[...], refining[...])
     for rows in earlier:
         first_row[:first, :] = rows[...]
     for level in range(levels):
-        base = level * PER_LEVEL
+        base = level * per_level
         value = fine[level, 0]
-        for j in range(8):
-            value = value + double_taps[j + 1] * jnp.where(up_a, keep * got_b[base + 7 - j], got_a[base + 7 - j])
+        if not chunk:
+            for j in range(8):
+                value = value + double_taps[j + 1] * jnp.where(up_a, keep * got_b[base + 7 - j], got_a[base + 7 - j])
         value = turned[level, 0] * (weight * value + refined[level * 8:level * 8 + 8, :])
-        first_row[first + level:first + level + 1, :LANES] = jnp.sum(value, axis=0, keepdims=True) * (1.0 / 7.0)
+        value = jnp.sum(value, axis=0, keepdims=True)
+        if chunk:
+            value = value + jnp.where(up_a, keep * got_b[base, 0:1, :], got_a[base, 0:1, :])
+        first_row[first + level:first + level + 1, :LANES] = value * (1.0 / 7.0)
     first_row[first:, LANES:] = beyond[...]
 
 
 def combine_kernel(chunk, levels, height, fine, coarse, got_a, got_b, turned, refining, combined, stacked, refined):
     blocks = height // GROUP
     half, quarter = height // 2, height // 4
-    first = chunk * levels
+    per_level = per_level_of(chunk)
     up_a = lax.axis_index("gy") % 2 == 0
     lane = lax.broadcasted_iota(jnp.int32, (8, LANES), 1)
     second = lane < 64
@@ -531,17 +567,20 @@
     keep = jnp.where((gy == 0) | (gy == ny - 1), 0.0, 1.0).astype(F32)
 
     def level_step(level, _):
+        base = level * per_level
+
         def north(r):
-            return jnp.where(up_a, got_a[level * PER_LEVEL + r], keep * got_b[level * PER_LEVEL + r])
+            return jnp.where(up_a, got_a[base + r], keep * got_b[base + r])
 
         def south(r):
-            return jnp.where(up_a, keep * got_b[level * PER_LEVEL + r], got_a[level * PER_LEVEL + r])
-
-        below = coarse_rows([south(8 + r) for r in range(6)], lane)
-        above = coarse_rows([north(8 + r) for r in range(6)], lane)
-        fine_south = outside(lambda j: south(7 - j))
+            return jnp.where(up_a, keep * got_b[base + r], got_a[base + r])
+
+        below = coarse_rows([south(per_level - 6 + r) for r in range(6)], lane)
+        above = coarse_rows([north(per_level - 6 + r) for r in range(6)], lane)
+        if not chunk:
+            fine_south = outside(lambda j: south(7 - j))
+            fine_north = outside(north)
         coarse_south = outside(lambda j: below[7 - j])
-        fine_north = outside(north)
         coarse_north = outside(lambda j: above[j])
         parts = []
         for r in range(half):
@@ -562,13 +601,17 @@
             for line in range(GROUP):
                 y = block * GROUP + line
                 value = fine[level, y]
-                if y < 8:
+                if y < 8 and not chunk:
                     value = value + fine_south[y]
-                if y >= height - 8:
+                if y >= height - 8 and not chunk:
                     value = value + fine_north[height - 1 - y]
                 value = weight * value + refined[y // 2 * 8:y // 2 * 8 + 8, :]
                 weighted.append(turned[level, y] * value)
             total = jnp.sum(jnp.swapaxes(jnp.stack(weighted), 0, 1), axis=0)
+            if chunk and block == 0:
+                total = total + south(0)
+            if chunk and block == blocks - 1:
+                total = total + north(0)
             combined[level, block * GROUP:(block + 1) * GROUP, :] = total * (1.0 / 7.0)
         return 0
 
@@ -602,7 +645,7 @@
 
 def early_kernel(combined, beyond, interpolation, out, tails, extended, rows, ready, sems):
     levels = combined.shape[0]
-    part = levels // 2
+    part = levels // PARTS
     done = ready.shape[1] - 8
     copies = []
     for start in range(0, levels, part):
@@ -617,7 +660,7 @@
 
 def late_kernel(first, before, combined, beyond, north, interpolation, tails, out, extended, rows, ready, ends, kept, shifted, sems):
     levels = combined.shape[0]
-    part = levels // 2
+    part = levels // PARTS
     lane = lax.broadcasted_iota(jnp.int32, shifted.shape, 1)
     inside = jnp.where(lax.axis_index("gy") == lax.axis_size("gy") - 1, 0.0, 1.0).astype(F32)
     corner = jnp.broadcast_to(north[:, LANES:LANES + 1], shifted.shape) * inside
@@ -630,7 +673,7 @@
     for level in range(first):
         ends[level, 7:8, :] = ends[level, 7:8, :] + row[level:level + 1, :]
     done = ready.shape[1] - 8
-    copies.append(pltpu.make_async_copy(ends, out.at[pl.ds(0, first), pl.ds(done, 8)], sems.at[2]))
+    copies.append(pltpu.make_async_copy(ends, out.at[pl.ds(0, first), pl.ds(done, 8)], sems.at[PARTS]))
     copies[-1].start()
     for start in range(0, levels, part):
         span = pl.ds(start, part)
@@ -697,23 +740,24 @@
     row_highs, row_lows = map(jnp.asarray, halves_of(np.stack([column_rows_table(height, i == 0, i == 2) for i in range(3)])))
     choice = jnp.asarray(edge_choice_table(), BF16)
     flops = 10**9 // CHUNKS
-    far_rows = (levels * (PER_LEVEL + 1), 8, LANES)
 
     hbm_of = functools.partial(pltpu.with_memory_space_constraint, memory_space=pltpu.HBM)
     constants = tuple(map(hbm_of, (jnp.asarray(own_tables), jnp.asarray(halo_tables), jnp.asarray(places, BF16), interpolation)))
-    gradient, members, far_restrict = map(hbm_of, (gradient, members, restrict))
+    far_inputs = tuple(map(hbm_of, (gradient, members, restrict)))
     prepared, packed = [], []
     for chunk in range(CHUNKS):
         outs = [(2, levels, 8 + 2 * height, LANES), (levels, height, 8, LANES), (levels * height, LANES)]
-        scratch = [(levels, fine_height, fine_width), (8, levels, height, LANES), pltpu.VMEM(restrict.shape, BF16)]
         if chunk == 0:
             outs += [((4, 2 * LANES, 2 * LANES), BF16), ((4, 2 * LANES, 2 * LANES), BF16), (interpolation.shape, BF16)]
-            scratch += [pltpu.VMEM(shape, BF16) for shape in (own_tables.shape[1:], halo_tables.shape[1:], places.shape)]
-        extra = constants if chunk == 0 else (packed[-1][3],)
-        prepared.append(call(
-            functools.partial(prepare_kernel, chunk, levels, height), outs, scratch + [pltpu.SemaphoreType.DMA((9,))],
-            flops, gradient, members, far_restrict, *extra, in_hbm=3 if chunk else 7,
-        ))
+            scratch = [(levels, fine_height, fine_width), (8, levels, height, LANES)]
+            shapes = (restrict.shape, own_tables.shape[1:], halo_tables.shape[1:], places.shape)
+            scratch += [pltpu.VMEM(shape, BF16) for shape in shapes] + [pltpu.SemaphoreType.DMA((9,))]
+            kernel = functools.partial(prepare_kernel, levels, height)
+            prepared.append(call(kernel, outs, scratch, flops, *far_inputs, *constants, in_hbm=7))
+        else:
+            outs += [(levels, 8, 8, LANES), (levels, 8, 8, LANES)]
+            kernel = functools.partial(prepare_more_kernel, chunk, levels, height)
+            prepared.append(call(kernel, outs, [], flops, gradient, members, restrict, packed[-1][3]))
         packed.append(call(
             functools.partial(pack_kernel, chunk, levels, height),
             [(GROUP, groups * 8, LANES), (groups * 8, LANES), (groups * 8, LANES), (3, levels, 8, LANES), (7, levels // 2, 8, LANES)],
@@ -721,27 +765,27 @@
             flops, *prepared[-1][:3], south, restrict, packing,
         ))
     high_weights, low_weights, interpolation = prepared[0][3:]
-    got = [(around(to_east, "gx", 1), around(to_west, "gx", -1)) for *_, to_east, to_west in packed]
-    filtered = [
-        call(
-            functools.partial(columns_kernel, levels, height),
+    got = [(around(packed[chunk][3], "gx", 1), around(packed[chunk][4], "gx", -1)) for chunk in range(CHUNKS)]
+    rim_a, rim_b = prepared[1][3:]
+    rims = swap(rim_a, False), swap(rim_b, True)
+    filtered, far, own = [], [], []
+    for chunk in range(CHUNKS):
+        far_rows = (levels * (per_level_of(chunk) + 1), 8, LANES)
+        more = (*rims, own[0][1]) if chunk else (packed[1][3],)
+        filtered.append(call(
+            functools.partial(columns_kernel, chunk, levels, height),
             [(groups, GROUP, 8, 2 * LANES), far_rows, far_rows, (levels, 8, LANES)],
-            [],
-            flops, *packed[chunk][:3], *got[chunk], high_weights, low_weights, beyond_high, beyond_low, choice,
-        )
-        for chunk in range(CHUNKS)
-    ]
-    far = [(swap(rows_a, False), swap(rows_b, True)) for _, rows_a, rows_b, _ in filtered]
-    own = [
-        call(
+            [(2, 8, 8, LANES)] if chunk else [],
+            flops, *packed[chunk][:3], *got[chunk], high_weights, low_weights, beyond_high, beyond_low, choice, *more,
+        ))
+        far.append((swap(filtered[-1][1], False), swap(filtered[-1][2], True)))
+        own.append(call(
             functools.partial(own_rows_kernel, levels, height),
             [(levels, height, 8, LANES), (levels, height // 2, 8, LANES)],
             [],
-            flops, filtered[chunk][0],
-        )
-        for chunk in range(CHUNKS)
-    ]
-    part = levels // 2
+            flops, filtered[-1][0],
+        ))
+    part = levels // PARTS
     buffers = [(2, part, height + 8, LANES), (2, part, 2 * height, LANES), (levels, fine_height, fine_width)]
     vmem, hbm = pl.BlockSpec(memory_space=pltpu.VMEM), pl.BlockSpec(memory_space=pltpu.HBM)
     out_shape = jax.ShapeDtypeStruct(gradient.shape, F32)
@@ -750,7 +794,7 @@
 
     def first_rows_of(chunk, *earlier):
         return call(
-            functools.partial(first_row_kernel, chunk, levels, height),
+            functools.partial(first_row_kernel, chunk, levels),
             [(levels, LANES), ((chunk + 1) * levels, 2 * LANES)],
             [(levels * 8, LANES)],
             flops, *own[chunk], *far[chunk], filtered[chunk][1], filtered[chunk][3], prepared[chunk][1], refining, row_highs, row_lows, *earlier,
@@ -769,7 +813,7 @@
         early_kernel,
         out_shape=(out_shape, jax.ShapeDtypeStruct((levels, 8, fine_width), F32)),
         in_specs=[vmem] * 3, out_specs=(hbm, vmem),
-        scratch_shapes=[pltpu.VMEM(shape, F32) for shape in buffers] + [pltpu.SemaphoreType.DMA((2,))],
+        scratch_shapes=[pltpu.VMEM(shape, F32) for shape in buffers] + [pltpu.SemaphoreType.DMA((PARTS,))],
         compiler_params=params, cost_estimate=cost,
     )(combined_of(0), early_beyond, interpolation)
     beyond, rows = first_rows_of(1, early_rows, tails)
@@ -779,7 +823,7 @@
         out_shape=out_shape,
         in_specs=[hbm] + [vmem] * 5, out_specs=hbm,
         scratch_shapes=[pltpu.VMEM(shape, F32) for shape in buffers + [(levels, 8, fine_width), (all_levels, LANES), (all_levels, LANES)]]
-        + [pltpu.SemaphoreType.DMA((3,))],
+        + [pltpu.SemaphoreType.DMA((PARTS + 1,))],
         input_output_aliases={0: 0},
         compiler_params=params, cost_estimate=cost,
     )(out, combined_of(1), beyond, north, interpolation, tails)
@@ -789,4 +833,5 @@
 def solution(mesh):
     in_specs = (P(None, "gy", "gx"), P(None, None, "gy", "gx"))
     out_specs = P(None, "gy", "gx")
+
     return jax.shard_map(shards, mesh=mesh, in_specs=in_specs, out_specs=out_specs, check_vma=False)

time: 36.4 us -> 50.5 us (1.39)
  the two profiles are of different devices: /device:TPU:0 before, /device:TPU:1 now
where the time goes in v6:
time: 50.5 us; the launch traced here: 50.4 us
  starting transfers between devices  18.3 us (36%)
  Pallas kernels  15.8 us (31%)
  waiting for transfers between devices  14.9 us (30%)
  local copies, waits for them, and re-layouts  1.07 us (2%)
    pallas_call x12, Pallas kernels, call(): pl.pallas_call(kernel, out_shape=tuple((jax.ShapeDtypeStruct(*out) if isi...  13.3 us
    ppermute x6, waiting for transfers between devices, around(): lax.ppermute(value, axis, [(i, (i + step) % size) for i in range(size)])  12.8 us
    ppermute x6, starting transfers between devices, swap(): return lax.ppermute(value, ('gx', 'gy'), pairs)  11.2 us
    ppermute x6, starting transfers between devices, around(): lax.ppermute(value, axis, [(i, (i + step) % size) for i in range(size)])  7.11 us
    ppermute x6, waiting for transfers between devices, swap(): return lax.ppermute(value, ('gx', 'gy'), pairs)  2.09 us
    pallas_call x1, Pallas kernels, shards(): pl.pallas_call(functools.partial(late_kernel, levels), out_shape=out_shap...  1.31 us
    pallas_call x1, Pallas kernels, shards(): pl.pallas_call(early_kernel, out_shape=(out_shape, jax.ShapeDtypeStruct((...  1.26 us
  transfers between devices with their start and end apart: 12, of which 5 were waited for; matrix products, arithmetic and copies ran while one was open for 0% of the time, Pallas kernels for 23%

profile of v6, /device:TPU:1, one launch (start us, length us, event | category | flops | bytes accessed | tf_op | source)
XLA Modules:
  0.0 50.4 jit_solution(6507563678371697051)
XLA Ops:
  0.0 0.0 copy-start.2
  0.0 0.0 copy-start.3
  0.0 1.0 %slice.3 = f32[16,1,256]{2,1,0:T(1,128)S(1)} slice(f32[16,64,256]{2,1,0:T(8,128)} %gradient.3), slice={[0:16], [63:64], [0:256]} | slice | bytes 32768 | tf_op jit(solution)/shard_map/slice | solution.py:729
  1.0 2.7 %collective-permute-start = (f32[16,256]{1,0:T(8,128)S(1)}, f32[16,256]{1,0:T(8,128)S(1)}, u32[]{:S(2)}, u32[]{:S(2)}) collective-permute-start(f32[16,256]{1,0:T(8,128)S(1)} %bitcast.3), channel_id=1, source_target_pairs={{0,1},{1,2},{2,3},{3,4},{4,5},{5,6},{6,7},{7,0},{8,9},{9,10},{10,1... | collective-permute-start | bytes 49160 | tf_op jit(solution)/shard_map/ppermute | solution.py:690
  3.7 0.0 copy-start.1
  3.7 2.5 %shard_map.136 = (f32[2,8,72,128]{3,2,1,0:T(8,128)S(1)}, f32[8,32,8,128]{3,2,1,0:T(8,128)S(1)}, f32[256,128]{1,0:T(8,128)S(1)}, bf16[4,256,256]{2,1,0:T(8,128)(2...) custom-call(f32[16,64,256]{2,1,0:T(8,128)} %gradient.3, f32[8,16,32,128]{3,2,1,0:T(8,128)} %members.3, ...), custom_call_target="tpu_custom_call" | custom-call | flops 500000000 | bytes 1048576 | tf_op jit(solution)/shard_map/pallas_call | solution.py:705
  6.2 0.0 copy-start
  6.2 0.0 collective-permute-done.south
  6.2 0.0 copy-done.2
  6.3 0.0 copy-done.3
  6.3 1.0 %shard_map.137 = (f32[8,256,128]{2,1,0:T(8,128)S(1)}, f32[256,128]{1,0:T(8,128)S(1)}, f32[256,128]{1,0:T(8,128)S(1)}, f32[3,8,8,128]{3,2,1,0:T(8,128)S(1)}, f32[7,4,8,128]{3,2,1,0:T(8,128)S(1)}) custom-call(f32[2,8,72,128]{3,2,1,0:T(8,128)S(1)} %get-tuple-element.44.across, f32[8,32,8,128]{3,2,1,0:T(8,128)S(1)} %get-tuple-element.45.turned, ...), custom_call_target="tpu_custom_call" | custom-call | flops 500000000 | bytes 1048576 | tf_op jit(solution)/shard_map/pallas_call | solution.py:705
  7.2 2.2 %collective-permute-start.2 = (f32[7,4,8,128]{3,2,1,0:T(8,128)S(1)}, f32[7,4,8,128]{3,2,1,0:T(8,128)S(1)}, u32[]{:S(2)}, u32[]{:S(2)}) collective-permute-start(f32[7,4,8,128]{3,2,1,0:T(8,128)S(1)} %get-tuple-element.51), channel_id=1, source_target_pairs={{0,24},{8,0},{16,8},{24,16},{1,25},{9,1},{17,9},{25,17},{2,26},{10... | collective-permute-start | bytes 344072 | tf_op jit(solution)/shard_map/ppermute | solution.py:690
  9.4 0.0 copy-start.7
  9.4 0.0 copy-start.8
  9.5 0.0 copy-start.9
  9.5 0.0 collective-permute-start.1
  9.5 0.0 copy-done.1
  9.5 0.0 copy-done
  9.5 0.8 %shard_map.138 = (f32[2,8,72,128]{3,2,1,0:T(8,128)S(1)}, f32[8,32,8,128]{3,2,1,0:T(8,128)S(1)}, f32[256,128]{1,0:T(8,128)S(1)}, f32[8,8,8,128]{3,2,1,0:T(8,128)S(1)}, f32[8,8,8,128]{3,2,1,0:T(8,128)S(1)}) custom-call(f32[16,64,256]{2,1,0:T(8,128)S(1)} %copy-done.1, f32[8,16,32,128]{3,2,1,0:T(8,128)S(1)} %copy-done, bf16[256,256]{1,0:T(8,128)(2,1)S(1)} %copy-done.3, ...), custom_call_target="tpu_custom_call" | custom-call | flops 500000000 | bytes 1048576 | tf_op jit(solution)/shard_map/pallas_call | solution.py:705
  10.2 1.0 %shard_map.139 = (f32[8,256,128]{2,1,0:T(8,128)S(1)}, f32[256,128]{1,0:T(8,128)S(1)}, f32[256,128]{1,0:T(8,128)S(1)}, f32[3,8,8,128]{3,2,1,0:T(8,128)S(1)}, f32[7,4,8,128]{3,2,1,0:T(8,128)S(1)}) custom-call(f32[2,8,72,128]{3,2,1,0:T(8,128)S(1)} %get-tuple-element.54.across, f32[8,32,8,128]{3,2,1,0:T(8,128)S(1)} %get-tuple-element.55.turned, ...), custom_call_target="tpu_custom_call" | custom-call | flops 500000000 | bytes 1048576 | tf_op jit(solution)/shard_map/pallas_call | solution.py:705
  11.2 3.4 %collective-permute-done.1.from_west = f32[3,8,8,128]{3,2,1,0:T(8,128)S(1)} collective-permute-done((f32[3,8,8,128]{3,2,1,0:T(8,128)S(1)}, f32[3,8,8,128]{3,2,1,0:T(8,128)S(1)}, u32[]{:S(2)}, u32[]{:S(2)}) %collective-permute-start.1) | collective-permute-done | bytes 98336 | tf_op jit(solution)/shard_map/ppermute | solution.py:690
  14.7 0.0 collective-permute-done.2.from_east
  14.7 0.0 copy-done.7
  14.7 0.0 copy-done.8
  14.7 0.0 copy-done.9
  14.7 1.4 %shard_map.140 = (f32[32,8,8,256]{3,2,1,0:T(8,128)S(1)}, f32[120,8,128]{2,1,0:T(8,128)S(1)}, f32[120,8,128]{2,1,0:T(8,128)S(1)}, f32[8,8,128]{2,1,0:T(8,128)S(1)}) custom-call(f32[8,256,128]{2,1,0:T(8,128)S(1)} %get-tuple-element.47.products, f32[256,128]{1,0:T(8,128)S(1)} %get-tuple-element.48.own_a, f32[256,128]{1,0:T(8,128)S(1)} %get-tuple-element.49.own_b, ...), custom_call_target="tpu_custom_call" | custom-call | flops 500000000 | bytes 1048576 | tf_op jit(solution)/shard_map/pallas_call | solution.py:705
  16.1 1.9 %collective-permute-start.3 = (f32[120,8,128]{2,1,0:T(8,128)S(1)}, f32[120,8,128]{2,1,0:T(8,128)S(1)}, u32[]{:S(2)}, u32[]{:S(2)}) collective-permute-start(f32[120,8,128]{2,1,0:T(8,128)S(1)} %get-tuple-element.61.own_rows), channel_id=1, source_target_pairs={{0,1},{1,0},{2,3},{3,2},{4,5},{5,4},{6,7},{7,6},{8,9},{9,8},{10,11... | collective-permute-start | bytes 1474568 | tf_op jit(solution)/shard_map/ppermute | solution.py:700
  18.0 0.5 %collective-permute-start.4 = (f32[120,8,128]{2,1,0:T(8,128)S(1)}, f32[120,8,128]{2,1,0:T(8,128)S(1)}, u32[]{:S(2)}, u32[]{:S(2)}) collective-permute-start(f32[120,8,128]{2,1,0:T(8,128)S(1)} %get-tuple-element.62), channel_id=1, source_target_pairs={{0,8},{1,2},{2,1},{3,4},{4,3},{5,6},{6,5},{7,15},{8,0},{9,10},{10,... | collective-permute-start | bytes 1474568 | tf_op jit(solution)/shard_map/ppermute | solution.py:700
  18.6 0.4 collective-permute-start.7
  19.0 1.3 %collective-permute-start.8 = (f32[8,8,8,128]{3,2,1,0:T(8,128)S(1)}, f32[8,8,8,128]{3,2,1,0:T(8,128)S(1)}, u32[]{:S(2)}, u32[]{:S(2)}) collective-permute-start(f32[8,8,8,128]{3,2,1,0:T(8,128)S(1)} %get-tuple-element.72), channel_id=1, source_target_pairs={{0,8},{1,2},{2,1},{3,4},{4,3},{5,6},{6,5},{7,15},{8,0},{9,10},{10,... | collective-permute-start | bytes 786440 | tf_op jit(solution)/shard_map/ppermute | solution.py:700
  20.3 1.2 %collective-permute-start.5 = (f32[3,8,8,128]{3,2,1,0:T(8,128)S(1)}, f32[3,8,8,128]{3,2,1,0:T(8,128)S(1)}, u32[]{:S(2)}, u32[]{:S(2)}) collective-permute-start(f32[3,8,8,128]{3,2,1,0:T(8,128)S(1)} %get-tuple-element.57.refs_0_), channel_id=1, source_target_pairs={{0,8},{8,16},{16,24},{24,0},{1,9},{9,17},{17,25},{25,1},{2,10},{10... | collective-permute-start | bytes 294920 | tf_op jit(solution)/shard_map/ppermute | solution.py:690
  21.5 4.2 %collective-permute-done.5.from_west = f32[3,8,8,128]{3,2,1,0:T(8,128)S(1)} collective-permute-done((f32[3,8,8,128]{3,2,1,0:T(8,128)S(1)}, f32[3,8,8,128]{3,2,1,0:T(8,128)S(1)}, u32[]{:S(2)}, u32[]{:S(2)}) %collective-permute-start.5) | collective-permute-done | bytes 98336 | tf_op jit(solution)/shard_map/ppermute | solution.py:690
  25.7 0.5 %collective-permute-start.6 = (f32[7,4,8,128]{3,2,1,0:T(8,128)S(1)}, f32[7,4,8,128]{3,2,1,0:T(8,128)S(1)}, u32[]{:S(2)}, u32[]{:S(2)}) collective-permute-start(f32[7,4,8,128]{3,2,1,0:T(8,128)S(1)} %get-tuple-element.70), channel_id=1, source_target_pairs={{0,24},{8,0},{16,8},{24,16},{1,25},{9,1},{17,9},{25,17},{2,26},{10... | collective-permute-start | bytes 344072 | tf_op jit(solution)/shard_map/ppermute | solution.py:690
  26.2 1.3 %shard_map.141 = (f32[8,32,8,128]{3,2,1,0:T(8,128)S(1)}, f32[8,16,8,128]{3,2,1,0:T(8,128)S(1)}) custom-call(f32[32,8,8,256]{3,2,1,0:T(8,128)S(1)} %get-tuple-element.58.filtered), custom_call_target="tpu_custom_call" | custom-call | flops 500000000 | bytes 1048576 | tf_op jit(solution)/shard_map/pallas_call | solution.py:705
  27.6 3.3 %collective-permute-done.6.from_east = f32[7,4,8,128]{3,2,1,0:T(8,128)S(1)} collective-permute-done((f32[7,4,8,128]{3,2,1,0:T(8,128)S(1)}, f32[7,4,8,128]{3,2,1,0:T(8,128)S(1)}, u32[]{:S(2)}, u32[]{:S(2)}) %collective-permute-start.6) | collective-permute-done | bytes 114720 | tf_op jit(solution)/shard_map/ppermute | solution.py:690
  30.9 0.0 collective-permute-done.7.refs_0_
  30.9 0.0 collective-permute-done.8.refs_1_
  30.9 0.0 copy-start.6
  30.9 1.6 %shard_map.145 = (f32[32,8,8,256]{3,2,1,0:T(8,128)S(1)}, f32[64,8,128]{2,1,0:T(8,128)S(1)}, f32[64,8,128]{2,1,0:T(8,128)S(1)}, f32[8,8,128]{2,1,0:T(8,128)S(1)}) custom-call(f32[8,256,128]{2,1,0:T(8,128)S(1)} %get-tuple-element.67.products, f32[256,128]{1,0:T(8,128)S(1)} %get-tuple-element.68.own_a, f32[256,128]{1,0:T(8,128)S(1)} %get-tuple-element.69.own_b, ...), custom_call_target="tpu_custom_call" | custom-call | flops 500000000 | bytes 1048576 | tf_op jit(solution)/shard_map/pallas_call | solution.py:705
  32.5 7.0 %collective-permute-start.9 = (f32[64,8,128]{2,1,0:T(8,128)S(1)}, f32[64,8,128]{2,1,0:T(8,128)S(1)}, u32[]{:S(2)}, u32[]{:S(2)}) collective-permute-start(f32[64,8,128]{2,1,0:T(8,128)S(1)} %get-tuple-element.76.own_rows), channel_id=1, source_target_pairs={{0,1},{1,0},{2,3},{3,2},{4,5},{5,4},{6,7},{7,6},{8,9},{9,8},{10,11... | collective-permute-start | bytes 786440 | tf_op jit(solution)/shard_map/ppermute | solution.py:700
  39.5 0.0 collective-permute-start.10
  39.5 1.3 %shard_map.146 = (f32[8,32,8,128]{3,2,1,0:T(8,128)S(1)}, f32[8,16,8,128]{3,2,1,0:T(8,128)S(1)}) custom-call(f32[32,8,8,256]{3,2,1,0:T(8,128)S(1)} %get-tuple-element.73.filtered), custom_call_target="tpu_custom_call" | custom-call | flops 500000000 | bytes 1048576 | tf_op jit(solution)/shard_map/pallas_call | solution.py:705
  40.9 0.0 copy-start.4
  40.9 0.0 copy-start.5
  40.9 0.0 collective-permute-done.3.got_a
  40.9 0.0 collective-permute-done.4.got_b
  40.9 0.0 copy-done.6
  40.9 0.9 %shard_map.142.combined = f32[8,32,128]{2,1,0:T(8,128)S(1)} custom-call(f32[8,32,8,128]{3,2,1,0:T(8,128)S(1)} %get-tuple-element.59.fine, f32[8,16,8,128]{3,2,1,0:T(8,128)S(1)} %get-tuple-element.60.coarse.refs_2_, f32[120,8,128]{2,1,0:T(8,128)S(1)} %collective-permute-done.3.got_a, f32[120,8,128]{2,1,0:T(8,128)S(1)} %collective-permute-done.4.got_b, ...), custom_call_target="tpu_custom_call" | custom-call | flops 500000000 | bytes 1048576 | tf_op jit(solution)/shard_map/pallas_call | solution.py:705
  41.9 0.0 copy-done.4
  41.9 0.0 copy-done.5
  41.9 0.3 shard_map.143
  42.2 1.3 %shard_map.144 = (f32[16,64,256]{2,1,0:T(8,128)}, f32[8,8,256]{2,1,0:T(8,128)S(1)}) custom-call(f32[8,32,128]{2,1,0:T(8,128)S(1)} %shard_map.142.combined, f32[8,128]{1,0:T(8,128)S(1)} %get-tuple-element.64.beyond, bf16[256,256]{1,0:T(8,128)(2,1)S(1)} %get-tuple-element.65.interpolation), custom_call_target="tpu_custom_call" | custom-call | flops 500000000 | bytes 1048576 | tf_op jit(solution)/shard_map/pallas_call | solution.py:812
  43.5 0.0 collective-permute-done.9.got_a
  43.5 2.1 %collective-permute-done.10.got_b = f32[64,8,128]{2,1,0:T(8,128)S(1)} collective-permute-done((f32[64,8,128]{2,1,0:T(8,128)S(1)}, f32[64,8,128]{2,1,0:T(8,128)S(1)}, u32[]{:S(2)}, u32[]{:S(2)}) %collective-permute-start.10) | collective-permute-done | bytes 262176 | tf_op jit(solution)/shard_map/ppermute | solution.py:700
  45.6 0.3 shard_map.148
  45.9 0.4 collective-permute-start.11
  46.3 0.9 %shard_map.147.combined = f32[8,32,128]{2,1,0:T(8,128)S(1)} custom-call(f32[8,32,8,128]{3,2,1,0:T(8,128)S(1)} %get-tuple-element.74.fine, f32[8,16,8,128]{3,2,1,0:T(8,128)S(1)} %get-tuple-element.75.coarse, f32[64,8,128]{2,1,0:T(8,128)S(1)} %collective-permute-done.9.got_a, f32[64,8,128]{2,1,0:T(8,128)S(1)} %collective-permute-done.10.got_b, ...), custom_call_target="tpu_custom_call" | custom-call | flops 500000000 | bytes 1048576 | tf_op jit(solution)/shard_map/pallas_call | solution.py:705
  47.2 1.9 %collective-permute-done.11.north = f32[16,256]{1,0:T(8,128)S(1)} collective-permute-done((f32[16,256]{1,0:T(8,128)S(1)}, f32[16,256]{1,0:T(8,128)S(1)}, u32[]{:S(2)}, u32[]{:S(2)}) %collective-permute-start.11) | collective-permute-done | bytes 16416 | tf_op jit(solution)/shard_map/ppermute | solution.py:690
  49.1 1.3 %shard_map.149 = f32[16,64,256]{2,1,0:T(8,128)} custom-call(f32[16,64,256]{2,1,0:T(8,128)} %get-tuple-element.66.before, f32[8,32,128]{2,1,0:T(8,128)S(1)} %shard_map.147.combined, f32[8,128]{1,0:T(8,128)S(1)} %get-tuple-element.81.beyond, f32[16,256]{1,0:T(8,128)S(1)} %collective-permute-done.11.north, ...), custom_call_target="tpu_custom_call", output_to_operand_aliasing={{}: (0, {})} | custom-call | flops 500000000 | bytes 1048576 | tf_op jit(solution)/shard_map/pallas_call | solution.py:821
  (1 shorter events, 0.0 us)
Async XLA Ops:
  0.0 6.2 %copy-start.2 = (bf16[1024,256]{1,0:T(8,128)(2,1)S(1)}, bf16[1024,256]{1,0:T(8,128)(2,1)}, u32[]{:S(2)}) copy-start(bf16[1024,256]{1,0:T(8,128)(2,1)} %constant.36.packing) | copy-start | bytes 1572868
  0.0 6.3 %copy-start.3 = (bf16[256,256]{1,0:T(8,128)(2,1)S(1)}, bf16[256,256]{1,0:T(8,128)(2,1)}, u32[]{:S(2)}) copy-start(bf16[256,256]{1,0:T(8,128)(2,1)} %constant.24.clone.restrict) | copy-start | bytes 393220
  1.0 5.2 %collective-permute-start = (f32[16,256]{1,0:T(8,128)S(1)}, f32[16,256]{1,0:T(8,128)S(1)}, u32[]{:S(2)}, u32[]{:S(2)}) collective-permute-start(f32[16,256]{1,0:T(8,128)S(1)} %bitcast.3), channel_id=1, source_target_pairs={{0,1},{1,2},{2,3},{3,4},{4,5},{5,6},{6,7},{7,0},{8,9},{9,10},{10,1... | collective-permute-start | bytes 49160 | tf_op jit(solution)/shard_map/ppermute | solution.py:690
  3.7 5.7 %copy-start.1 = (f32[16,64,256]{2,1,0:T(8,128)S(1)}, f32[16,64,256]{2,1,0:T(8,128)}, u32[]{:S(2)}) copy-start(f32[16,64,256]{2,1,0:T(8,128)} %gradient.3) | copy-start | bytes 3145732
  6.2 3.3 %copy-start = (f32[8,16,32,128]{3,2,1,0:T(8,128)S(1)}, f32[8,16,32,128]{3,2,1,0:T(8,128)}, u32[]{:S(2)}) copy-start(f32[8,16,32,128]{3,2,1,0:T(8,128)} %members.3) | copy-start | bytes 6291460
  7.2 7.4 %collective-permute-start.2 = (f32[7,4,8,128]{3,2,1,0:T(8,128)S(1)}, f32[7,4,8,128]{3,2,1,0:T(8,128)S(1)}, u32[]{:S(2)}, u32[]{:S(2)}) collective-permute-start(f32[7,4,8,128]{3,2,1,0:T(8,128)S(1)} %get-tuple-element.51), channel_id=1, source_target_pairs={{0,24},{8,0},{16,8},{24,16},{1,25},{9,1},{17,9},{25,17},{2,26},{10... | collective-permute-start | bytes 344072 | tf_op jit(solution)/shard_map/ppermute | solution.py:690
  9.4 5.2 %copy-start.7 = (bf16[256,128]{1,0:T(8,128)(2,1)S(1)}, bf16[256,128]{1,0:T(8,128)(2,1)}, u32[]{:S(2)}) copy-start(bf16[256,128]{1,0:T(8,128)(2,1)} %constant.28.clone.beyond_high) | copy-start | bytes 196612
  9.4 5.2 %copy-start.8 = (bf16[256,128]{1,0:T(8,128)(2,1)S(1)}, bf16[256,128]{1,0:T(8,128)(2,1)}, u32[]{:S(2)}) copy-start(bf16[256,128]{1,0:T(8,128)(2,1)} %constant.29.clone.beyond_low) | copy-start | bytes 196612
  9.5 5.2 %copy-start.9 = (bf16[128,128]{1,0:T(8,128)(2,1)S(1)}, bf16[128,128]{1,0:T(8,128)(2,1)}, u32[]{:S(2)}) copy-start(bf16[128,128]{1,0:T(8,128)(2,1)} %constant.32.clone.choice) | copy-start | bytes 98308
  9.5 5.2 %collective-permute-start.1 = (f32[3,8,8,128]{3,2,1,0:T(8,128)S(1)}, f32[3,8,8,128]{3,2,1,0:T(8,128)S(1)}, u32[]{:S(2)}, u32[]{:S(2)}) collective-permute-start(f32[3,8,8,128]{3,2,1,0:T(8,128)S(1)} %get-tuple-element.50._), channel_id=1, source_target_pairs={{0,8},{8,16},{16,24},{24,0},{1,9},{9,17},{17,25},{25,1},{2,10},{10... | collective-permute-start | bytes 294920 | tf_op jit(solution)/shard_map/ppermute | solution.py:690
  16.1 24.8 %collective-permute-start.3 = (f32[120,8,128]{2,1,0:T(8,128)S(1)}, f32[120,8,128]{2,1,0:T(8,128)S(1)}, u32[]{:S(2)}, u32[]{:S(2)}) collective-permute-start(f32[120,8,128]{2,1,0:T(8,128)S(1)} %get-tuple-element.61.own_rows), channel_id=1, source_target_pairs={{0,1},{1,0},{2,3},{3,2},{4,5},{5,4},{6,7},{7,6},{8,9},{9,8},{10,11... | collective-permute-start | bytes 1474568 | tf_op jit(solution)/shard_map/ppermute | solution.py:700
  18.0 22.9 %collective-permute-start.4 = (f32[120,8,128]{2,1,0:T(8,128)S(1)}, f32[120,8,128]{2,1,0:T(8,128)S(1)}, u32[]{:S(2)}, u32[]{:S(2)}) collective-permute-start(f32[120,8,128]{2,1,0:T(8,128)S(1)} %get-tuple-element.62), channel_id=1, source_target_pairs={{0,8},{1,2},{2,1},{3,4},{4,3},{5,6},{6,5},{7,15},{8,0},{9,10},{10,... | collective-permute-start | bytes 1474568 | tf_op jit(solution)/shard_map/ppermute | solution.py:700
  18.6 12.3 %collective-permute-start.7 = (f32[8,8,8,128]{3,2,1,0:T(8,128)S(1)}, f32[8,8,8,128]{3,2,1,0:T(8,128)S(1)}, u32[]{:S(2)}, u32[]{:S(2)}) collective-permute-start(f32[8,8,8,128]{3,2,1,0:T(8,128)S(1)} %get-tuple-element.71), channel_id=1, source_target_pairs={{0,1},{1,0},{2,3},{3,2},{4,5},{5,4},{6,7},{7,6},{8,9},{9,8},{10,11... | collective-permute-start | bytes 786440 | tf_op jit(solution)/shard_map/ppermute | solution.py:700
  19.0 11.9 %collective-permute-start.8 = (f32[8,8,8,128]{3,2,1,0:T(8,128)S(1)}, f32[8,8,8,128]{3,2,1,0:T(8,128)S(1)}, u32[]{:S(2)}, u32[]{:S(2)}) collective-permute-start(f32[8,8,8,128]{3,2,1,0:T(8,128)S(1)} %get-tuple-element.72), channel_id=1, source_target_pairs={{0,8},{1,2},{2,1},{3,4},{4,3},{5,6},{6,5},{7,15},{8,0},{9,10},{10,... | collective-permute-start | bytes 786440 | tf_op jit(solution)/shard_map/ppermute | solution.py:700
  20.3 5.4 %collective-permute-start.5 = (f32[3,8,8,128]{3,2,1,0:T(8,128)S(1)}, f32[3,8,8,128]{3,2,1,0:T(8,128)S(1)}, u32[]{:S(2)}, u32[]{:S(2)}) collective-permute-start(f32[3,8,8,128]{3,2,1,0:T(8,128)S(1)} %get-tuple-element.57.refs_0_), channel_id=1, source_target_pairs={{0,8},{8,16},{16,24},{24,0},{1,9},{9,17},{17,25},{25,1},{2,10},{10... | collective-permute-start | bytes 294920 | tf_op jit(solution)/shard_map/ppermute | solution.py:690
  25.7 5.2 %collective-permute-start.6 = (f32[7,4,8,128]{3,2,1,0:T(8,128)S(1)}, f32[7,4,8,128]{3,2,1,0:T(8,128)S(1)}, u32[]{:S(2)}, u32[]{:S(2)}) collective-permute-start(f32[7,4,8,128]{3,2,1,0:T(8,128)S(1)} %get-tuple-element.70), channel_id=1, source_target_pairs={{0,24},{8,0},{16,8},{24,16},{1,25},{9,1},{17,9},{25,17},{2,26},{10... | collective-permute-start | bytes 344072 | tf_op jit(solution)/shard_map/ppermute | solution.py:690
  30.9 10.0 %copy-start.6 = (bf16[128,128]{1,0:T(8,128)(2,1)S(1)}, bf16[128,128]{1,0:T(8,128)(2,1)}, u32[]{:S(2)}) copy-start(bf16[128,128]{1,0:T(8,128)(2,1)} %constant.26.clone.refining) | copy-start | bytes 98308
  32.5 11.0 %collective-permute-start.9 = (f32[64,8,128]{2,1,0:T(8,128)S(1)}, f32[64,8,128]{2,1,0:T(8,128)S(1)}, u32[]{:S(2)}, u32[]{:S(2)}) collective-permute-start(f32[64,8,128]{2,1,0:T(8,128)S(1)} %get-tuple-element.76.own_rows), channel_id=1, source_target_pairs={{0,1},{1,0},{2,3},{3,2},{4,5},{5,4},{6,7},{7,6},{8,9},{9,8},{10,11... | collective-permute-start | bytes 786440 | tf_op jit(solution)/shard_map/ppermute | solution.py:700
  39.5 6.1 %collective-permute-start.10 = (f32[64,8,128]{2,1,0:T(8,128)S(1)}, f32[64,8,128]{2,1,0:T(8,128)S(1)}, u32[]{:S(2)}, u32[]{:S(2)}) collective-permute-start(f32[64,8,128]{2,1,0:T(8,128)S(1)} %get-tuple-element.77), channel_id=1, source_target_pairs={{0,8},{1,2},{2,1},{3,4},{4,3},{5,6},{6,5},{7,15},{8,0},{9,10},{10,... | collective-permute-start | bytes 786440 | tf_op jit(solution)/shard_map/ppermute | solution.py:700
  40.9 1.0 %copy-start.4 = (bf16[3,3,128,128]{3,2,1,0:T(8,128)(2,1)S(1)}, bf16[3,3,128,128]{3,2,1,0:T(8,128)(2,1)}, u32[]{:S(2)}) copy-start(bf16[3,3,128,128]{3,2,1,0:T(8,128)(2,1)} %constant.30.clone.row_highs) | copy-start | bytes 884740
  40.9 1.0 %copy-start.5 = (bf16[3,3,128,128]{3,2,1,0:T(8,128)(2,1)S(1)}, bf16[3,3,128,128]{3,2,1,0:T(8,128)(2,1)}, u32[]{:S(2)}) copy-start(bf16[3,3,128,128]{3,2,1,0:T(8,128)(2,1)} %constant.31.clone.row_lows) | copy-start | bytes 884740
  45.9 3.2 %collective-permute-start.11 = (f32[16,256]{1,0:T(8,128)S(1)}, f32[16,256]{1,0:T(8,128)S(1)}, u32[]{:S(2)}, u32[]{:S(2)}) collective-permute-start(f32[16,256]{1,0:T(8,128)S(1)} %get-tuple-element.82), channel_id=1, source_target_pairs={{0,7},{1,0},{2,1},{3,2},{4,3},{5,4},{6,5},{7,6},{8,15},{9,8},{10,9... | collective-permute-start | bytes 49160 | tf_op jit(solution)/shard_map/ppermute | solution.py:690

commit v7 on v6

--- a/solution.py
+++ b/solution.py
@@ -246,14 +246,11 @@
         across[half, start:start + count, 0:8, :] = jnp.zeros((count, 8, LANES), F32)
 
 
-def prepare_kernel(levels, height, gradient, members, restrict, own_tables, halo_tables, places, refine,
-                   across, turned, edges, high_weights, low_weights, refine_out, fine, raw, table, own_case, halo_case, placing, sems):
+def prepare_kernel(levels, height, gradient, members, restrict, across, turned, edges, fine, raw, table, sems):
     part = levels // 2
-    case = column_case()
     moves = [(restrict, table)]
     moves += [(gradient.at[pl.ds(i * part, part)], fine.at[pl.ds(i * part, part)]) for i in range(2)]
     moves += [(members.at[:, pl.ds(i * part, part)], raw.at[:, pl.ds(i * part, part)]) for i in range(2)]
-    moves += [(own_tables.at[case], own_case), (halo_tables.at[case], halo_case), (places, placing), (refine, refine_out)]
     copies = [pltpu.make_async_copy(source, target, sems.at[i]) for i, (source, target) in enumerate(moves)]
     for copy in copies:
         copy.start()
@@ -264,15 +261,16 @@
     for i in range(2):
         copies[3 + i].wait()
         turn_members(height, raw, 0, turned, edges, i * part, (i + 1) * part)
-    for copy in copies[5:]:
-        copy.wait()
+
+
+def prepare_more_kernel(chunk, levels, height, gradient, members, restrict, _, own_tables, halo_tables, places, refine,
+                        across, turned, edges, rim_a, rim_b, high_weights, low_weights, refine_out):
+    case = column_case()
+    refine_out[...] = refine[...]
     for which, target in ((0, high_weights), (1, low_weights)):
         for variant in range(4):
-            target[variant, :LANES, :] = own_case[which]
-            target[variant, LANES:, :] = mul(placing[variant], halo_case[which]).astype(BF16)
-
-
-def prepare_more_kernel(chunk, levels, height, gradient, members, restrict, _, across, turned, edges, rim_a, rim_b):
+            target[variant, :LANES, :] = own_tables[case, which]
+            target[variant, LANES:, :] = mul(places[variant], halo_tables[case, which]).astype(BF16)
     reduce_columns(gradient, chunk * levels, levels, height, restrict, across, 0)
     turn_members(height, members, chunk * levels, turned, edges, 0, levels, (rim_a, rim_b))
 
@@ -742,31 +740,29 @@
     flops = 10**9 // CHUNKS
 
     hbm_of = functools.partial(pltpu.with_memory_space_constraint, memory_space=pltpu.HBM)
-    constants = tuple(map(hbm_of, (jnp.asarray(own_tables), jnp.asarray(halo_tables), jnp.asarray(places, BF16), interpolation)))
+    constants = (jnp.asarray(own_tables), jnp.asarray(halo_tables), jnp.asarray(places, BF16), interpolation)
     far_inputs = tuple(map(hbm_of, (gradient, members, restrict)))
     prepared, packed = [], []
     for chunk in range(CHUNKS):
         outs = [(2, levels, 8 + 2 * height, LANES), (levels, height, 8, LANES), (levels * height, LANES)]
         if chunk == 0:
-            outs += [((4, 2 * LANES, 2 * LANES), BF16), ((4, 2 * LANES, 2 * LANES), BF16), (interpolation.shape, BF16)]
-            scratch = [(levels, fine_height, fine_width), (8, levels, height, LANES)]
-            shapes = (restrict.shape, own_tables.shape[1:], halo_tables.shape[1:], places.shape)
-            scratch += [pltpu.VMEM(shape, BF16) for shape in shapes] + [pltpu.SemaphoreType.DMA((9,))]
+            scratch = [(levels, fine_height, fine_width), (8, levels, height, LANES), pltpu.VMEM(restrict.shape, BF16)]
             kernel = functools.partial(prepare_kernel, levels, height)
-            prepared.append(call(kernel, outs, scratch, flops, *far_inputs, *constants, in_hbm=7))
+            prepared.append(call(kernel, outs, scratch + [pltpu.SemaphoreType.DMA((5,))], flops, *far_inputs, in_hbm=3))
         else:
             outs += [(levels, 8, 8, LANES), (levels, 8, 8, LANES)]
+            outs += [((4, 2 * LANES, 2 * LANES), BF16), ((4, 2 * LANES, 2 * LANES), BF16), (interpolation.shape, BF16)]
             kernel = functools.partial(prepare_more_kernel, chunk, levels, height)
-            prepared.append(call(kernel, outs, [], flops, gradient, members, restrict, packed[-1][3]))
+            prepared.append(call(kernel, outs, [], flops, gradient, members, restrict, packed[-1][3], *constants))
         packed.append(call(
             functools.partial(pack_kernel, chunk, levels, height),
             [(GROUP, groups * 8, LANES), (groups * 8, LANES), (groups * 8, LANES), (3, levels, 8, LANES), (7, levels // 2, 8, LANES)],
             [(2, height, LANES), (2, all_levels, LANES)],
             flops, *prepared[-1][:3], south, restrict, packing,
         ))
-    high_weights, low_weights, interpolation = prepared[0][3:]
+    high_weights, low_weights, interpolation = prepared[1][5:]
     got = [(around(packed[chunk][3], "gx", 1), around(packed[chunk][4], "gx", -1)) for chunk in range(CHUNKS)]
-    rim_a, rim_b = prepared[1][3:]
+    rim_a, rim_b = prepared[1][3:5]
     rims = swap(rim_a, False), swap(rim_b, True)
     filtered, far, own = [], [], []
     for chunk in range(CHUNKS):

time: 50.5 us -> 50.6 us (level)
  no operation moved by 1% of the time
where the time goes in v7:
time: 50.6 us; the launch traced here: 50.5 us
  starting transfers between devices  18.6 us (37%)
  Pallas kernels  15.6 us (31%)
  waiting for transfers between devices  14.9 us (29%)
  local copies, waits for them, and re-layouts  1.11 us (2%)
    pallas_call x12, Pallas kernels, call(): pl.pallas_call(kernel, out_shape=tuple((jax.ShapeDtypeStruct(*out) if isi...  13 us
    ppermute x6, waiting for transfers between devices, around(): lax.ppermute(value, axis, [(i, (i + step) % size) for i in range(size)])  12.8 us
    ppermute x6, starting transfers between devices, swap(): return lax.ppermute(value, ('gx', 'gy'), pairs)  11.4 us
    ppermute x6, starting transfers between devices, around(): lax.ppermute(value, axis, [(i, (i + step) % size) for i in range(size)])  7.16 us
    ppermute x6, waiting for transfers between devices, swap(): return lax.ppermute(value, ('gx', 'gy'), pairs)  2.09 us
    pallas_call x1, Pallas kernels, shards(): pl.pallas_call(functools.partial(late_kernel, levels), out_shape=out_shap...  1.31 us
    pallas_call x1, Pallas kernels, shards(): pl.pallas_call(early_kernel, out_shape=(out_shape, jax.ShapeDtypeStruct((...  1.27 us
  transfers between devices with their start and end apart: 12, of which 5 were waited for; matrix products, arithmetic and copies ran while one was open for 0% of the time, Pallas kernels for 23%

profile of v7, /device:TPU:1, one launch (start us, length us, event | category | flops | bytes accessed | tf_op | source)
XLA Modules:
  0.0 50.5 jit_solution(14593026498392302197)
XLA Ops:
  0.0 1.0 %slice.3 = f32[16,1,256]{2,1,0:T(1,128)S(1)} slice(f32[16,64,256]{2,1,0:T(8,128)} %gradient.3), slice={[0:16], [63:64], [0:256]} | slice | bytes 32768 | tf_op jit(solution)/shard_map/slice | solution.py:727
  1.0 0.0 copy-start
  1.0 0.0 copy-start.1
  1.0 0.0 copy-start.7
  1.0 0.0 copy-start.10
  1.1 0.0 copy-start.11
  1.1 0.0 copy-start.12
  1.1 2.7 %collective-permute-start = (f32[16,256]{1,0:T(8,128)S(1)}, f32[16,256]{1,0:T(8,128)S(1)}, u32[]{:S(2)}, u32[]{:S(2)}) collective-permute-start(f32[16,256]{1,0:T(8,128)S(1)} %bitcast.3), channel_id=1, source_target_pairs={{0,1},{1,2},{2,3},{3,4},{4,5},{5,6},{6,7},{7,0},{8,9},{9,10},{10,1... | collective-permute-start | bytes 49160 | tf_op jit(solution)/shard_map/ppermute | solution.py:688
  3.8 2.1 %shard_map.136 = (f32[2,8,72,128]{3,2,1,0:T(8,128)S(1)}, f32[8,32,8,128]{3,2,1,0:T(8,128)S(1)}, f32[256,128]{1,0:T(8,128)S(1)}) custom-call(f32[16,64,256]{2,1,0:T(8,128)} %gradient.3, f32[8,16,32,128]{3,2,1,0:T(8,128)} %members.3, bf16[256,256]{1,0:T(8,128)(2,1)} %constant.24.clone.restrict), custom_call_target="tpu_custom_call" | custom-call | flops 500000000 | bytes 1048576 | tf_op jit(solution)/shard_map/pallas_call | solution.py:703
  5.9 0.0 collective-permute-done.south
  5.9 0.0 copy-done.3
  5.9 0.0 copy-done.2
  5.9 1.0 %shard_map.137 = (f32[8,256,128]{2,1,0:T(8,128)S(1)}, f32[256,128]{1,0:T(8,128)S(1)}, f32[256,128]{1,0:T(8,128)S(1)}, f32[3,8,8,128]{3,2,1,0:T(8,128)S(1)}, f32[7,4,8,128]{3,2,1,0:T(8,128)S(1)}) custom-call(f32[2,8,72,128]{3,2,1,0:T(8,128)S(1)} %get-tuple-element.44.across, f32[8,32,8,128]{3,2,1,0:T(8,128)S(1)} %get-tuple-element.45.turned, ...), custom_call_target="tpu_custom_call" | custom-call | flops 500000000 | bytes 1048576 | tf_op jit(solution)/shard_map/pallas_call | solution.py:703
  6.9 2.2 %collective-permute-start.2 = (f32[7,4,8,128]{3,2,1,0:T(8,128)S(1)}, f32[7,4,8,128]{3,2,1,0:T(8,128)S(1)}, u32[]{:S(2)}, u32[]{:S(2)}) collective-permute-start(f32[7,4,8,128]{3,2,1,0:T(8,128)S(1)} %get-tuple-element.51), channel_id=1, source_target_pairs={{0,24},{8,0},{16,8},{24,16},{1,25},{9,1},{17,9},{25,17},{2,26},{10... | collective-permute-start | bytes 344072 | tf_op jit(solution)/shard_map/ppermute | solution.py:688
  9.1 0.0 collective-permute-start.1
  9.1 0.0 copy-done
  9.1 0.0 copy-done.1
  9.1 0.0 copy-done.7
  9.1 0.0 copy-done.10
  9.1 0.0 copy-done.11
  9.1 0.0 copy-done.12
  9.2 0.9 %shard_map.138 = (f32[2,8,72,128]{3,2,1,0:T(8,128)S(1)}, f32[8,32,8,128]{3,2,1,0:T(8,128)S(1)}, f32[256,128]{1,0:T(8,128)S(1)}, f32[8,8,8,128]{3,2,1,0:T(8,128)S...) custom-call(f32[16,64,256]{2,1,0:T(8,128)S(1)} %copy-done.1, ...), custom_call_target="tpu_custom_call" | custom-call | flops 500000000 | bytes 1048576 | tf_op jit(solution)/shard_map/pallas_call | solution.py:703
  10.0 0.0 copy-start.8
  10.1 0.0 copy-start.9
  10.1 0.0 copy-start.13
  10.1 1.0 %shard_map.139 = (f32[8,256,128]{2,1,0:T(8,128)S(1)}, f32[256,128]{1,0:T(8,128)S(1)}, f32[256,128]{1,0:T(8,128)S(1)}, f32[3,8,8,128]{3,2,1,0:T(8,128)S(1)}, f32[7,4,8,128]{3,2,1,0:T(8,128)S(1)}) custom-call(f32[2,8,72,128]{3,2,1,0:T(8,128)S(1)} %get-tuple-element.54.across, f32[8,32,8,128]{3,2,1,0:T(8,128)S(1)} %get-tuple-element.55.turned, ...), custom_call_target="tpu_custom_call" | custom-call | flops 500000000 | bytes 1048576 | tf_op jit(solution)/shard_map/pallas_call | solution.py:703
  11.1 3.4 %collective-permute-done.1.from_west = f32[3,8,8,128]{3,2,1,0:T(8,128)S(1)} collective-permute-done((f32[3,8,8,128]{3,2,1,0:T(8,128)S(1)}, f32[3,8,8,128]{3,2,1,0:T(8,128)S(1)}, u32[]{:S(2)}, u32[]{:S(2)}) %collective-permute-start.1) | collective-permute-done | bytes 98336 | tf_op jit(solution)/shard_map/ppermute | solution.py:688
  14.5 0.0 collective-permute-done.2.from_east
  14.5 0.0 copy-done.8
  14.5 0.0 copy-done.9
  14.5 0.0 copy-done.13
  14.5 1.4 %shard_map.140 = (f32[32,8,8,256]{3,2,1,0:T(8,128)S(1)}, f32[120,8,128]{2,1,0:T(8,128)S(1)}, f32[120,8,128]{2,1,0:T(8,128)S(1)}, f32[8,8,128]{2,1,0:T(8,128)S(1)}) custom-call(f32[8,256,128]{2,1,0:T(8,128)S(1)} %get-tuple-element.47.products, f32[256,128]{1,0:T(8,128)S(1)} %get-tuple-element.48.own_a, f32[256,128]{1,0:T(8,128)S(1)} %get-tuple-element.49.own_b, ...), custom_call_target="tpu_custom_call" | custom-call | flops 500000000 | bytes 1048576 | tf_op jit(solution)/shard_map/pallas_call | solution.py:703
  16.0 2.2 %collective-permute-start.3 = (f32[120,8,128]{2,1,0:T(8,128)S(1)}, f32[120,8,128]{2,1,0:T(8,128)S(1)}, u32[]{:S(2)}, u32[]{:S(2)}) collective-permute-start(f32[120,8,128]{2,1,0:T(8,128)S(1)} %get-tuple-element.61.own_rows), channel_id=1, source_target_pairs={{0,1},{1,0},{2,3},{3,2},{4,5},{5,4},{6,7},{7,6},{8,9},{9,8},{10,11... | collective-permute-start | bytes 1474568 | tf_op jit(solution)/shard_map/ppermute | solution.py:698
  18.1 0.2 collective-permute-start.4
  18.4 0.3 collective-permute-start.7
  18.7 1.4 %collective-permute-start.8 = (f32[8,8,8,128]{3,2,1,0:T(8,128)S(1)}, f32[8,8,8,128]{3,2,1,0:T(8,128)S(1)}, u32[]{:S(2)}, u32[]{:S(2)}) collective-permute-start(f32[8,8,8,128]{3,2,1,0:T(8,128)S(1)} %get-tuple-element.72), channel_id=1, source_target_pairs={{0,8},{1,2},{2,1},{3,4},{4,3},{5,6},{6,5},{7,15},{8,0},{9,10},{10,... | collective-permute-start | bytes 786440 | tf_op jit(solution)/shard_map/ppermute | solution.py:698
  20.1 1.2 %collective-permute-start.5 = (f32[3,8,8,128]{3,2,1,0:T(8,128)S(1)}, f32[3,8,8,128]{3,2,1,0:T(8,128)S(1)}, u32[]{:S(2)}, u32[]{:S(2)}) collective-permute-start(f32[3,8,8,128]{3,2,1,0:T(8,128)S(1)} %get-tuple-element.57.refs_0_), channel_id=1, source_target_pairs={{0,8},{8,16},{16,24},{24,0},{1,9},{9,17},{17,25},{25,1},{2,10},{10... | collective-permute-start | bytes 294920 | tf_op jit(solution)/shard_map/ppermute | solution.py:688
  21.3 4.2 %collective-permute-done.5.from_west = f32[3,8,8,128]{3,2,1,0:T(8,128)S(1)} collective-permute-done((f32[3,8,8,128]{3,2,1,0:T(8,128)S(1)}, f32[3,8,8,128]{3,2,1,0:T(8,128)S(1)}, u32[]{:S(2)}, u32[]{:S(2)}) %collective-permute-start.5) | collective-permute-done | bytes 98336 | tf_op jit(solution)/shard_map/ppermute | solution.py:688
  25.5 0.6 %collective-permute-start.6 = (f32[7,4,8,128]{3,2,1,0:T(8,128)S(1)}, f32[7,4,8,128]{3,2,1,0:T(8,128)S(1)}, u32[]{:S(2)}, u32[]{:S(2)}) collective-permute-start(f32[7,4,8,128]{3,2,1,0:T(8,128)S(1)} %get-tuple-element.70), channel_id=1, source_target_pairs={{0,24},{8,0},{16,8},{24,16},{1,25},{9,1},{17,9},{25,17},{2,26},{10... | collective-permute-start | bytes 344072 | tf_op jit(solution)/shard_map/ppermute | solution.py:688
  26.0 1.3 %shard_map.141 = (f32[8,32,8,128]{3,2,1,0:T(8,128)S(1)}, f32[8,16,8,128]{3,2,1,0:T(8,128)S(1)}) custom-call(f32[32,8,8,256]{3,2,1,0:T(8,128)S(1)} %get-tuple-element.58.filtered), custom_call_target="tpu_custom_call" | custom-call | flops 500000000 | bytes 1048576 | tf_op jit(solution)/shard_map/pallas_call | solution.py:703
  27.4 3.3 %collective-permute-done.6.from_east = f32[7,4,8,128]{3,2,1,0:T(8,128)S(1)} collective-permute-done((f32[7,4,8,128]{3,2,1,0:T(8,128)S(1)}, f32[7,4,8,128]{3,2,1,0:T(8,128)S(1)}, u32[]{:S(2)}, u32[]{:S(2)}) %collective-permute-start.6) | collective-permute-done | bytes 114720 | tf_op jit(solution)/shard_map/ppermute | solution.py:688
  30.6 0.0 collective-permute-done.7.refs_0_
  30.6 0.0 collective-permute-done.8.refs_1_
  30.6 1.6 %shard_map.145 = (f32[32,8,8,256]{3,2,1,0:T(8,128)S(1)}, f32[64,8,128]{2,1,0:T(8,128)S(1)}, f32[64,8,128]{2,1,0:T(8,128)S(1)}, f32[8,8,128]{2,1,0:T(8,128)S(1)}) custom-call(f32[8,256,128]{2,1,0:T(8,128)S(1)} %get-tuple-element.67.products, f32[256,128]{1,0:T(8,128)S(1)} %get-tuple-element.68.own_a, f32[256,128]{1,0:T(8,128)S(1)} %get-tuple-element.69.own_b, ...), custom_call_target="tpu_custom_call" | custom-call | flops 500000000 | bytes 1048576 | tf_op jit(solution)/shard_map/pallas_call | solution.py:703
  32.3 7.3 %collective-permute-start.9 = (f32[64,8,128]{2,1,0:T(8,128)S(1)}, f32[64,8,128]{2,1,0:T(8,128)S(1)}, u32[]{:S(2)}, u32[]{:S(2)}) collective-permute-start(f32[64,8,128]{2,1,0:T(8,128)S(1)} %get-tuple-element.76.own_rows), channel_id=1, source_target_pairs={{0,1},{1,0},{2,3},{3,2},{4,5},{5,4},{6,7},{7,6},{8,9},{9,8},{10,11... | collective-permute-start | bytes 786440 | tf_op jit(solution)/shard_map/ppermute | solution.py:698
  39.6 0.0 collective-permute-start.10
  39.6 1.3 %shard_map.146 = (f32[8,32,8,128]{3,2,1,0:T(8,128)S(1)}, f32[8,16,8,128]{3,2,1,0:T(8,128)S(1)}) custom-call(f32[32,8,8,256]{3,2,1,0:T(8,128)S(1)} %get-tuple-element.73.filtered), custom_call_target="tpu_custom_call" | custom-call | flops 500000000 | bytes 1048576 | tf_op jit(solution)/shard_map/pallas_call | solution.py:703
  41.0 0.0 copy-start.4
  41.0 0.0 copy-start.5
  41.0 0.0 collective-permute-done.3.got_a
  41.0 0.0 collective-permute-done.4.got_b
  41.0 0.0 copy-done.6
  41.0 0.9 %shard_map.142.combined = f32[8,32,128]{2,1,0:T(8,128)S(1)} custom-call(f32[8,32,8,128]{3,2,1,0:T(8,128)S(1)} %get-tuple-element.59.fine, f32[8,16,8,128]{3,2,1,0:T(8,128)S(1)} %get-tuple-element.60.coarse.refs_2_, f32[120,8,128]{2,1,0:T(8,128)S(1)} %collective-permute-done.3.got_a, f32[120,8,128]{2,1,0:T(8,128)S(1)} %collective-permute-done.4.got_b, ...), custom_call_target="tpu_custom_call" | custom-call | flops 500000000 | bytes 1048576 | tf_op jit(solution)/shard_map/pallas_call | solution.py:703
  42.0 0.0 copy-done.4
  42.0 0.0 copy-done.5
  42.0 0.3 shard_map.143
  42.3 1.3 %shard_map.144 = (f32[16,64,256]{2,1,0:T(8,128)}, f32[8,8,256]{2,1,0:T(8,128)S(1)}) custom-call(f32[8,32,128]{2,1,0:T(8,128)S(1)} %shard_map.142.combined, f32[8,128]{1,0:T(8,128)S(1)} %get-tuple-element.64.beyond, bf16[256,256]{1,0:T(8,128)(2,1)S(1)} %get-tuple-element.65.interpolation), custom_call_target="tpu_custom_call" | custom-call | flops 500000000 | bytes 1048576 | tf_op jit(solution)/shard_map/pallas_call | solution.py:808
  43.6 0.0 collective-permute-done.9.got_a
  43.6 2.1 %collective-permute-done.10.got_b = f32[64,8,128]{2,1,0:T(8,128)S(1)} collective-permute-done((f32[64,8,128]{2,1,0:T(8,128)S(1)}, f32[64,8,128]{2,1,0:T(8,128)S(1)}, u32[]{:S(2)}, u32[]{:S(2)}) %collective-permute-start.10) | collective-permute-done | bytes 262176 | tf_op jit(solution)/shard_map/ppermute | solution.py:698
  45.7 0.3 shard_map.148
  45.9 0.4 collective-permute-start.11
  46.4 0.9 %shard_map.147.combined = f32[8,32,128]{2,1,0:T(8,128)S(1)} custom-call(f32[8,32,8,128]{3,2,1,0:T(8,128)S(1)} %get-tuple-element.74.fine, f32[8,16,8,128]{3,2,1,0:T(8,128)S(1)} %get-tuple-element.75.coarse, f32[64,8,128]{2,1,0:T(8,128)S(1)} %collective-permute-done.9.got_a, f32[64,8,128]{2,1,0:T(8,128)S(1)} %collective-permute-done.10.got_b, ...), custom_call_target="tpu_custom_call" | custom-call | flops 500000000 | bytes 1048576 | tf_op jit(solution)/shard_map/pallas_call | solution.py:703
  47.3 1.9 %collective-permute-done.11.north = f32[16,256]{1,0:T(8,128)S(1)} collective-permute-done((f32[16,256]{1,0:T(8,128)S(1)}, f32[16,256]{1,0:T(8,128)S(1)}, u32[]{:S(2)}, u32[]{:S(2)}) %collective-permute-start.11) | collective-permute-done | bytes 16416 | tf_op jit(solution)/shard_map/ppermute | solution.py:688
  49.2 1.3 %shard_map.149 = f32[16,64,256]{2,1,0:T(8,128)} custom-call(f32[16,64,256]{2,1,0:T(8,128)} %get-tuple-element.66.before, f32[8,32,128]{2,1,0:T(8,128)S(1)} %shard_map.147.combined, f32[8,128]{1,0:T(8,128)S(1)} %get-tuple-element.81.beyond, f32[16,256]{1,0:T(8,128)S(1)} %collective-permute-done.11.north, ...), custom_call_target="tpu_custom_call", output_to_operand_aliasing={{}: (0, {})} | custom-call | flops 500000000 | bytes 1048576 | tf_op jit(solution)/shard_map/pallas_call | solution.py:817
  (4 shorter events, 0.0 us)
Async XLA Ops:
  0.0 5.9 %copy-start.3 = (bf16[256,256]{1,0:T(8,128)(2,1)S(1)}, bf16[256,256]{1,0:T(8,128)(2,1)}, u32[]{:S(2)}) copy-start(bf16[256,256]{1,0:T(8,128)(2,1)} %constant.24.clone.restrict) | copy-start | bytes 393220
  0.0 5.9 %copy-start.2 = (bf16[1024,256]{1,0:T(8,128)(2,1)S(1)}, bf16[1024,256]{1,0:T(8,128)(2,1)}, u32[]{:S(2)}) copy-start(bf16[1024,256]{1,0:T(8,128)(2,1)} %constant.36.packing) | copy-start | bytes 1572868
  1.0 8.1 %copy-start = (f32[8,16,32,128]{3,2,1,0:T(8,128)S(1)}, f32[8,16,32,128]{3,2,1,0:T(8,128)}, u32[]{:S(2)}) copy-start(f32[8,16,32,128]{3,2,1,0:T(8,128)} %members.3) | copy-start | bytes 6291460
  1.0 8.1 %copy-start.1 = (f32[16,64,256]{2,1,0:T(8,128)S(1)}, f32[16,64,256]{2,1,0:T(8,128)}, u32[]{:S(2)}) copy-start(f32[16,64,256]{2,1,0:T(8,128)} %gradient.3) | copy-start | bytes 3145732
  1.0 8.1 %copy-start.7 = (bf16[3,2,128,256]{3,2,1,0:T(8,128)(2,1)S(1)}, bf16[3,2,128,256]{3,2,1,0:T(8,128)(2,1)}, u32[]{:S(2)}) copy-start(bf16[3,2,128,256]{3,2,1,0:T(8,128)(2,1)} %constant.33.clone.own_tables) | copy-start | bytes 1179652
  1.0 8.1 %copy-start.10 = (bf16[3,2,64,256]{3,2,1,0:T(8,128)(2,1)S(1)}, bf16[3,2,64,256]{3,2,1,0:T(8,128)(2,1)}, u32[]{:S(2)}) copy-start(bf16[3,2,64,256]{3,2,1,0:T(8,128)(2,1)} %constant.34.clone.halo_tables) | copy-start | bytes 589828
  1.1 8.1 %copy-start.11 = (bf16[4,128,64]{2,1,0:T(8,128)(2,1)S(1)}, bf16[4,128,64]{2,1,0:T(8,128)(2,1)}, u32[]{:S(2)}) copy-start(bf16[4,128,64]{2,1,0:T(8,128)(2,1)} %constant.35.clone.places) | copy-start | bytes 196612
  1.1 8.1 %copy-start.12 = (bf16[256,256]{1,0:T(8,128)(2,1)S(1)}, bf16[256,256]{1,0:T(8,128)(2,1)}, u32[]{:S(2)}) copy-start(bf16[256,256]{1,0:T(8,128)(2,1)} %constant.27.clone.refine) | copy-start | bytes 393220
  1.1 4.8 %collective-permute-start = (f32[16,256]{1,0:T(8,128)S(1)}, f32[16,256]{1,0:T(8,128)S(1)}, u32[]{:S(2)}, u32[]{:S(2)}) collective-permute-start(f32[16,256]{1,0:T(8,128)S(1)} %bitcast.3), channel_id=1, source_target_pairs={{0,1},{1,2},{2,3},{3,4},{4,5},{5,6},{6,7},{7,0},{8,9},{9,10},{10,1... | collective-permute-start | bytes 49160 | tf_op jit(solution)/shard_map/ppermute | solution.py:688
  6.9 7.6 %collective-permute-start.2 = (f32[7,4,8,128]{3,2,1,0:T(8,128)S(1)}, f32[7,4,8,128]{3,2,1,0:T(8,128)S(1)}, u32[]{:S(2)}, u32[]{:S(2)}) collective-permute-start(f32[7,4,8,128]{3,2,1,0:T(8,128)S(1)} %get-tuple-element.51), channel_id=1, source_target_pairs={{0,24},{8,0},{16,8},{24,16},{1,25},{9,1},{17,9},{25,17},{2,26},{10... | collective-permute-start | bytes 344072 | tf_op jit(solution)/shard_map/ppermute | solution.py:688
  9.1 5.4 %collective-permute-start.1 = (f32[3,8,8,128]{3,2,1,0:T(8,128)S(1)}, f32[3,8,8,128]{3,2,1,0:T(8,128)S(1)}, u32[]{:S(2)}, u32[]{:S(2)}) collective-permute-start(f32[3,8,8,128]{3,2,1,0:T(8,128)S(1)} %get-tuple-element.50._), channel_id=1, source_target_pairs={{0,8},{8,16},{16,24},{24,0},{1,9},{9,17},{17,25},{25,1},{2,10},{10... | collective-permute-start | bytes 294920 | tf_op jit(solution)/shard_map/ppermute | solution.py:688
  10.0 4.5 %copy-start.8 = (bf16[256,128]{1,0:T(8,128)(2,1)S(1)}, bf16[256,128]{1,0:T(8,128)(2,1)}, u32[]{:S(2)}) copy-start(bf16[256,128]{1,0:T(8,128)(2,1)} %constant.28.clone.beyond_high) | copy-start | bytes 196612
  10.1 4.4 %copy-start.9 = (bf16[256,128]{1,0:T(8,128)(2,1)S(1)}, bf16[256,128]{1,0:T(8,128)(2,1)}, u32[]{:S(2)}) copy-start(bf16[256,128]{1,0:T(8,128)(2,1)} %constant.29.clone.beyond_low) | copy-start | bytes 196612
  10.1 4.4 %copy-start.13 = (bf16[128,128]{1,0:T(8,128)(2,1)S(1)}, bf16[128,128]{1,0:T(8,128)(2,1)}, u32[]{:S(2)}) copy-start(bf16[128,128]{1,0:T(8,128)(2,1)} %constant.32.clone.choice) | copy-start | bytes 98308
  16.0 25.0 %collective-permute-start.3 = (f32[120,8,128]{2,1,0:T(8,128)S(1)}, f32[120,8,128]{2,1,0:T(8,128)S(1)}, u32[]{:S(2)}, u32[]{:S(2)}) collective-permute-start(f32[120,8,128]{2,1,0:T(8,128)S(1)} %get-tuple-element.61.own_rows), channel_id=1, source_target_pairs={{0,1},{1,0},{2,3},{3,2},{4,5},{5,4},{6,7},{7,6},{8,9},{9,8},{10,11... | collective-permute-start | bytes 1474568 | tf_op jit(solution)/shard_map/ppermute | solution.py:698
  18.1 22.9 %collective-permute-start.4 = (f32[120,8,128]{2,1,0:T(8,128)S(1)}, f32[120,8,128]{2,1,0:T(8,128)S(1)}, u32[]{:S(2)}, u32[]{:S(2)}) collective-permute-start(f32[120,8,128]{2,1,0:T(8,128)S(1)} %get-tuple-element.62), channel_id=1, source_target_pairs={{0,8},{1,2},{2,1},{3,4},{4,3},{5,6},{6,5},{7,15},{8,0},{9,10},{10,... | collective-permute-start | bytes 1474568 | tf_op jit(solution)/shard_map/ppermute | solution.py:698
  18.4 12.3 %collective-permute-start.7 = (f32[8,8,8,128]{3,2,1,0:T(8,128)S(1)}, f32[8,8,8,128]{3,2,1,0:T(8,128)S(1)}, u32[]{:S(2)}, u32[]{:S(2)}) collective-permute-start(f32[8,8,8,128]{3,2,1,0:T(8,128)S(1)} %get-tuple-element.71), channel_id=1, source_target_pairs={{0,1},{1,0},{2,3},{3,2},{4,5},{5,4},{6,7},{7,6},{8,9},{9,8},{10,11... | collective-permute-start | bytes 786440 | tf_op jit(solution)/shard_map/ppermute | solution.py:698
  18.7 12.0 %collective-permute-start.8 = (f32[8,8,8,128]{3,2,1,0:T(8,128)S(1)}, f32[8,8,8,128]{3,2,1,0:T(8,128)S(1)}, u32[]{:S(2)}, u32[]{:S(2)}) collective-permute-start(f32[8,8,8,128]{3,2,1,0:T(8,128)S(1)} %get-tuple-element.72), channel_id=1, source_target_pairs={{0,8},{1,2},{2,1},{3,4},{4,3},{5,6},{6,5},{7,15},{8,0},{9,10},{10,... | collective-permute-start | bytes 786440 | tf_op jit(solution)/shard_map/ppermute | solution.py:698
  20.1 5.4 %collective-permute-start.5 = (f32[3,8,8,128]{3,2,1,0:T(8,128)S(1)}, f32[3,8,8,128]{3,2,1,0:T(8,128)S(1)}, u32[]{:S(2)}, u32[]{:S(2)}) collective-permute-start(f32[3,8,8,128]{3,2,1,0:T(8,128)S(1)} %get-tuple-element.57.refs_0_), channel_id=1, source_target_pairs={{0,8},{8,16},{16,24},{24,0},{1,9},{9,17},{17,25},{25,1},{2,10},{10... | collective-permute-start | bytes 294920 | tf_op jit(solution)/shard_map/ppermute | solution.py:688
  25.5 5.2 %collective-permute-start.6 = (f32[7,4,8,128]{3,2,1,0:T(8,128)S(1)}, f32[7,4,8,128]{3,2,1,0:T(8,128)S(1)}, u32[]{:S(2)}, u32[]{:S(2)}) collective-permute-start(f32[7,4,8,128]{3,2,1,0:T(8,128)S(1)} %get-tuple-element.70), channel_id=1, source_target_pairs={{0,24},{8,0},{16,8},{24,16},{1,25},{9,1},{17,9},{25,17},{2,26},{10... | collective-permute-start | bytes 344072 | tf_op jit(solution)/shard_map/ppermute | solution.py:688
  30.6 10.4 %copy-start.6 = (bf16[128,128]{1,0:T(8,128)(2,1)S(1)}, bf16[128,128]{1,0:T(8,128)(2,1)}, u32[]{:S(2)}) copy-start(bf16[128,128]{1,0:T(8,128)(2,1)} %constant.26.clone.refining) | copy-start | bytes 98308
  32.3 11.3 %collective-permute-start.9 = (f32[64,8,128]{2,1,0:T(8,128)S(1)}, f32[64,8,128]{2,1,0:T(8,128)S(1)}, u32[]{:S(2)}, u32[]{:S(2)}) collective-permute-start(f32[64,8,128]{2,1,0:T(8,128)S(1)} %get-tuple-element.76.own_rows), channel_id=1, source_target_pairs={{0,1},{1,0},{2,3},{3,2},{4,5},{5,4},{6,7},{7,6},{8,9},{9,8},{10,11... | collective-permute-start | bytes 786440 | tf_op jit(solution)/shard_map/ppermute | solution.py:698
  39.6 6.1 %collective-permute-start.10 = (f32[64,8,128]{2,1,0:T(8,128)S(1)}, f32[64,8,128]{2,1,0:T(8,128)S(1)}, u32[]{:S(2)}, u32[]{:S(2)}) collective-permute-start(f32[64,8,128]{2,1,0:T(8,128)S(1)} %get-tuple-element.77), channel_id=1, source_target_pairs={{0,8},{1,2},{2,1},{3,4},{4,3},{5,6},{6,5},{7,15},{8,0},{9,10},{10,... | collective-permute-start | bytes 786440 | tf_op jit(solution)/shard_map/ppermute | solution.py:698
  41.0 1.0 %copy-start.4 = (bf16[3,3,128,128]{3,2,1,0:T(8,128)(2,1)S(1)}, bf16[3,3,128,128]{3,2,1,0:T(8,128)(2,1)}, u32[]{:S(2)}) copy-start(bf16[3,3,128,128]{3,2,1,0:T(8,128)(2,1)} %constant.30.clone.row_highs) | copy-start | bytes 884740
  41.0 1.0 %copy-start.5 = (bf16[3,3,128,128]{3,2,1,0:T(8,128)(2,1)S(1)}, bf16[3,3,128,128]{3,2,1,0:T(8,128)(2,1)}, u32[]{:S(2)}) copy-start(bf16[3,3,128,128]{3,2,1,0:T(8,128)(2,1)} %constant.31.clone.row_lows) | copy-start | bytes 884740
  45.9 3.2 %collective-permute-start.11 = (f32[16,256]{1,0:T(8,128)S(1)}, f32[16,256]{1,0:T(8,128)S(1)}, u32[]{:S(2)}, u32[]{:S(2)}) collective-permute-start(f32[16,256]{1,0:T(8,128)S(1)} %get-tuple-element.82), channel_id=1, source_target_pairs={{0,7},{1,0},{2,1},{3,2},{4,3},{5,4},{6,5},{7,6},{8,15},{9,8},{10,9... | collective-permute-start | bytes 49160 | tf_op jit(solution)/shard_map/ppermute | solution.py:688
